TPU v7x, 512 devices: a whole 4x4x16 slice. The times are simulated.
512 devices in a mesh: scen: 16 (over z_hi, x, core), col: 32 (over y, z_lo).
Axes of the slice: x: 4, y: 4, z: 16 (z_hi: 2, z_lo: 8; z = z_hi * 8 + z_lo), core: 2. Of those that a mesh axis runs over, the one named last changes fastest.
Arguments:
- coupling: float32 [16, 512, 16384], P('scen', None, 'col'), may hold values from -0.25 to 0.25
- inverse_slabs: float32 [16, 512, 512], P('scen', 'col'), as said below
- barrier_diagonal: float32 [16384], replicated, may hold values from 1 to 16
Outputs:
- panel_factor: float32 [16384, 256], P('col')
Inputs may be any that keep to these rules, and one draw needn't show every extreme that they name: `inverse_slabs`: each slab is symmetric positive definite.
All inputs are finite; a program needn't handle non-finite values.
Results may differ from a plain program's by a relative error of at most 0.0001.
Values sent between devices are 32-bit elements; how exact they have to be, the bound alone decides.
No kernel may reach another device: no remote copies, remote signals or barrier semaphores. Data moves between devices by JAX's collectives and lax.ppermute only.
A program may use at most 64 MiB of HBM per device.

v0:
```python
import functools

import jax
import jax.numpy as jnp
from jax import lax
from jax.experimental import pallas as pl
from jax.experimental.pallas import tpu as pltpu
from jax.sharding import Mesh, PartitionSpec as P

PANEL = 256
BLOCK = 64
LANES = 128
AXES = ("zh", "x", "core", "y", "zl")
HIGHEST = lax.Precision.HIGHEST
VMEM = pl.BlockSpec(memory_space=pltpu.VMEM)
PARAMS = pltpu.CompilerParams(vmem_limit_bytes=12 << 20)


def f32(*shape):
    return jax.ShapeDtypeStruct(shape, jnp.float32)


def dot(a, b, da, db):
    return lax.dot_general(
        a, b, (((da,), (db,)), ((), ())), precision=HIGHEST, preferred_element_type=jnp.float32
    )


def call(body, outs, *args, flops=0):
    size = sum(a.size for a in args) * 4
    return pl.pallas_call(
        body,
        compiler_params=PARAMS,
        out_shape=outs,
        in_specs=[VMEM] * len(args),
        out_specs=jax.tree.map(lambda _: VMEM, outs),
        cost_estimate=pl.CostEstimate(flops=flops, bytes_accessed=size, transcendentals=0),
    )(*args)


def lane_of(x, c): return jnp.broadcast_to(x[:, c:c+1], (8, LANES))


def row_of(x, r): return jnp.broadcast_to(x[r:r+1, :], (8, LANES))


def base(tiles, lane0):
    row = lax.broadcasted_iota(jnp.int32, (8, LANES), 0)
    n = len(tiles)
    for s in range(n):
        x = tiles[s]
        cols = [lane_of(x, lane0 + 8*s + j) for j in range(8)]
        rest = [[lane_of(tiles[t], lane0 + 8*s + j) for j in range(8)] for t in range(s+1, n)]
        done = None
        for j in range(8):
            rs = lax.rsqrt(row_of(cols[j], j))
            u = row_of(x, j)
            scaled = u * rs
            g = scaled * rs
            done = scaled if done is None else jnp.where(row >= j, scaled, done)
            x = jnp.where(row == j, g, x - cols[j] * g)
            for l in range(j+1, 8):
                cl = row_of(cols[l], j) * (rs * rs)
                cols[l] = jnp.where(row == j, cl, cols[l] - cols[j] * cl)
        tiles[s] = done
        gs = [row_of(x, j) for j in range(8)]
        for i, t in enumerate(range(s+1, n)):
            acc = tiles[t]
            for j in range(8): acc = acc - rest[i][j] * gs[j]
            tiles[t] = acc
    return tiles


def factor_body(p_ref, diag_ref, m_ref, u_ref):
    a = p_ref[...]
    r = lax.broadcasted_iota(jnp.int32, (PANEL, PANEL), 0)
    c = lax.broadcasted_iota(jnp.int32, (PANEL, PANEL), 1)
    m_ref[...] = 0.5 * (a + a.T) + jnp.where(r == c, diag_ref[...], 0.0)
    lane = lax.broadcasted_iota(jnp.int32, (BLOCK, LANES), 1)
    sub = lax.broadcasted_iota(jnp.int32, (BLOCK, LANES), 0)
    wlane = lax.broadcasted_iota(jnp.int32, (BLOCK, PANEL), 1)
    wsub = lax.broadcasted_iota(jnp.int32, (BLOCK, PANEL), 0)
    for k in range(PANEL // BLOCK):
        odd = k % 2
        seg = m_ref[BLOCK*k:BLOCK*k+BLOCK, LANES*(k//2):LANES*(k//2)+LANES]
        eye = (lane == sub + BLOCK*(1-odd)).astype(jnp.float32)
        own = (lane // BLOCK) == odd
        x = jnp.where(own, seg, eye)
        tiles = base([x[8*t:8*t+8] for t in range(BLOCK//8)], BLOCK*odd)
        x = jnp.concatenate(tiles, axis=0)
        u_ref[BLOCK*k:BLOCK*k+BLOCK, :] = x
        left = jnp.where(own, 0.0, x)
        mrow = m_ref[BLOCK*k:BLOCK*k+BLOCK, :]
        mrow = jnp.where(wlane // BLOCK == k, (wlane == wsub + BLOCK*k).astype(jnp.float32), mrow)
        z = jnp.zeros((BLOCK, PANEL), jnp.float32)
        rhs = jnp.concatenate([mrow, z] if odd else [z, mrow], axis=0)
        nk = lax.dot_general(left, rhs, (((1,),(0,)),((),())), precision=HIGHEST, preferred_element_type=jnp.float32)
        m_ref[BLOCK*k:BLOCK*k+BLOCK, :] = nk
        if k + 1 < PANEL // BLOCK:
            upd = lax.dot_general(nk, nk, (((0,),(0,)),((),())), precision=HIGHEST, preferred_element_type=jnp.float32)
            lo = BLOCK*(k+1)
            below = m_ref[lo:, :]
            wl = lax.broadcasted_iota(jnp.int32, below.shape, 1)
            m_ref[lo:, :] = jnp.where(wl // BLOCK == k, 0.0, below) - upd[lo:, :]


def prepare_body(own_ref, slab_ref, panel_ref, slabs_ref):
    panel_ref[...] = own_ref[0].reshape(panel_ref.shape)
    slabs_ref[...] = jnp.broadcast_to(slab_ref[...], slabs_ref.shape)


def prepare(coupling, slabs, n_y, n_zl):
    _, depth, _ = coupling.shape
    own, slab = (1, depth, PANEL), slabs.shape
    outs = [f32(n_y, depth // n_y, PANEL), f32(n_zl, *slab[1:])]
    return pl.pallas_call(
        prepare_body,
        name="prepare",
        compiler_params=PARAMS,
        grid=(1,),
        out_shape=outs,
        in_specs=[pl.BlockSpec(own, lambda i: (0, 0, 0)), pl.BlockSpec(slab, lambda i: (0, 0, 0))],
        out_specs=[pl.BlockSpec(o.shape, lambda i: (0, 0, 0)) for o in outs],
    )(coupling, slabs)


def copies_body(*refs):
    *ins, out = refs
    total = ins[0][...]
    for ref in ins[1:]:
        total = total + ref[...]
    for i in range(out.shape[0]):
        out[i] = total


def copies(n, *parts):
    return call(copies_body, f32(n, *parts[0].shape), *parts)


def total_body(x_ref, o_ref):
    total = x_ref[0]
    for i in range(1, x_ref.shape[0]):
        total = total + x_ref[i]
    o_ref[...] = total


def total(x):
    return call(total_body, f32(*x.shape[1:]), x)


def solve_body(inv_ref, panel_ref, o_ref):
    rows = dot(inv_ref[...], panel_ref[...], 1, 0)
    for i in range(o_ref.shape[0]):
        o_ref[i] = rows


def product_body(a_ref, b_ref, o_ref):
    o_ref[...] = dot(a_ref[...], b_ref[...], 0, 0).reshape(o_ref.shape)


def finish_body(top_ref, s_ref, m_ref, u_ref, o_ref, left):
    step, per = pl.program_id(0), s_ref.shape[0]
    block = lambda shape, d: lax.broadcasted_iota(jnp.int32, shape, d)

    @pl.when(step == 0)
    def _():
        r, c = block((PANEL, PANEL), 0), block((PANEL, PANEL), 1)
        left[...] = jnp.where(r >= c, m_ref[...], 0.0)

    o_ref[...] = dot(s_ref[...], left[...], 1, 1)

    @pl.when((top_ref[0] == 1) & (step < PANEL // per))
    def _():
        r, c = block((PANEL, LANES), 0), block((PANEL, LANES), 1)
        for half in range(PANEL // LANES):
            lanes = slice(LANES * half, LANES * half + LANES)
            inside = (r // BLOCK) == (c + LANES * half) // BLOCK
            upper = jnp.where(inside, u_ref[...], m_ref[:, lanes])
            upper = jnp.where(r <= c + LANES * half, upper, 0.0).T
            for s in range(LANES // per):
                @pl.when(step == half * (LANES // per) + s)
                def _():
                    o_ref[...] = upper[per * s : per * s + per]


def finish(top, rows, m, u):
    width, per = rows.shape[0], 128
    whole = lambda x: pl.BlockSpec(x.shape, lambda i: (0, 0))
    return pl.pallas_call(
        finish_body,
        name="finish",
        compiler_params=PARAMS,
        grid=(width // per,),
        out_shape=f32(width, PANEL),
        in_specs=[
            pl.BlockSpec(memory_space=pltpu.SMEM),
            pl.BlockSpec((per, PANEL), lambda i: (i, 0)),
            whole(m),
            whole(u),
        ],
        out_specs=pl.BlockSpec((per, PANEL), lambda i: (i, 0)),
        scratch_shapes=[pltpu.VMEM((PANEL, PANEL), jnp.float32)],
        cost_estimate=pl.CostEstimate(
            flops=2 * width * PANEL * PANEL, bytes_accessed=8 * width * PANEL, transcendentals=0
        ),
    )(top, rows, m, u)


def shards(sizes, coupling, inverse_slabs, barrier_diagonal):
    n_zh, n_x, n_core, n_y, n_zl = (sizes[a] for a in AXES)
    n_xc, n_z = n_x * n_core, n_zh * n_zl
    own = coupling[0]
    depth, width = own.shape
    y, zl = lax.axis_index("y"), lax.axis_index("zl")
    swap = functools.partial(lax.all_to_all, split_axis=0, concat_axis=0)

    panel, slabs = prepare(coupling, inverse_slabs, n_y, n_zl)
    inv = swap(slabs, "zl").reshape(-1, depth)

    mine = jnp.where((y == 0) & (zl == 0), panel[0], 0.0)
    parts = []
    for k in range(1, n_y):
        parts.append(lax.ppermute(panel[k], ("y", "zl"), [(0, k * n_zl)]))
    for part in parts:
        mine = mine + part
    step = n_zl // 2
    while step:
        pairs = [(j, j + step) for j in range(0, n_zl, 2 * step)]
        got = lax.ppermute(mine, "zl", pairs)
        if step > 1:
            mine = mine + got
        step //= 2
    panel = swap(copies(n_y, mine, got), "y").reshape(depth, PANEL)

    solved = call(
        solve_body, f32(n_y, depth // n_y, PANEL), inv, panel,
        flops=2 * depth // n_y * depth * PANEL,
    )
    solved = swap(solved, "y").reshape(depth, PANEL)

    pivot = call(
        product_body, f32(n_xc, PANEL // n_xc, PANEL), panel, solved,
        flops=2 * PANEL * depth * PANEL,
    )
    pivot = total(swap(pivot, ("x", "core")))
    half = n_zl // 2
    flip = [(z, (z + (half if z // half % 2 else -half)) % n_z) for z in range(n_z)]
    other = lax.ppermute(pivot, ("zh", "zl"), flip)
    pivot = swap(copies(n_xc, pivot, other), ("x", "core")).reshape(PANEL, PANEL)

    rows = call(
        product_body, f32(n_xc, width // n_xc, PANEL), own, solved,
        flops=2 * width * depth * PANEL,
    )
    rows = total(swap(rows, ("x", "core")))
    other = lax.ppermute(rows, "zh", [(0, 1), (1, 0)])
    rows = swap(copies(n_xc, rows, other), ("x", "core")).reshape(width, PANEL)

    m, u = call(
        factor_body, [f32(PANEL, PANEL), f32(PANEL, LANES)],
        pivot, barrier_diagonal[:PANEL].reshape(1, PANEL),
        flops=6 * 10**9,
    )
    top = ((y == 0) & (zl == 0)).astype(jnp.int32).reshape(1)
    return finish(top, rows, m, u)


def solution(mesh):
    sizes = {"zh": 2, "x": 4, "core": 2, "y": 4, "zl": 8}
    fine = Mesh(mesh.devices.reshape([sizes[a] for a in AXES]), AXES)
    return jax.shard_map(
        functools.partial(shards, sizes),
        mesh=fine,
        in_specs=(
            P(("zh", "x", "core"), None, ("y", "zl")),
            P(("zh", "x", "core"), ("y", "zl"), None),
            P(),
        ),
        out_specs=P(("y", "zl"), None),
        check_vma=False,
    )
```

profile of v0, /device:TPU:6, one launch (start us, length us, event | category | flops | bytes accessed | tf_op | source)
XLA Modules:
  0.0 142.9 jit_solution(13911705381934389953)
XLA Ops:
  0.0 0.0 copy-start
  0.0 1.2 copy-done
  1.2 0.0 copy-start.2
  1.2 0.8 copy-done.2
  2.0 0.1 prepare.1
  2.1 3.5 %collective-permute-start = (f32[128,256]{1,0:T(8,128)S(1)}, f32[128,256]{1,0:T(8,128)S(1)}, u32[]{:S(2)}, u32[]{:S(2)}) collective-permute-start(f32[128,256]{1,0:T(8,128)S(1)} %get-tuple-element.13), channel_id=1, source_target_pairs={{0,8},{32,40},{64,72},{96,104},{128,136},{160,168},{192,200},{224,... | collective-permute-start | bytes 393224 | tf_op jit(solution)/shard_map/ppermute | solution.py:223
  5.6 2.3 %collective-permute-start.1 = (f32[128,256]{1,0:T(8,128)S(1)}, f32[128,256]{1,0:T(8,128)S(1)}, u32[]{:S(2)}, u32[]{:S(2)}) collective-permute-start(f32[128,256]{1,0:T(8,128)S(1)} %get-tuple-element.15), channel_id=1, source_target_pairs={{0,16},{32,48},{64,80},{96,112},{128,144},{160,176},{192,208},{224... | collective-permute-start | bytes 393224 | tf_op jit(solution)/shard_map/ppermute | solution.py:223
  7.9 1.3 collective-permute-start.2
  9.2 0.0 collective-permute-done
  9.2 1.9 %collective-permute-done.1 = f32[128,256]{1,0:T(8,128)S(1)} collective-permute-done((f32[128,256]{1,0:T(8,128)S(1)}, f32[128,256]{1,0:T(8,128)S(1)}, u32[]{:S(2)}, u32[]{:S(2)}) %collective-permute-start.1) | collective-permute-done | bytes 131104 | tf_op jit(solution)/shard_map/ppermute | solution.py:223
  11.1 0.8 collective-permute-done.2
  11.9 1.4 collective-permute-start.3
  13.3 2.7 %collective-permute-done.3 = f32[128,256]{1,0:T(8,128)S(1)} collective-permute-done((f32[128,256]{1,0:T(8,128)S(1)}, f32[128,256]{1,0:T(8,128)S(1)}, u32[]{:S(2)}, u32[]{:S(2)}) %collective-permute-start.3) | collective-permute-done | bytes 131104 | tf_op jit(solution)/shard_map/ppermute | solution.py:229
  16.0 1.3 collective-permute-start.4
  17.4 2.5 %collective-permute-done.4 = f32[128,256]{1,0:T(8,128)S(1)} collective-permute-done((f32[128,256]{1,0:T(8,128)S(1)}, f32[128,256]{1,0:T(8,128)S(1)}, u32[]{:S(2)}, u32[]{:S(2)}) %collective-permute-start.4) | collective-permute-done | bytes 131104 | tf_op jit(solution)/shard_map/ppermute | solution.py:229
  19.9 1.3 collective-permute-start.5
  21.2 2.5 %collective-permute-done.5.refs_1_ = f32[128,256]{1,0:T(8,128)S(1)} collective-permute-done((f32[128,256]{1,0:T(8,128)S(1)}, f32[128,256]{1,0:T(8,128)S(1)}, u32[]{:S(2)}, u32[]{:S(2)}) %collective-permute-start.5) | collective-permute-done | bytes 131104 | tf_op jit(solution)/shard_map/ppermute | solution.py:229
  23.7 13.0 %all_to_all.35 = f32[4,128,256]{2,1,0:T(8,128)S(1)} all-to-all(f32[4,128,256]{2,1,0:T(8,128)S(1)} %shard_map.37), channel_id=1, replica_groups=mesh['zh'=2,'x'=4,'core'=2,'y'=4,'zl'=8] {'y'}, dimensions={0} | all-to-all | bytes 1048576 | tf_op jit(solution)/shard_map/all_to_all | solution.py:233
  36.7 25.5 %all_to_all.36 = f32[8,16,512]{2,1,0:T(8,128)S(1)} all-to-all(f32[8,16,512]{2,1,0:T(8,128)S(1)} %get-tuple-element.9), channel_id=1, replica_groups=mesh['zh'=2,'x'=4,'core'=2,'y'=4,'zl'=8] {'zl'}, dimensions={0} | all-to-all | bytes 524288 | tf_op jit(solution)/shard_map/all_to_all | solution.py:218
  62.2 0.4 shard_map.38
  62.6 10.5 %all_to_all.37 = f32[4,128,256]{2,1,0:T(8,128)S(1)} all-to-all(f32[4,128,256]{2,1,0:T(8,128)S(1)} %shard_map.38), channel_id=1, replica_groups=mesh['zh'=2,'x'=4,'core'=2,'y'=4,'zl'=8] {'y'}, dimensions={0} | all-to-all | bytes 1048576 | tf_op jit(solution)/shard_map/all_to_all | solution.py:239
  73.1 0.0 copy-start.1
  73.1 1.4 shard_map.42
  74.5 6.0 %all-to-all-start.5 = ((f32[8,32,256]{2,1,0:T(8,128)}), f32[8,32,256]{2,1,0:T(8,128)S(1)}, u32[]{:S(2)}, u32[]{:S(2)}) async-start(f32[8,32,256]{2,1,0:T(8,128)} %shard_map.42), calls=%async_computation.5 | async-start | bytes 524288 | tf_op jit(solution)/shard_map/all_to_all | solution.py:245
  80.5 0.0 copy-done.1
  80.5 2.0 %shard_map.39 = f32[8,64,256]{2,1,0:T(8,128)} custom-call(f32[512,512]{1,0:T(8,128)S(1)} %bitcast.24, f32[512,256]{1,0:T(8,128)S(1)} %bitcast.23), custom_call_target="tpu_custom_call" | custom-call | flops 134217728 | bytes 1572864 | tf_op jit(solution)/shard_map/pallas_call | solution.py:31
  82.5 3.4 %all-to-all-done.5.x_ref = f32[8,32,256]{2,1,0:T(8,128)S(1)} async-done(((f32[8,32,256]{2,1,0:T(8,128)}), f32[8,32,256]{2,1,0:T(8,128)S(1)}, u32[]{:S(2)}, u32[]{:S(2)}) %all-to-all-start.5) | async-done | bytes 262176 | tf_op jit(solution)/shard_map/all_to_all | solution.py:245
  85.9 5.5 %all-to-all-start.3 = ((f32[8,64,256]{2,1,0:T(8,128)}), f32[8,64,256]{2,1,0:T(8,128)S(1)}, u32[]{:S(2)}, u32[]{:S(2)}) async-start(f32[8,64,256]{2,1,0:T(8,128)} %shard_map.39), calls=%async_computation.3 | async-start | bytes 1048576 | tf_op jit(solution)/shard_map/all_to_all | solution.py:255
  91.4 9.2 %collective-permute-start.7 = (f32[32,256]{1,0:T(8,128)S(1)}, f32[32,256]{1,0:T(8,128)S(1)}, u32[]{:S(2)}, u32[]{:S(2)}) collective-permute-start(f32[32,256]{1,0:T(8,128)S(1)} %shard_map.43.refs_0_), channel_id=1, source_target_pairs={{0,260},{1,261},{2,262},{3,263},{4,256},{5,257},{6,258},{7,259},{2... | collective-permute-start | bytes 98312 | tf_op jit(solution)/shard_map/ppermute | solution.py:248
  100.7 2.1 %collective-permute-done.7.refs_1_ = f32[32,256]{1,0:T(8,128)S(1)} collective-permute-done((f32[32,256]{1,0:T(8,128)S(1)}, f32[32,256]{1,0:T(8,128)S(1)}, u32[]{:S(2)}, u32[]{:S(2)}) %collective-permute-start.7) | collective-permute-done | bytes 32800 | tf_op jit(solution)/shard_map/ppermute | solution.py:248
  102.7 0.7 shard_map.44
  103.4 0.0 all-to-all-done.3.x_ref
  103.5 4.8 %all-to-all-start.6 = ((f32[8,32,256]{2,1,0:T(8,128)}), f32[8,32,256]{2,1,0:T(8,128)S(1)}, u32[]{:S(2)}, u32[]{:S(2)}) async-start(f32[8,32,256]{2,1,0:T(8,128)} %shard_map.44), calls=%async_computation.6 | async-start | bytes 524288 | tf_op jit(solution)/shard_map/all_to_all | solution.py:249
  108.3 12.9 %collective-permute-start.6 = (f32[64,256]{1,0:T(8,128)S(1)}, f32[64,256]{1,0:T(8,128)S(1)}, u32[]{:S(2)}, u32[]{:S(2)}) collective-permute-start(f32[64,256]{1,0:T(8,128)S(1)} %shard_map.40.refs_0_), channel_id=1, source_target_pairs={{0,256},{256,0},{1,257},{257,1},{2,258},{258,2},{3,259},{259,3},{4... | collective-permute-start | bytes 196616 | tf_op jit(solution)/shard_map/ppermute | solution.py:256
  121.2 0.7 slice.19
  121.9 1.9 %collective-permute-done.6.refs_1_ = f32[64,256]{1,0:T(8,128)S(1)} collective-permute-done((f32[64,256]{1,0:T(8,128)S(1)}, f32[64,256]{1,0:T(8,128)S(1)}, u32[]{:S(2)}, u32[]{:S(2)}) %collective-permute-start.6) | collective-permute-done | bytes 65568 | tf_op jit(solution)/shard_map/ppermute | solution.py:256
  123.8 0.8 shard_map.41
  124.6 0.0 all-to-all-done.6
  124.6 4.8 %all-to-all-start.4 = ((f32[8,64,256]{2,1,0:T(8,128)}), f32[8,64,256]{2,1,0:T(8,128)S(1)}, u32[]{:S(2)}, u32[]{:S(2)}) async-start(f32[8,64,256]{2,1,0:T(8,128)} %shard_map.41), calls=%async_computation.4 | async-start | bytes 1048576 | tf_op jit(solution)/shard_map/all_to_all | solution.py:257
  129.4 10.5 %shard_map.45 = (f32[256,256]{1,0:T(8,128)S(1)}, f32[256,128]{1,0:T(8,128)S(1)}) custom-call(f32[256,256]{1,0:T(8,128)S(1)} %bitcast.27, f32[1,256]{1,0:T(1,128)S(1)} %bitcast.28), custom_call_target="tpu_custom_call" | custom-call | flops 6000000000 | bytes 263168 | tf_op jit(solution)/shard_map/pallas_call | solution.py:31
  140.0 0.0 all-to-all-done.4
  140.0 3.0 %finish.1 = f32[512,256]{1,0:T(8,128)} custom-call(s32[1]{0:T(128)} %bitcast.top_ref, f32[512,256]{1,0:T(8,128)S(1)} %bitcast.25, f32[256,256]{1,0:T(8,128)S(1)} %get-tuple-element.11.m_ref, f32[256,128]{1,0:T(8,128)S(1)} %get-tuple-element.12.u_ref), custom_call_target="tpu_custom_call" | custom-call | flops 67108864 | bytes 1048576 | tf_op jit(solution)/shard_map/finish/pallas_call | solution.py:189
  (7 shorter events, 0.2 us)
Async XLA Ops:
  0.0 1.2 copy-start
  1.2 0.8 copy-start.2
  2.1 7.1 %collective-permute-start = (f32[128,256]{1,0:T(8,128)S(1)}, f32[128,256]{1,0:T(8,128)S(1)}, u32[]{:S(2)}, u32[]{:S(2)}) collective-permute-start(f32[128,256]{1,0:T(8,128)S(1)} %get-tuple-element.13), channel_id=1, source_target_pairs={{0,8},{32,40},{64,72},{96,104},{128,136},{160,168},{192,200},{224,... | collective-permute-start | bytes 393224 | tf_op jit(solution)/shard_map/ppermute | solution.py:223
  5.6 5.5 %collective-permute-start.1 = (f32[128,256]{1,0:T(8,128)S(1)}, f32[128,256]{1,0:T(8,128)S(1)}, u32[]{:S(2)}, u32[]{:S(2)}) collective-permute-start(f32[128,256]{1,0:T(8,128)S(1)} %get-tuple-element.15), channel_id=1, source_target_pairs={{0,16},{32,48},{64,80},{96,112},{128,144},{160,176},{192,208},{224... | collective-permute-start | bytes 393224 | tf_op jit(solution)/shard_map/ppermute | solution.py:223
  7.9 4.0 %collective-permute-start.2 = (f32[128,256]{1,0:T(8,128)S(1)}, f32[128,256]{1,0:T(8,128)S(1)}, u32[]{:S(2)}, u32[]{:S(2)}) collective-permute-start(f32[128,256]{1,0:T(8,128)S(1)} %get-tuple-element.14), channel_id=1, source_target_pairs={{0,24},{32,56},{64,88},{96,120},{128,152},{160,184},{192,216},{224... | collective-permute-start | bytes 393224 | tf_op jit(solution)/shard_map/ppermute | solution.py:223
  11.9 4.1 %collective-permute-start.3 = (f32[128,256]{1,0:T(8,128)S(1)}, f32[128,256]{1,0:T(8,128)S(1)}, u32[]{:S(2)}, u32[]{:S(2)}) collective-permute-start(f32[128,256]{1,0:T(8,128)S(1)} %fusion.1), channel_id=1, source_target_pairs={{0,4},{8,12},{16,20},{24,28},{32,36},{40,44},{48,52},{56,60},{64,6... | collective-permute-start | bytes 393224 | tf_op jit(solution)/shard_map/ppermute | solution.py:229
  16.0 3.8 %collective-permute-start.4 = (f32[128,256]{1,0:T(8,128)S(1)}, f32[128,256]{1,0:T(8,128)S(1)}, u32[]{:S(2)}, u32[]{:S(2)}) collective-permute-start(f32[128,256]{1,0:T(8,128)S(1)} %add.18), channel_id=1, source_target_pairs={{0,2},{4,6},{8,10},{12,14},{16,18},{20,22},{24,26},{28,30},{32,34}... | collective-permute-start | bytes 393224 | tf_op jit(solution)/shard_map/ppermute | solution.py:229
  19.9 3.8 %collective-permute-start.5 = (f32[128,256]{1,0:T(8,128)S(1)}, f32[128,256]{1,0:T(8,128)S(1)}, u32[]{:S(2)}, u32[]{:S(2)}) collective-permute-start(f32[128,256]{1,0:T(8,128)S(1)} %add.19.refs_0_), channel_id=1, source_target_pairs={{0,1},{2,3},{4,5},{6,7},{8,9},{10,11},{12,13},{14,15},{16,17},{18,... | collective-permute-start | bytes 393224 | tf_op jit(solution)/shard_map/ppermute | solution.py:229
  73.1 7.4 %copy-start.1 = (f32[1,512,512]{2,1,0:T(8,128)S(1)}, f32[1,512,512]{2,1,0:T(8,128)}, u32[]{:S(2)}) copy-start(f32[1,512,512]{2,1,0:T(8,128)} %own_ref.1) | copy-start | bytes 3145732
  74.5 11.4 %all-to-all-start.5 = ((f32[8,32,256]{2,1,0:T(8,128)}), f32[8,32,256]{2,1,0:T(8,128)S(1)}, u32[]{:S(2)}, u32[]{:S(2)}) async-start(f32[8,32,256]{2,1,0:T(8,128)} %shard_map.42), calls=%async_computation.5 | async-start | bytes 524288 | tf_op jit(solution)/shard_map/all_to_all | solution.py:245
  85.9 17.5 %all-to-all-start.3 = ((f32[8,64,256]{2,1,0:T(8,128)}), f32[8,64,256]{2,1,0:T(8,128)S(1)}, u32[]{:S(2)}, u32[]{:S(2)}) async-start(f32[8,64,256]{2,1,0:T(8,128)} %shard_map.39), calls=%async_computation.3 | async-start | bytes 1048576 | tf_op jit(solution)/shard_map/all_to_all | solution.py:255
  91.4 11.3 %collective-permute-start.7 = (f32[32,256]{1,0:T(8,128)S(1)}, f32[32,256]{1,0:T(8,128)S(1)}, u32[]{:S(2)}, u32[]{:S(2)}) collective-permute-start(f32[32,256]{1,0:T(8,128)S(1)} %shard_map.43.refs_0_), channel_id=1, source_target_pairs={{0,260},{1,261},{2,262},{3,263},{4,256},{5,257},{6,258},{7,259},{2... | collective-permute-start | bytes 98312 | tf_op jit(solution)/shard_map/ppermute | solution.py:248
  103.5 21.2 %all-to-all-start.6 = ((f32[8,32,256]{2,1,0:T(8,128)}), f32[8,32,256]{2,1,0:T(8,128)S(1)}, u32[]{:S(2)}, u32[]{:S(2)}) async-start(f32[8,32,256]{2,1,0:T(8,128)} %shard_map.44), calls=%async_computation.6 | async-start | bytes 524288 | tf_op jit(solution)/shard_map/all_to_all | solution.py:249
  108.3 15.5 %collective-permute-start.6 = (f32[64,256]{1,0:T(8,128)S(1)}, f32[64,256]{1,0:T(8,128)S(1)}, u32[]{:S(2)}, u32[]{:S(2)}) collective-permute-start(f32[64,256]{1,0:T(8,128)S(1)} %shard_map.40.refs_0_), channel_id=1, source_target_pairs={{0,256},{256,0},{1,257},{257,1},{2,258},{258,2},{3,259},{259,3},{4... | collective-permute-start | bytes 196616 | tf_op jit(solution)/shard_map/ppermute | solution.py:256
  124.6 15.3 %all-to-all-start.4 = ((f32[8,64,256]{2,1,0:T(8,128)}), f32[8,64,256]{2,1,0:T(8,128)S(1)}, u32[]{:S(2)}, u32[]{:S(2)}) async-start(f32[8,64,256]{2,1,0:T(8,128)} %shard_map.41), calls=%async_computation.4 | async-start | bytes 1048576 | tf_op jit(solution)/shard_map/all_to_all | solution.py:257
where the time goes:
time: 145 us; the launch traced here: 143 us
  starting transfers between devices  54.3 us (37%)
  blocking collectives  48.9 us (34%)
  Pallas kernels  19.1 us (13%)
  waiting for transfers between devices  17.7 us (12%)
  local copies, waits for them, and re-layouts  2.7 us (2%)
    all_to_all x1, blocking collectives, shards(): inv = swap(slabs, 'zl').reshape(-1, depth)  25.5 us
    pallas_call x9, Pallas kernels, call(): pl.pallas_call(body, compiler_params=PARAMS, out_shape=outs, in_specs=[VM...  16.1 us
    all_to_all x1, blocking collectives, shards(): panel = swap(copies(n_y, mine, got), 'y').reshape(depth, PANEL)  13 us
    ppermute x1, starting transfers between devices, shards(): other = lax.ppermute(rows, 'zh', [(0, 1), (1, 0)])  12.9 us
    all_to_all x1, blocking collectives, shards(): solved = swap(solved, 'y').reshape(depth, PANEL)  10.5 us
    ppermute x1, starting transfers between devices, shards(): other = lax.ppermute(pivot, ('zh', 'zl'), flip)  9.23 us
    ppermute x3, waiting for transfers between devices, shards(): got = lax.ppermute(mine, 'zl', pairs)  7.72 us
    ppermute x3, starting transfers between devices, shards(): parts.append(lax.ppermute(panel[k], ('y', 'zl'), [(0, k * n_zl)]))  7.07 us
  transfers between devices with their start and end apart: 12, of which 8 were waited for; matrix products, arithmetic and copies ran while one was open for 0% of the time, Pallas kernels for 10%

commit v1 on v0

--- a/solution.py
+++ b/solution.py
@@ -104,26 +104,6 @@
             m_ref[lo:, :] = jnp.where(wl // BLOCK == k, 0.0, below) - upd[lo:, :]
 
 
-def prepare_body(own_ref, slab_ref, panel_ref, slabs_ref):
-    panel_ref[...] = own_ref[0].reshape(panel_ref.shape)
-    slabs_ref[...] = jnp.broadcast_to(slab_ref[...], slabs_ref.shape)
-
-
-def prepare(coupling, slabs, n_y, n_zl):
-    _, depth, _ = coupling.shape
-    own, slab = (1, depth, PANEL), slabs.shape
-    outs = [f32(n_y, depth // n_y, PANEL), f32(n_zl, *slab[1:])]
-    return pl.pallas_call(
-        prepare_body,
-        name="prepare",
-        compiler_params=PARAMS,
-        grid=(1,),
-        out_shape=outs,
-        in_specs=[pl.BlockSpec(own, lambda i: (0, 0, 0)), pl.BlockSpec(slab, lambda i: (0, 0, 0))],
-        out_specs=[pl.BlockSpec(o.shape, lambda i: (0, 0, 0)) for o in outs],
-    )(coupling, slabs)
-
-
 def copies_body(*refs):
     *ins, out = refs
     total = ins[0][...]
@@ -137,15 +117,15 @@
     return call(copies_body, f32(n, *parts[0].shape), *parts)
 
 
-def total_body(x_ref, o_ref):
-    total = x_ref[0]
-    for i in range(1, x_ref.shape[0]):
-        total = total + x_ref[i]
-    o_ref[...] = total
-
-
-def total(x):
-    return call(total_body, f32(*x.shape[1:]), x)
+def total_body(x_ref, *outs):
+    at = 0
+    for out in outs:
+        rows = slice(at, at + out.shape[0])
+        total = x_ref[0, rows]
+        for i in range(1, x_ref.shape[0]):
+            total = total + x_ref[i, rows]
+        out[...] = total
+        at += out.shape[0]
 
 
 def solve_body(inv_ref, panel_ref, o_ref):
@@ -154,8 +134,34 @@
         o_ref[i] = rows
 
 
-def product_body(a_ref, b_ref, o_ref):
-    o_ref[...] = dot(a_ref[...], b_ref[...], 0, 0).reshape(o_ref.shape)
+def halves(x):
+    high = x.astype(jnp.bfloat16)
+    return high, (x - high.astype(jnp.float32)).astype(jnp.bfloat16)
+
+
+def dot_halves(a, b, da, db):
+    one = lambda p, q: lax.dot_general(
+        p, q, (((da,), (db,)), ((), ())), preferred_element_type=jnp.float32
+    )
+    return one(a[0], b[0]) + (one(a[0], b[1]) + one(a[1], b[0]))
+
+
+def turn_body(own_ref, panel_ref, high_ref, low_ref):
+    at = 0
+    for x in (own_ref[0], panel_ref[...]):
+        rows = slice(at, at + x.shape[1])
+        high_ref[rows], low_ref[rows] = halves(x.T)
+        at += x.shape[1]
+
+
+def terms_body(high_ref, low_ref, solved_ref, o_ref):
+    width = high_ref.shape[0] - PANEL
+    s = halves(solved_ref[...])
+    n = o_ref.shape[0]
+    for at, rows, out in ((0, width, 0), (width, PANEL, width // n)):
+        part = slice(at, at + rows)
+        x = dot_halves((high_ref[part], low_ref[part]), s, 1, 0)
+        o_ref[:, out : out + rows // n] = x.reshape(n, rows // n, PANEL)
 
 
 def finish_body(top_ref, s_ref, m_ref, u_ref, o_ref, left):
@@ -165,9 +171,9 @@
     @pl.when(step == 0)
     def _():
         r, c = block((PANEL, PANEL), 0), block((PANEL, PANEL), 1)
-        left[...] = jnp.where(r >= c, m_ref[...], 0.0)
-
-    o_ref[...] = dot(s_ref[...], left[...], 1, 1)
+        left[0], left[1] = halves(jnp.where(r >= c, m_ref[...], 0.0))
+
+    o_ref[...] = dot_halves(halves(s_ref[...]), (left[0], left[1]), 1, 1)
 
     @pl.when((top_ref[0] == 1) & (step < PANEL // per))
     def _():
@@ -199,7 +205,7 @@
             whole(u),
         ],
         out_specs=pl.BlockSpec((per, PANEL), lambda i: (i, 0)),
-        scratch_shapes=[pltpu.VMEM((PANEL, PANEL), jnp.float32)],
+        scratch_shapes=[pltpu.VMEM((2, PANEL, PANEL), jnp.bfloat16)],
         cost_estimate=pl.CostEstimate(
             flops=2 * width * PANEL * PANEL, bytes_accessed=8 * width * PANEL, transcendentals=0
         ),
@@ -214,13 +220,13 @@
     y, zl = lax.axis_index("y"), lax.axis_index("zl")
     swap = functools.partial(lax.all_to_all, split_axis=0, concat_axis=0)
 
-    panel, slabs = prepare(coupling, inverse_slabs, n_y, n_zl)
-    inv = swap(slabs, "zl").reshape(-1, depth)
-
-    mine = jnp.where((y == 0) & (zl == 0), panel[0], 0.0)
+    per = depth // n_y
+    cut = lambda k: own[per * k : per * k + per, :PANEL]
     parts = []
     for k in range(1, n_y):
-        parts.append(lax.ppermute(panel[k], ("y", "zl"), [(0, k * n_zl)]))
+        parts.append(lax.ppermute(cut(k), ("y", "zl"), [(0, k * n_zl)]))
+    inv = swap(copies(n_zl, inverse_slabs[0]), "zl").reshape(-1, depth)
+    mine = jnp.where((y == 0) & (zl == 0), cut(0), 0.0)
     for part in parts:
         mine = mine + part
     step = n_zl // 2
@@ -238,21 +244,22 @@
     )
     solved = swap(solved, "y").reshape(depth, PANEL)
 
-    pivot = call(
-        product_body, f32(n_xc, PANEL // n_xc, PANEL), panel, solved,
-        flops=2 * PANEL * depth * PANEL,
-    )
-    pivot = total(swap(pivot, ("x", "core")))
+    high, low = call(
+        turn_body, [jax.ShapeDtypeStruct((width + PANEL, depth), jnp.bfloat16)] * 2,
+        coupling, panel, flops=10**9,
+    )
+    n_row, n_piv = width // n_xc, PANEL // n_xc
+    terms = call(
+        terms_body, f32(n_xc, n_row + n_piv, PANEL), high, low, solved,
+        flops=6 * (width + PANEL) * depth * PANEL,
+    )
+    terms = swap(terms, ("x", "core"))
+    rows, pivot = call(total_body, [f32(n_row, PANEL), f32(n_piv, PANEL)], terms)
+
     half = n_zl // 2
     flip = [(z, (z + (half if z // half % 2 else -half)) % n_z) for z in range(n_z)]
     other = lax.ppermute(pivot, ("zh", "zl"), flip)
     pivot = swap(copies(n_xc, pivot, other), ("x", "core")).reshape(PANEL, PANEL)
-
-    rows = call(
-        product_body, f32(n_xc, width // n_xc, PANEL), own, solved,
-        flops=2 * width * depth * PANEL,
-    )
-    rows = total(swap(rows, ("x", "core")))
     other = lax.ppermute(rows, "zh", [(0, 1), (1, 0)])
     rows = swap(copies(n_xc, rows, other), ("x", "core")).reshape(width, PANEL)
 

time: 145 us -> 149 us (1.028)
  waiting for transfers between devices: 17.7 us -> 30.7 us
  blocking collectives: 48.9 us -> 41.6 us
  starting transfers between devices: 54.3 us -> 52.8 us
    all_to_all x2, waiting for transfers between devices: 3.39 us -> 14.4 us  [the longest x1 8.06 us: shards(): panel = swap(copies(n_y, mine, got), 'y').reshape(depth, PANEL)]
    all_to_all x3 -> x2, blocking collectives: 48.9 us -> 41.6 us  [the longest x1 25.5 us: shards(): inv = swap(copies(n_zl, inverse_slabs[0]), 'zl').reshape(-1, depth)]
    all_to_all x2, starting transfers between devices: 11.5 us -> 8.68 us  [the longest x1 5.21 us: shards(): panel = swap(copies(n_y, mine, got), 'y').reshape(depth, PANEL)]
    ppermute x1, waiting for transfers between devices: 1.86 us -> 3.71 us  [shards(): other = lax.ppermute(rows, 'zh', [(0, 1), (1, 0)])]
  transfers between devices with their start and end apart: 12 -> 12, of which waited for: 8 -> 9; matrix products, arithmetic and copies ran while one was open for 0% -> 0% of each run, Pallas kernels for 10% -> 8%
where the time goes in v1:
time: 149 us; the launch traced here: 147 us
  starting transfers between devices  52.8 us (35%)
  blocking collectives  41.6 us (28%)
  waiting for transfers between devices  30.7 us (21%)
  Pallas kernels  18.1 us (12%)
  local copies, waits for them, and re-layouts  2.97 us (2%)
    all_to_all x1, blocking collectives, shards(): inv = swap(copies(n_zl, inverse_slabs[0]), 'zl').reshape(-1, depth)  25.5 us
    all_to_all x1, blocking collectives, shards(): terms = swap(terms, ('x', 'core'))  16.1 us
    pallas_call x9, Pallas kernels, call(): pl.pallas_call(body, compiler_params=PARAMS, out_shape=outs, in_specs=[VM...  15.5 us
    ppermute x1, starting transfers between devices, shards(): other = lax.ppermute(rows, 'zh', [(0, 1), (1, 0)])  12.9 us
    ppermute x1, starting transfers between devices, shards(): other = lax.ppermute(pivot, ('zh', 'zl'), flip)  9.96 us
    all_to_all x1, waiting for transfers between devices, shards(): panel = swap(copies(n_y, mine, got), 'y').reshape(depth, PANEL)  8.06 us
    ppermute x3, waiting for transfers between devices, shards(): got = lax.ppermute(mine, 'zl', pairs)  7.72 us
    ppermute x3, starting transfers between devices, shards(): parts.append(lax.ppermute(cut(k), ('y', 'zl'), [(0, k * n_zl)]))  7.07 us
  transfers between devices with their start and end apart: 12, of which 9 were waited for; matrix products, arithmetic and copies ran while one was open for 0% of the time, Pallas kernels for 8%

profile of v1, /device:TPU:6, one launch (start us, length us, event | category | flops | bytes accessed | tf_op | source)
XLA Modules:
  0.0 147.4 jit_solution(12903256766194949989)
XLA Ops:
  0.0 1.1 fusion.3
  1.1 3.5 %collective-permute-start = (f32[128,256]{1,0:T(8,128)S(1)}, f32[128,256]{1,0:T(8,128)S(1)}, u32[]{:S(2)}, u32[]{:S(2)}) collective-permute-start(f32[128,256]{1,0:T(8,128)S(1)} %get-tuple-element.17), channel_id=1, source_target_pairs={{0,8},{32,40},{64,72},{96,104},{128,136},{160,168},{192,200},{224,... | collective-permute-start | bytes 393224 | tf_op jit(solution)/shard_map/ppermute | solution.py:227
  4.6 2.3 %collective-permute-start.1 = (f32[128,256]{1,0:T(8,128)S(1)}, f32[128,256]{1,0:T(8,128)S(1)}, u32[]{:S(2)}, u32[]{:S(2)}) collective-permute-start(f32[128,256]{1,0:T(8,128)S(1)} %get-tuple-element.19), channel_id=1, source_target_pairs={{0,16},{32,48},{64,80},{96,112},{128,144},{160,176},{192,208},{224... | collective-permute-start | bytes 393224 | tf_op jit(solution)/shard_map/ppermute | solution.py:227
  6.8 1.3 collective-permute-start.2
  8.2 0.0 collective-permute-done
  8.2 1.9 %collective-permute-done.1 = f32[128,256]{1,0:T(8,128)S(1)} collective-permute-done((f32[128,256]{1,0:T(8,128)S(1)}, f32[128,256]{1,0:T(8,128)S(1)}, u32[]{:S(2)}, u32[]{:S(2)}) %collective-permute-start.1) | collective-permute-done | bytes 131104 | tf_op jit(solution)/shard_map/ppermute | solution.py:227
  10.1 0.8 collective-permute-done.2
  10.9 0.9 fusion.2
  11.8 1.4 collective-permute-start.3
  13.2 2.7 %collective-permute-done.3 = f32[128,256]{1,0:T(8,128)S(1)} collective-permute-done((f32[128,256]{1,0:T(8,128)S(1)}, f32[128,256]{1,0:T(8,128)S(1)}, u32[]{:S(2)}, u32[]{:S(2)}) %collective-permute-start.3) | collective-permute-done | bytes 131104 | tf_op jit(solution)/shard_map/ppermute | solution.py:235
  15.9 1.3 collective-permute-start.4
  17.2 2.5 %collective-permute-done.4 = f32[128,256]{1,0:T(8,128)S(1)} collective-permute-done((f32[128,256]{1,0:T(8,128)S(1)}, f32[128,256]{1,0:T(8,128)S(1)}, u32[]{:S(2)}, u32[]{:S(2)}) %collective-permute-start.4) | collective-permute-done | bytes 131104 | tf_op jit(solution)/shard_map/ppermute | solution.py:235
  19.8 1.3 collective-permute-start.5
  21.1 2.5 %collective-permute-done.5.refs_1_ = f32[128,256]{1,0:T(8,128)S(1)} collective-permute-done((f32[128,256]{1,0:T(8,128)S(1)}, f32[128,256]{1,0:T(8,128)S(1)}, u32[]{:S(2)}, u32[]{:S(2)}) %collective-permute-start.5) | collective-permute-done | bytes 131104 | tf_op jit(solution)/shard_map/ppermute | solution.py:235
  23.6 0.8 shard_map.37
  24.4 0.0 copy-start.1
  24.4 5.2 %all-to-all-start = ((f32[4,128,256]{2,1,0:T(8,128)}), f32[4,128,256]{2,1,0:T(8,128)S(1)}, u32[]{:S(2)}, u32[]{:S(2)}) async-start(f32[4,128,256]{2,1,0:T(8,128)} %shard_map.37), calls=%async_computation | async-start | bytes 1048576 | tf_op jit(solution)/shard_map/all_to_all | solution.py:239
  29.6 0.0 copy-done.1
  29.6 8.1 %all-to-all-done = f32[4,128,256]{2,1,0:T(8,128)S(1)} async-done(((f32[4,128,256]{2,1,0:T(8,128)}), f32[4,128,256]{2,1,0:T(8,128)S(1)}, u32[]{:S(2)}, u32[]{:S(2)}) %all-to-all-start) | async-done | bytes 524320 | tf_op jit(solution)/shard_map/all_to_all | solution.py:239
  37.7 25.5 %all_to_all.30 = f32[8,16,512]{2,1,0:T(8,128)S(1)} all-to-all(f32[8,16,512]{2,1,0:T(8,128)S(1)} %shard_map.39), channel_id=1, replica_groups=mesh['zh'=2,'x'=4,'core'=2,'y'=4,'zl'=8] {'zl'}, dimensions={0} | all-to-all | bytes 524288 | tf_op jit(solution)/shard_map/all_to_all | solution.py:228
  63.2 1.2 shard_map.40
  64.4 3.5 %all-to-all-start.2 = ((f32[4,128,256]{2,1,0:T(8,128)}), f32[4,128,256]{2,1,0:T(8,128)S(1)}, u32[]{:S(2)}, u32[]{:S(2)}) async-start(f32[4,128,256]{2,1,0:T(8,128)} %shard_map.40), calls=%async_computation.2 | async-start | bytes 1048576 | tf_op jit(solution)/shard_map/all_to_all | solution.py:245
  67.9 0.0 copy-start
  67.9 1.2 copy-done
  69.1 0.5 shard_map.38
  69.6 6.3 %all-to-all-done.2 = f32[4,128,256]{2,1,0:T(8,128)S(1)} async-done(((f32[4,128,256]{2,1,0:T(8,128)}), f32[4,128,256]{2,1,0:T(8,128)S(1)}, u32[]{:S(2)}, u32[]{:S(2)}) %all-to-all-start.2) | async-done | bytes 524320 | tf_op jit(solution)/shard_map/all_to_all | solution.py:245
  75.9 0.8 shard_map.41
  76.7 16.1 %all_to_all.31.x_ref = f32[8,96,256]{2,1,0:T(8,128)S(1)} all-to-all(f32[8,96,256]{2,1,0:T(8,128)S(1)} %shard_map.41), channel_id=1, replica_groups=mesh['zh'=2,'x'=4,'core'=2,'y'=4,'zl'=8] {'x','core'}, dimensions={0} | all-to-all | bytes 1572864 | tf_op jit(solution)/shard_map/all_to_all | solution.py:256
  92.9 10.0 %collective-permute-start.7 = (f32[32,256]{1,0:T(8,128)S(1)}, f32[32,256]{1,0:T(8,128)S(1)}, u32[]{:S(2)}, u32[]{:S(2)}) collective-permute-start(f32[32,256]{1,0:T(8,128)S(1)} %get-tuple-element.14.refs_0_), channel_id=1, source_target_pairs={{0,260},{1,261},{2,262},{3,263},{4,256},{5,257},{6,258},{7,259},{2... | collective-permute-start | bytes 98312 | tf_op jit(solution)/shard_map/ppermute | solution.py:261
  102.9 2.1 %collective-permute-done.7.refs_1_ = f32[32,256]{1,0:T(8,128)S(1)} collective-permute-done((f32[32,256]{1,0:T(8,128)S(1)}, f32[32,256]{1,0:T(8,128)S(1)}, u32[]{:S(2)}, u32[]{:S(2)}) %collective-permute-start.7) | collective-permute-done | bytes 32800 | tf_op jit(solution)/shard_map/ppermute | solution.py:261
  105.0 0.7 shard_map.44
  105.7 5.4 %all-to-all-start.5 = ((f32[8,32,256]{2,1,0:T(8,128)}), f32[8,32,256]{2,1,0:T(8,128)S(1)}, u32[]{:S(2)}, u32[]{:S(2)}) async-start(f32[8,32,256]{2,1,0:T(8,128)} %shard_map.44), calls=%async_computation.5 | async-start | bytes 524288 | tf_op jit(solution)/shard_map/all_to_all | solution.py:262
  111.2 12.9 %collective-permute-start.6 = (f32[64,256]{1,0:T(8,128)S(1)}, f32[64,256]{1,0:T(8,128)S(1)}, u32[]{:S(2)}, u32[]{:S(2)}) collective-permute-start(f32[64,256]{1,0:T(8,128)S(1)} %get-tuple-element.13.refs_0_), channel_id=1, source_target_pairs={{0,256},{256,0},{1,257},{257,1},{2,258},{258,2},{3,259},{259,3},{4... | collective-permute-start | bytes 196616 | tf_op jit(solution)/shard_map/ppermute | solution.py:263
  124.1 0.7 slice.19
  124.8 3.7 %collective-permute-done.6.refs_1_ = f32[64,256]{1,0:T(8,128)S(1)} collective-permute-done((f32[64,256]{1,0:T(8,128)S(1)}, f32[64,256]{1,0:T(8,128)S(1)}, u32[]{:S(2)}, u32[]{:S(2)}) %collective-permute-start.6) | collective-permute-done | bytes 65568 | tf_op jit(solution)/shard_map/ppermute | solution.py:263
  128.5 0.8 shard_map.43
  129.3 0.0 all-to-all-done.5
  129.3 4.8 %all-to-all-start.4 = ((f32[8,64,256]{2,1,0:T(8,128)}), f32[8,64,256]{2,1,0:T(8,128)S(1)}, u32[]{:S(2)}, u32[]{:S(2)}) async-start(f32[8,64,256]{2,1,0:T(8,128)} %shard_map.43), calls=%async_computation.4 | async-start | bytes 1048576 | tf_op jit(solution)/shard_map/all_to_all | solution.py:264
  134.1 10.5 %shard_map.45 = (f32[256,256]{1,0:T(8,128)S(1)}, f32[256,128]{1,0:T(8,128)S(1)}) custom-call(f32[256,256]{1,0:T(8,128)S(1)} %bitcast.16, f32[1,256]{1,0:T(1,128)S(1)} %bitcast.18), custom_call_target="tpu_custom_call" | custom-call | flops 6000000000 | bytes 263168 | tf_op jit(solution)/shard_map/pallas_call | solution.py:31
  144.7 0.0 all-to-all-done.4
  144.7 2.7 %finish.1 = f32[512,256]{1,0:T(8,128)} custom-call(s32[1]{0:T(128)} %bitcast.top_ref, f32[512,256]{1,0:T(8,128)S(1)} %bitcast.11, f32[256,256]{1,0:T(8,128)S(1)} %get-tuple-element.15.m_ref, f32[256,128]{1,0:T(8,128)S(1)} %get-tuple-element.16.u_ref), custom_call_target="tpu_custom_call" | custom-call | flops 67108864 | bytes 1048576 | tf_op jit(solution)/shard_map/finish/pallas_call | solution.py:195
  (4 shorter events, 0.1 us)
Async XLA Ops:
  1.1 7.1 %collective-permute-start = (f32[128,256]{1,0:T(8,128)S(1)}, f32[128,256]{1,0:T(8,128)S(1)}, u32[]{:S(2)}, u32[]{:S(2)}) collective-permute-start(f32[128,256]{1,0:T(8,128)S(1)} %get-tuple-element.17), channel_id=1, source_target_pairs={{0,8},{32,40},{64,72},{96,104},{128,136},{160,168},{192,200},{224,... | collective-permute-start | bytes 393224 | tf_op jit(solution)/shard_map/ppermute | solution.py:227
  4.6 5.5 %collective-permute-start.1 = (f32[128,256]{1,0:T(8,128)S(1)}, f32[128,256]{1,0:T(8,128)S(1)}, u32[]{:S(2)}, u32[]{:S(2)}) collective-permute-start(f32[128,256]{1,0:T(8,128)S(1)} %get-tuple-element.19), channel_id=1, source_target_pairs={{0,16},{32,48},{64,80},{96,112},{128,144},{160,176},{192,208},{224... | collective-permute-start | bytes 393224 | tf_op jit(solution)/shard_map/ppermute | solution.py:227
  6.8 4.0 %collective-permute-start.2 = (f32[128,256]{1,0:T(8,128)S(1)}, f32[128,256]{1,0:T(8,128)S(1)}, u32[]{:S(2)}, u32[]{:S(2)}) collective-permute-start(f32[128,256]{1,0:T(8,128)S(1)} %get-tuple-element.18), channel_id=1, source_target_pairs={{0,24},{32,56},{64,88},{96,120},{128,152},{160,184},{192,216},{224... | collective-permute-start | bytes 393224 | tf_op jit(solution)/shard_map/ppermute | solution.py:227
  11.8 4.1 %collective-permute-start.3 = (f32[128,256]{1,0:T(8,128)S(1)}, f32[128,256]{1,0:T(8,128)S(1)}, u32[]{:S(2)}, u32[]{:S(2)}) collective-permute-start(f32[128,256]{1,0:T(8,128)S(1)} %fusion.2), channel_id=1, source_target_pairs={{0,4},{8,12},{16,20},{24,28},{32,36},{40,44},{48,52},{56,60},{64,6... | collective-permute-start | bytes 393224 | tf_op jit(solution)/shard_map/ppermute | solution.py:235
  15.9 3.8 %collective-permute-start.4 = (f32[128,256]{1,0:T(8,128)S(1)}, f32[128,256]{1,0:T(8,128)S(1)}, u32[]{:S(2)}, u32[]{:S(2)}) collective-permute-start(f32[128,256]{1,0:T(8,128)S(1)} %add.18), channel_id=1, source_target_pairs={{0,2},{4,6},{8,10},{12,14},{16,18},{20,22},{24,26},{28,30},{32,34}... | collective-permute-start | bytes 393224 | tf_op jit(solution)/shard_map/ppermute | solution.py:235
  19.8 3.8 %collective-permute-start.5 = (f32[128,256]{1,0:T(8,128)S(1)}, f32[128,256]{1,0:T(8,128)S(1)}, u32[]{:S(2)}, u32[]{:S(2)}) collective-permute-start(f32[128,256]{1,0:T(8,128)S(1)} %add.19.refs_0_), channel_id=1, source_target_pairs={{0,1},{2,3},{4,5},{6,7},{8,9},{10,11},{12,13},{14,15},{16,17},{18,... | collective-permute-start | bytes 393224 | tf_op jit(solution)/shard_map/ppermute | solution.py:235
  24.4 5.2 %copy-start.1 = (f32[1,16,512]{2,1,0:T(8,128)S(1)}, f32[1,16,512]{2,1,0:T(8,128)}, u32[]{:S(2)}) copy-start(f32[1,16,512]{2,1,0:T(8,128)} %param.4) | copy-start | bytes 98308
  24.4 13.3 %all-to-all-start = ((f32[4,128,256]{2,1,0:T(8,128)}), f32[4,128,256]{2,1,0:T(8,128)S(1)}, u32[]{:S(2)}, u32[]{:S(2)}) async-start(f32[4,128,256]{2,1,0:T(8,128)} %shard_map.37), calls=%async_computation | async-start | bytes 1048576 | tf_op jit(solution)/shard_map/all_to_all | solution.py:239
  64.4 11.5 %all-to-all-start.2 = ((f32[4,128,256]{2,1,0:T(8,128)}), f32[4,128,256]{2,1,0:T(8,128)S(1)}, u32[]{:S(2)}, u32[]{:S(2)}) async-start(f32[4,128,256]{2,1,0:T(8,128)} %shard_map.40), calls=%async_computation.2 | async-start | bytes 1048576 | tf_op jit(solution)/shard_map/all_to_all | solution.py:245
  67.9 1.2 copy-start
  92.9 12.1 %collective-permute-start.7 = (f32[32,256]{1,0:T(8,128)S(1)}, f32[32,256]{1,0:T(8,128)S(1)}, u32[]{:S(2)}, u32[]{:S(2)}) collective-permute-start(f32[32,256]{1,0:T(8,128)S(1)} %get-tuple-element.14.refs_0_), channel_id=1, source_target_pairs={{0,260},{1,261},{2,262},{3,263},{4,256},{5,257},{6,258},{7,259},{2... | collective-permute-start | bytes 98312 | tf_op jit(solution)/shard_map/ppermute | solution.py:261
  105.7 23.6 %all-to-all-start.5 = ((f32[8,32,256]{2,1,0:T(8,128)}), f32[8,32,256]{2,1,0:T(8,128)S(1)}, u32[]{:S(2)}, u32[]{:S(2)}) async-start(f32[8,32,256]{2,1,0:T(8,128)} %shard_map.44), calls=%async_computation.5 | async-start | bytes 524288 | tf_op jit(solution)/shard_map/all_to_all | solution.py:262
  111.2 17.3 %collective-permute-start.6 = (f32[64,256]{1,0:T(8,128)S(1)}, f32[64,256]{1,0:T(8,128)S(1)}, u32[]{:S(2)}, u32[]{:S(2)}) collective-permute-start(f32[64,256]{1,0:T(8,128)S(1)} %get-tuple-element.13.refs_0_), channel_id=1, source_target_pairs={{0,256},{256,0},{1,257},{257,1},{2,258},{258,2},{3,259},{259,3},{4... | collective-permute-start | bytes 196616 | tf_op jit(solution)/shard_map/ppermute | solution.py:263
  129.3 15.3 %all-to-all-start.4 = ((f32[8,64,256]{2,1,0:T(8,128)}), f32[8,64,256]{2,1,0:T(8,128)S(1)}, u32[]{:S(2)}, u32[]{:S(2)}) async-start(f32[8,64,256]{2,1,0:T(8,128)} %shard_map.43), calls=%async_computation.4 | async-start | bytes 1048576 | tf_op jit(solution)/shard_map/all_to_all | solution.py:264

commit v2 on v1

--- a/solution.py
+++ b/solution.py
@@ -20,10 +20,8 @@
     return jax.ShapeDtypeStruct(shape, jnp.float32)
 
 
-def dot(a, b, da, db):
-    return lax.dot_general(
-        a, b, (((da,), (db,)), ((), ())), precision=HIGHEST, preferred_element_type=jnp.float32
-    )
+def bf16(*shape):
+    return jax.ShapeDtypeStruct(shape, jnp.bfloat16)
 
 
 def call(body, outs, *args, flops=0):
@@ -72,10 +70,15 @@
 
 
 def factor_body(p_ref, diag_ref, m_ref, u_ref):
-    a = p_ref[...]
-    r = lax.broadcasted_iota(jnp.int32, (PANEL, PANEL), 0)
-    c = lax.broadcasted_iota(jnp.int32, (PANEL, PANEL), 1)
-    m_ref[...] = 0.5 * (a + a.T) + jnp.where(r == c, diag_ref[...], 0.0)
+    half = PANEL // 2
+    r = lax.broadcasted_iota(jnp.int32, (half, PANEL), 0)
+    c = lax.broadcasted_iota(jnp.int32, (half, PANEL), 1)
+    diag = diag_ref[...]
+    m_ref[:half] = p_ref[:half] + jnp.where(r == c, diag, 0.0)
+    last = p_ref[half:]
+    last = jnp.concatenate([last[:, :half], last[:, half:]], axis=0)
+    last = jnp.concatenate([jnp.zeros_like(last), last], axis=1)
+    m_ref[half:] = last + jnp.where(r + half == c, diag, 0.0)
     lane = lax.broadcasted_iota(jnp.int32, (BLOCK, LANES), 1)
     sub = lax.broadcasted_iota(jnp.int32, (BLOCK, LANES), 0)
     wlane = lax.broadcasted_iota(jnp.int32, (BLOCK, PANEL), 1)
@@ -113,6 +116,14 @@
         out[i] = total
 
 
+def sum_body(*refs):
+    *ins, out = refs
+    total = ins[0][...]
+    for ref in ins[1:]:
+        total = total + ref[...]
+    out[...] = total
+
+
 def copies(n, *parts):
     return call(copies_body, f32(n, *parts[0].shape), *parts)
 
@@ -128,12 +139,6 @@
         at += out.shape[0]
 
 
-def solve_body(inv_ref, panel_ref, o_ref):
-    rows = dot(inv_ref[...], panel_ref[...], 1, 0)
-    for i in range(o_ref.shape[0]):
-        o_ref[i] = rows
-
-
 def halves(x):
     high = x.astype(jnp.bfloat16)
     return high, (x - high.astype(jnp.float32)).astype(jnp.bfloat16)
@@ -146,22 +151,44 @@
     return one(a[0], b[0]) + (one(a[0], b[1]) + one(a[1], b[0]))
 
 
-def turn_body(own_ref, panel_ref, high_ref, low_ref):
-    at = 0
-    for x in (own_ref[0], panel_ref[...]):
-        rows = slice(at, at + x.shape[1])
-        high_ref[rows], low_ref[rows] = halves(x.T)
-        at += x.shape[1]
-
-
-def terms_body(high_ref, low_ref, solved_ref, o_ref):
-    width = high_ref.shape[0] - PANEL
-    s = halves(solved_ref[...])
-    n = o_ref.shape[0]
-    for at, rows, out in ((0, width, 0), (width, PANEL, width // n)):
-        part = slice(at, at + rows)
-        x = dot_halves((high_ref[part], low_ref[part]), s, 1, 0)
-        o_ref[:, out : out + rows // n] = x.reshape(n, rows // n, PANEL)
+def turn_body(own_ref, turned_ref):
+    turned_ref[0], turned_ref[1] = halves(own_ref[0].T)
+
+
+def terms_body(turned_ref, inv_ref, panel_ref, o_ref, turned, sem):
+    fetch = pltpu.make_async_copy(turned_ref, turned, sem)
+    fetch.start()
+    panel = panel_ref[...]
+    n, half = o_ref.shape[0], PANEL // 2
+    s = halves(dot_halves(halves(inv_ref[...]), halves(panel), 1, 0))
+    x = dot_halves(halves(panel.T), s, 1, 0)
+    last = jnp.concatenate(
+        [x[half : half + half // 2, half:], x[half + half // 2 :, half:]], axis=1
+    )
+    x = jnp.concatenate([x[:half], last], axis=0)
+    rows = turned.shape[1] // n
+    o_ref[:, rows:] = x.reshape(n, x.shape[0] // n, PANEL)
+    fetch.wait()
+    x = dot_halves((turned[0], turned[1]), s, 1, 0)
+    o_ref[:, :rows] = x.reshape(n, rows, PANEL)
+
+
+def multiply(turned, inv, panel, n):
+    _, width, depth = turned.shape
+    return pl.pallas_call(
+        terms_body,
+        name="terms",
+        out_shape=f32(n, (width + 3 * PANEL // 4) // n, PANEL),
+        compiler_params=PARAMS,
+        in_specs=[pl.BlockSpec(memory_space=pltpu.HBM), VMEM, VMEM],
+        out_specs=VMEM,
+        scratch_shapes=[pltpu.VMEM(turned.shape, turned.dtype), pltpu.SemaphoreType.DMA],
+        cost_estimate=pl.CostEstimate(
+            flops=6 * (width + PANEL + depth) * depth * PANEL,
+            bytes_accessed=4 * depth * (width + depth),
+            transcendentals=0,
+        ),
+    )(pltpu.with_memory_space_constraint(turned, pltpu.HBM), inv, panel)
 
 
 def finish_body(top_ref, s_ref, m_ref, u_ref, o_ref, left):
@@ -226,9 +253,9 @@
     for k in range(1, n_y):
         parts.append(lax.ppermute(cut(k), ("y", "zl"), [(0, k * n_zl)]))
     inv = swap(copies(n_zl, inverse_slabs[0]), "zl").reshape(-1, depth)
-    mine = jnp.where((y == 0) & (zl == 0), cut(0), 0.0)
-    for part in parts:
-        mine = mine + part
+    inv = swap(copies(n_y, inv), "y").reshape(depth, depth)
+    first = jnp.where((y == 0) & (zl == 0), cut(0), 0.0)
+    mine = call(sum_body, f32(per, PANEL), first, *parts)
     step = n_zl // 2
     while step:
         pairs = [(j, j + step) for j in range(0, n_zl, 2 * step)]
@@ -238,28 +265,16 @@
         step //= 2
     panel = swap(copies(n_y, mine, got), "y").reshape(depth, PANEL)
 
-    solved = call(
-        solve_body, f32(n_y, depth // n_y, PANEL), inv, panel,
-        flops=2 * depth // n_y * depth * PANEL,
-    )
-    solved = swap(solved, "y").reshape(depth, PANEL)
-
-    high, low = call(
-        turn_body, [jax.ShapeDtypeStruct((width + PANEL, depth), jnp.bfloat16)] * 2,
-        coupling, panel, flops=10**9,
-    )
-    n_row, n_piv = width // n_xc, PANEL // n_xc
-    terms = call(
-        terms_body, f32(n_xc, n_row + n_piv, PANEL), high, low, solved,
-        flops=6 * (width + PANEL) * depth * PANEL,
-    )
+    turned = call(turn_body, bf16(2, width, depth), coupling, flops=2 * 10**9)
+    n_row, n_piv = width // n_xc, 3 * PANEL // 4 // n_xc
+    terms = multiply(turned, inv, panel, n_xc)
     terms = swap(terms, ("x", "core"))
     rows, pivot = call(total_body, [f32(n_row, PANEL), f32(n_piv, PANEL)], terms)
 
     half = n_zl // 2
     flip = [(z, (z + (half if z // half % 2 else -half)) % n_z) for z in range(n_z)]
     other = lax.ppermute(pivot, ("zh", "zl"), flip)
-    pivot = swap(copies(n_xc, pivot, other), ("x", "core")).reshape(PANEL, PANEL)
+    pivot = swap(copies(n_xc, pivot, other), ("x", "core")).reshape(-1, PANEL)
     other = lax.ppermute(rows, "zh", [(0, 1), (1, 0)])
     rows = swap(copies(n_xc, rows, other), ("x", "core")).reshape(width, PANEL)
 

time: 149 us -> 137 us (0.919)
  blocking collectives: 41.6 us -> 15 us
  waiting for transfers between devices: 30.7 us -> 37 us
  starting transfers between devices: 52.8 us -> 58.6 us
  Pallas kernels: 18.1 us -> 20.6 us
    all_to_all x1 -> x0, blocking collectives: 25.5 us -> none  [shards(): inv = swap(copies(n_zl, inverse_slabs[0]), 'zl').reshape(-1, depth)]
    all_to_all x2 -> x3, starting transfers between devices: 8.89 us -> 21.4 us  [the longest x1 12.5 us: shards(): inv = swap(copies(n_zl, inverse_slabs[0]), 'zl').reshape(-1, depth)]
    ppermute x1, starting transfers between devices: 12.9 us -> 6.6 us  [shards(): other = lax.ppermute(rows, 'zh', [(0, 1), (1, 0)])]
    ppermute x1, waiting for transfers between devices: 3.71 us -> 7.69 us  [shards(): other = lax.ppermute(rows, 'zh', [(0, 1), (1, 0)])]
    all_to_all x2 -> x3, waiting for transfers between devices: 6.34 us -> 9.51 us  [the longest x1 9.5 us: shards(): inv = swap(copies(n_y, inv), 'y').reshape(depth, depth)]
    pallas_call x0 -> x1, Pallas kernels: none -> 3.01 us  [multiply(): pl.pallas_call(terms_body, name='terms', out_shape=f32(n, (width + 3 * PA...]
  transfers between devices with their start and end apart: 12 -> 13, of which waited for: 9 -> 9; matrix products, arithmetic and copies ran while one was open for 0% -> 1% of each run, Pallas kernels for 8% -> 10%
where the time goes in v2:
time: 137 us; the launch traced here: 135 us
  starting transfers between devices  58.6 us (43%)
  waiting for transfers between devices  37 us (27%)
  Pallas kernels  20.6 us (15%)
  blocking collectives  15 us (11%)
  local copies, waits for them, and re-layouts  2.44 us (2%)
    all_to_all x1, blocking collectives, shards(): terms = swap(terms, ('x', 'core'))  15 us
    pallas_call x9, Pallas kernels, call(): pl.pallas_call(body, compiler_params=PARAMS, out_shape=outs, in_specs=[VM...  14.9 us
    all_to_all x1, starting transfers between devices, shards(): inv = swap(copies(n_zl, inverse_slabs[0]), 'zl').reshape(-1, depth)  12.5 us
    all_to_all x1, waiting for transfers between devices, shards(): inv = swap(copies(n_y, inv), 'y').reshape(depth, depth)  9.5 us
    ppermute x1, starting transfers between devices, shards(): other = lax.ppermute(pivot, ('zh', 'zl'), flip)  9.29 us
    ppermute x3, waiting for transfers between devices, shards(): got = lax.ppermute(mine, 'zl', pairs)  8.27 us
    ppermute x1, waiting for transfers between devices, shards(): other = lax.ppermute(rows, 'zh', [(0, 1), (1, 0)])  7.69 us
    ppermute x3, starting transfers between devices, shards(): parts.append(lax.ppermute(cut(k), ('y', 'zl'), [(0, k * n_zl)]))  7.07 us
  transfers between devices with their start and end apart: 13, of which 9 were waited for; matrix products, arithmetic and copies ran while one was open for 1% of the time, Pallas kernels for 10%

profile of v2, /device:TPU:6, one launch (start us, length us, event | category | flops | bytes accessed | tf_op | source)
XLA Modules:
  0.0 134.9 jit_solution(7548984126492753011)
XLA Ops:
  0.0 0.0 copy-start.1
  0.0 0.8 copy-done.1
  0.8 0.7 shard_map.38
  1.5 12.5 %all-to-all-start = ((f32[8,16,512]{2,1,0:T(8,128)}), f32[8,16,512]{2,1,0:T(8,128)S(1)}, u32[]{:S(2)}, u32[]{:S(2)}) async-start(f32[8,16,512]{2,1,0:T(8,128)} %shard_map.38), calls=%async_computation | async-start | bytes 524288 | tf_op jit(solution)/shard_map/all_to_all | solution.py:255
  14.0 1.1 fusion
  15.1 3.5 %collective-permute-start = (f32[128,256]{1,0:T(8,128)S(1)}, f32[128,256]{1,0:T(8,128)S(1)}, u32[]{:S(2)}, u32[]{:S(2)}) collective-permute-start(f32[128,256]{1,0:T(8,128)S(1)} %get-tuple-element.15), channel_id=1, source_target_pairs={{0,8},{32,40},{64,72},{96,104},{128,136},{160,168},{192,200},{224,... | collective-permute-start | bytes 393224 | tf_op jit(solution)/shard_map/ppermute | solution.py:254
  18.6 2.3 %collective-permute-start.1 = (f32[128,256]{1,0:T(8,128)S(1)}, f32[128,256]{1,0:T(8,128)S(1)}, u32[]{:S(2)}, u32[]{:S(2)}) collective-permute-start(f32[128,256]{1,0:T(8,128)S(1)} %get-tuple-element.14), channel_id=1, source_target_pairs={{0,16},{32,48},{64,80},{96,112},{128,144},{160,176},{192,208},{224... | collective-permute-start | bytes 393224 | tf_op jit(solution)/shard_map/ppermute | solution.py:254
  20.9 1.3 collective-permute-start.2
  22.2 0.0 collective-permute-done.refs_1_
  22.3 1.7 %collective-permute-done.1.refs_2_ = f32[128,256]{1,0:T(8,128)S(1)} collective-permute-done((f32[128,256]{1,0:T(8,128)S(1)}, f32[128,256]{1,0:T(8,128)S(1)}, u32[]{:S(2)}, u32[]{:S(2)}) %collective-permute-start.1) | collective-permute-done | bytes 131104 | tf_op jit(solution)/shard_map/ppermute | solution.py:254
  23.9 0.8 collective-permute-done.2.refs_3_
  24.8 1.3 collective-permute-start.3
  26.1 2.6 %collective-permute-done.3 = f32[128,256]{1,0:T(8,128)S(1)} collective-permute-done((f32[128,256]{1,0:T(8,128)S(1)}, f32[128,256]{1,0:T(8,128)S(1)}, u32[]{:S(2)}, u32[]{:S(2)}) %collective-permute-start.3) | collective-permute-done | bytes 131104 | tf_op jit(solution)/shard_map/ppermute | solution.py:262
  28.7 1.3 collective-permute-start.4
  30.0 3.2 %collective-permute-done.4 = f32[128,256]{1,0:T(8,128)S(1)} collective-permute-done((f32[128,256]{1,0:T(8,128)S(1)}, f32[128,256]{1,0:T(8,128)S(1)}, u32[]{:S(2)}, u32[]{:S(2)}) %collective-permute-start.4) | collective-permute-done | bytes 131104 | tf_op jit(solution)/shard_map/ppermute | solution.py:262
  33.2 1.3 collective-permute-start.5
  34.5 2.5 %collective-permute-done.5.refs_1_ = f32[128,256]{1,0:T(8,128)S(1)} collective-permute-done((f32[128,256]{1,0:T(8,128)S(1)}, f32[128,256]{1,0:T(8,128)S(1)}, u32[]{:S(2)}, u32[]{:S(2)}) %collective-permute-start.5) | collective-permute-done | bytes 131104 | tf_op jit(solution)/shard_map/ppermute | solution.py:262
  37.0 0.8 shard_map.41
  37.8 0.0 all-to-all-done
  37.8 5.5 %all-to-all-start.2 = ((f32[4,128,256]{2,1,0:T(8,128)}), f32[4,128,256]{2,1,0:T(8,128)S(1)}, u32[]{:S(2)}, u32[]{:S(2)}) async-start(f32[4,128,256]{2,1,0:T(8,128)} %shard_map.41), calls=%async_computation.2 | async-start | bytes 1048576 | tf_op jit(solution)/shard_map/all_to_all | solution.py:266
  43.4 1.0 shard_map.39
  44.4 0.0 copy-start
  44.4 7.0 %all-to-all-done.2 = f32[4,128,256]{2,1,0:T(8,128)S(1)} async-done(((f32[4,128,256]{2,1,0:T(8,128)}), f32[4,128,256]{2,1,0:T(8,128)S(1)}, u32[]{:S(2)}, u32[]{:S(2)}) %all-to-all-start.2) | async-done | bytes 524320 | tf_op jit(solution)/shard_map/all_to_all | solution.py:266
  51.4 3.5 %all-to-all-start.1 = ((f32[4,128,512]{2,1,0:T(8,128)}), f32[4,128,512]{2,1,0:T(8,128)S(1)}, u32[]{:S(2)}, u32[]{:S(2)}) async-start(f32[4,128,512]{2,1,0:T(8,128)} %shard_map.39), calls=%async_computation.1 | async-start | bytes 2097152 | tf_op jit(solution)/shard_map/all_to_all | solution.py:256
  55.0 0.0 copy-done
  55.0 0.3 shard_map.37.turned_ref
  55.3 0.0 copy-start.2
  55.3 1.0 copy-done.2
  56.3 9.5 %all-to-all-done.1 = f32[4,128,512]{2,1,0:T(8,128)S(1)} async-done(((f32[4,128,512]{2,1,0:T(8,128)}), f32[4,128,512]{2,1,0:T(8,128)S(1)}, u32[]{:S(2)}, u32[]{:S(2)}) %all-to-all-start.1) | async-done | bytes 1048608 | tf_op jit(solution)/shard_map/all_to_all | solution.py:256
  65.8 3.0 %terms.1 = f32[8,88,256]{2,1,0:T(8,128)S(1)} custom-call(bf16[2,512,512]{2,1,0:T(8,128)(2,1)} %copy-done.2, f32[512,512]{1,0:T(8,128)S(1)} %bitcast.11, f32[512,256]{1,0:T(8,128)S(1)} %bitcast.12), custom_call_target="tpu_custom_call" | custom-call | flops 1006632960 | bytes 2097152 | tf_op jit(solution)/shard_map/terms/pallas_call | solution.py:178
  68.8 15.0 %all_to_all.30.x_ref = f32[8,88,256]{2,1,0:T(8,128)S(1)} all-to-all(f32[8,88,256]{2,1,0:T(8,128)S(1)} %terms.1), channel_id=1, replica_groups=mesh['zh'=2,'x'=4,'core'=2,'y'=4,'zl'=8] {'x','core'}, dimensions={0} | all-to-all | bytes 1441792 | tf_op jit(solution)/shard_map/all_to_all | solution.py:271
  83.8 9.3 %collective-permute-start.7 = (f32[24,256]{1,0:T(8,128)S(1)}, f32[24,256]{1,0:T(8,128)S(1)}, u32[]{:S(2)}, u32[]{:S(2)}) collective-permute-start(f32[24,256]{1,0:T(8,128)S(1)} %get-tuple-element.10.refs_0_), channel_id=1, source_target_pairs={{0,260},{1,261},{2,262},{3,263},{4,256},{5,257},{6,258},{7,259},{2... | collective-permute-start | bytes 73736 | tf_op jit(solution)/shard_map/ppermute | solution.py:276
  93.1 1.9 %collective-permute-done.7.refs_1_ = f32[24,256]{1,0:T(8,128)S(1)} collective-permute-done((f32[24,256]{1,0:T(8,128)S(1)}, f32[24,256]{1,0:T(8,128)S(1)}, u32[]{:S(2)}, u32[]{:S(2)}) %collective-permute-start.7) | collective-permute-done | bytes 24608 | tf_op jit(solution)/shard_map/ppermute | solution.py:276
  95.1 0.7 shard_map.44
  95.8 5.4 %all-to-all-start.5 = ((f32[8,24,256]{2,1,0:T(8,128)}), f32[8,24,256]{2,1,0:T(8,128)S(1)}, u32[]{:S(2)}, u32[]{:S(2)}) async-start(f32[8,24,256]{2,1,0:T(8,128)} %shard_map.44), calls=%async_computation.5 | async-start | bytes 393216 | tf_op jit(solution)/shard_map/all_to_all | solution.py:277
  101.2 6.6 %collective-permute-start.6 = (f32[64,256]{1,0:T(8,128)S(1)}, f32[64,256]{1,0:T(8,128)S(1)}, u32[]{:S(2)}, u32[]{:S(2)}) collective-permute-start(f32[64,256]{1,0:T(8,128)S(1)} %get-tuple-element.9.refs_0_), channel_id=1, source_target_pairs={{0,256},{256,0},{1,257},{257,1},{2,258},{258,2},{3,259},{259,3},{4... | collective-permute-start | bytes 196616 | tf_op jit(solution)/shard_map/ppermute | solution.py:278
  107.8 0.7 slice.19
  108.5 7.7 %collective-permute-done.6.refs_1_ = f32[64,256]{1,0:T(8,128)S(1)} collective-permute-done((f32[64,256]{1,0:T(8,128)S(1)}, f32[64,256]{1,0:T(8,128)S(1)}, u32[]{:S(2)}, u32[]{:S(2)}) %collective-permute-start.6) | collective-permute-done | bytes 65568 | tf_op jit(solution)/shard_map/ppermute | solution.py:278
  116.2 0.8 shard_map.43
  117.0 0.0 all-to-all-done.5
  117.0 4.8 %all-to-all-start.4 = ((f32[8,64,256]{2,1,0:T(8,128)}), f32[8,64,256]{2,1,0:T(8,128)S(1)}, u32[]{:S(2)}, u32[]{:S(2)}) async-start(f32[8,64,256]{2,1,0:T(8,128)} %shard_map.43), calls=%async_computation.4 | async-start | bytes 1048576 | tf_op jit(solution)/shard_map/all_to_all | solution.py:279
  121.8 10.4 %shard_map.45 = (f32[256,256]{1,0:T(8,128)S(1)}, f32[256,128]{1,0:T(8,128)S(1)}) custom-call(f32[192,256]{1,0:T(8,128)S(1)} %bitcast.14, f32[1,256]{1,0:T(1,128)S(1)} %bitcast.16), custom_call_target="tpu_custom_call" | custom-call | flops 6000000000 | bytes 197632 | tf_op jit(solution)/shard_map/pallas_call | solution.py:29
  132.2 0.0 all-to-all-done.4
  132.2 2.7 %finish.1 = f32[512,256]{1,0:T(8,128)} custom-call(s32[1]{0:T(128)} %bitcast.top_ref, f32[512,256]{1,0:T(8,128)S(1)} %bitcast.9, f32[256,256]{1,0:T(8,128)S(1)} %get-tuple-element.11.m_ref, f32[256,128]{1,0:T(8,128)S(1)} %get-tuple-element.12.u_ref), custom_call_target="tpu_custom_call" | custom-call | flops 67108864 | bytes 1048576 | tf_op jit(solution)/shard_map/finish/pallas_call | solution.py:222
  (4 shorter events, 0.1 us)
Async XLA Ops:
  0.0 0.8 copy-start.1
  1.5 36.4 %all-to-all-start = ((f32[8,16,512]{2,1,0:T(8,128)}), f32[8,16,512]{2,1,0:T(8,128)S(1)}, u32[]{:S(2)}, u32[]{:S(2)}) async-start(f32[8,16,512]{2,1,0:T(8,128)} %shard_map.38), calls=%async_computation | async-start | bytes 524288 | tf_op jit(solution)/shard_map/all_to_all | solution.py:255
  15.1 7.1 %collective-permute-start = (f32[128,256]{1,0:T(8,128)S(1)}, f32[128,256]{1,0:T(8,128)S(1)}, u32[]{:S(2)}, u32[]{:S(2)}) collective-permute-start(f32[128,256]{1,0:T(8,128)S(1)} %get-tuple-element.15), channel_id=1, source_target_pairs={{0,8},{32,40},{64,72},{96,104},{128,136},{160,168},{192,200},{224,... | collective-permute-start | bytes 393224 | tf_op jit(solution)/shard_map/ppermute | solution.py:254
  18.6 5.3 %collective-permute-start.1 = (f32[128,256]{1,0:T(8,128)S(1)}, f32[128,256]{1,0:T(8,128)S(1)}, u32[]{:S(2)}, u32[]{:S(2)}) collective-permute-start(f32[128,256]{1,0:T(8,128)S(1)} %get-tuple-element.14), channel_id=1, source_target_pairs={{0,16},{32,48},{64,80},{96,112},{128,144},{160,176},{192,208},{224... | collective-permute-start | bytes 393224 | tf_op jit(solution)/shard_map/ppermute | solution.py:254
  20.9 3.8 %collective-permute-start.2 = (f32[128,256]{1,0:T(8,128)S(1)}, f32[128,256]{1,0:T(8,128)S(1)}, u32[]{:S(2)}, u32[]{:S(2)}) collective-permute-start(f32[128,256]{1,0:T(8,128)S(1)} %get-tuple-element.13), channel_id=1, source_target_pairs={{0,24},{32,56},{64,88},{96,120},{128,152},{160,184},{192,216},{224... | collective-permute-start | bytes 393224 | tf_op jit(solution)/shard_map/ppermute | solution.py:254
  24.8 3.9 %collective-permute-start.3 = (f32[128,256]{1,0:T(8,128)S(1)}, f32[128,256]{1,0:T(8,128)S(1)}, u32[]{:S(2)}, u32[]{:S(2)}) collective-permute-start(f32[128,256]{1,0:T(8,128)S(1)} %shard_map.40), channel_id=1, source_target_pairs={{0,4},{8,12},{16,20},{24,28},{32,36},{40,44},{48,52},{56,60},{64,6... | collective-permute-start | bytes 393224 | tf_op jit(solution)/shard_map/ppermute | solution.py:262
  28.7 4.5 %collective-permute-start.4 = (f32[128,256]{1,0:T(8,128)S(1)}, f32[128,256]{1,0:T(8,128)S(1)}, u32[]{:S(2)}, u32[]{:S(2)}) collective-permute-start(f32[128,256]{1,0:T(8,128)S(1)} %add.6), channel_id=1, source_target_pairs={{0,2},{4,6},{8,10},{12,14},{16,18},{20,22},{24,26},{28,30},{32,34}... | collective-permute-start | bytes 393224 | tf_op jit(solution)/shard_map/ppermute | solution.py:262
  33.2 3.8 %collective-permute-start.5 = (f32[128,256]{1,0:T(8,128)S(1)}, f32[128,256]{1,0:T(8,128)S(1)}, u32[]{:S(2)}, u32[]{:S(2)}) collective-permute-start(f32[128,256]{1,0:T(8,128)S(1)} %add.7.refs_0_), channel_id=1, source_target_pairs={{0,1},{2,3},{4,5},{6,7},{8,9},{10,11},{12,13},{14,15},{16,17},{18,... | collective-permute-start | bytes 393224 | tf_op jit(solution)/shard_map/ppermute | solution.py:262
  37.8 13.6 %all-to-all-start.2 = ((f32[4,128,256]{2,1,0:T(8,128)}), f32[4,128,256]{2,1,0:T(8,128)S(1)}, u32[]{:S(2)}, u32[]{:S(2)}) async-start(f32[4,128,256]{2,1,0:T(8,128)} %shard_map.41), calls=%async_computation.2 | async-start | bytes 1048576 | tf_op jit(solution)/shard_map/all_to_all | solution.py:266
  44.4 10.6 %copy-start = (f32[1,512,512]{2,1,0:T(8,128)S(1)}, f32[1,512,512]{2,1,0:T(8,128)}, u32[]{:S(2)}) copy-start(f32[1,512,512]{2,1,0:T(8,128)} %own_ref.1) | copy-start | bytes 3145732
  51.4 14.4 %all-to-all-start.1 = ((f32[4,128,512]{2,1,0:T(8,128)}), f32[4,128,512]{2,1,0:T(8,128)S(1)}, u32[]{:S(2)}, u32[]{:S(2)}) async-start(f32[4,128,512]{2,1,0:T(8,128)} %shard_map.39), calls=%async_computation.1 | async-start | bytes 2097152 | tf_op jit(solution)/shard_map/all_to_all | solution.py:256
  55.3 1.0 copy-start.2
  83.8 11.2 %collective-permute-start.7 = (f32[24,256]{1,0:T(8,128)S(1)}, f32[24,256]{1,0:T(8,128)S(1)}, u32[]{:S(2)}, u32[]{:S(2)}) collective-permute-start(f32[24,256]{1,0:T(8,128)S(1)} %get-tuple-element.10.refs_0_), channel_id=1, source_target_pairs={{0,260},{1,261},{2,262},{3,263},{4,256},{5,257},{6,258},{7,259},{2... | collective-permute-start | bytes 73736 | tf_op jit(solution)/shard_map/ppermute | solution.py:276
  95.8 21.2 %all-to-all-start.5 = ((f32[8,24,256]{2,1,0:T(8,128)}), f32[8,24,256]{2,1,0:T(8,128)S(1)}, u32[]{:S(2)}, u32[]{:S(2)}) async-start(f32[8,24,256]{2,1,0:T(8,128)} %shard_map.44), calls=%async_computation.5 | async-start | bytes 393216 | tf_op jit(solution)/shard_map/all_to_all | solution.py:277
  101.2 15.0 %collective-permute-start.6 = (f32[64,256]{1,0:T(8,128)S(1)}, f32[64,256]{1,0:T(8,128)S(1)}, u32[]{:S(2)}, u32[]{:S(2)}) collective-permute-start(f32[64,256]{1,0:T(8,128)S(1)} %get-tuple-element.9.refs_0_), channel_id=1, source_target_pairs={{0,256},{256,0},{1,257},{257,1},{2,258},{258,2},{3,259},{259,3},{4... | collective-permute-start | bytes 196616 | tf_op jit(solution)/shard_map/ppermute | solution.py:278
  117.0 15.2 %all-to-all-start.4 = ((f32[8,64,256]{2,1,0:T(8,128)}), f32[8,64,256]{2,1,0:T(8,128)S(1)}, u32[]{:S(2)}, u32[]{:S(2)}) async-start(f32[8,64,256]{2,1,0:T(8,128)} %shard_map.43), calls=%async_computation.4 | async-start | bytes 1048576 | tf_op jit(solution)/shard_map/all_to_all | solution.py:279

commit v3 on v1

--- a/solution.py
+++ b/solution.py
@@ -20,19 +20,24 @@
     return jax.ShapeDtypeStruct(shape, jnp.float32)
 
 
+def bf16(*shape):
+    return jax.ShapeDtypeStruct(shape, jnp.bfloat16)
+
+
 def dot(a, b, da, db):
     return lax.dot_general(
         a, b, (((da,), (db,)), ((), ())), precision=HIGHEST, preferred_element_type=jnp.float32
     )
 
 
-def call(body, outs, *args, flops=0):
+def call(body, outs, *args, flops=0, scalars=0):
     size = sum(a.size for a in args) * 4
+    smem = pl.BlockSpec(memory_space=pltpu.SMEM)
     return pl.pallas_call(
         body,
         compiler_params=PARAMS,
         out_shape=outs,
-        in_specs=[VMEM] * len(args),
+        in_specs=[smem] * scalars + [VMEM] * (len(args) - scalars),
         out_specs=jax.tree.map(lambda _: VMEM, outs),
         cost_estimate=pl.CostEstimate(flops=flops, bytes_accessed=size, transcendentals=0),
     )(*args)
@@ -71,11 +76,20 @@
     return tiles
 
 
-def factor_body(p_ref, diag_ref, m_ref, u_ref):
-    a = p_ref[...]
-    r = lax.broadcasted_iota(jnp.int32, (PANEL, PANEL), 0)
-    c = lax.broadcasted_iota(jnp.int32, (PANEL, PANEL), 1)
-    m_ref[...] = 0.5 * (a + a.T) + jnp.where(r == c, diag_ref[...], 0.0)
+def factor_body(core_ref, mine_ref, other_ref, diag_ref, m_ref, u_ref):
+    half = PANEL // 2
+    r = lax.broadcasted_iota(jnp.int32, (half, PANEL), 0)
+    c = lax.broadcasted_iota(jnp.int32, (half, PANEL), 1)
+    diag = diag_ref[...]
+    mine, other, first = mine_ref[...], other_ref[...], core_ref[0] == 0
+    p = jnp.concatenate(
+        [jnp.where(first, mine, other), jnp.where(first, other, mine)], axis=0
+    )
+    m_ref[:half] = p[:half] + jnp.where(r == c, diag, 0.0)
+    last = p[half:]
+    last = jnp.concatenate([last[:, :half], last[:, half:]], axis=0)
+    last = jnp.concatenate([jnp.zeros_like(last), last], axis=1)
+    m_ref[half:] = last + jnp.where(r + half == c, diag, 0.0)
     lane = lax.broadcasted_iota(jnp.int32, (BLOCK, LANES), 1)
     sub = lax.broadcasted_iota(jnp.int32, (BLOCK, LANES), 0)
     wlane = lax.broadcasted_iota(jnp.int32, (BLOCK, PANEL), 1)
@@ -104,6 +118,14 @@
             m_ref[lo:, :] = jnp.where(wl // BLOCK == k, 0.0, below) - upd[lo:, :]
 
 
+def sum_body(*refs):
+    *ins, out = refs
+    total = ins[0][...]
+    for ref in ins[1:]:
+        total = total + ref[...]
+    out[...] = total
+
+
 def copies_body(*refs):
     *ins, out = refs
     total = ins[0][...]
@@ -115,6 +137,15 @@
 
 def copies(n, *parts):
     return call(copies_body, f32(n, *parts[0].shape), *parts)
+
+
+def solve_body(first_ref, second_ref, panel_ref, o_ref):
+    panel = panel_ref[...]
+    half = first_ref.shape[0]
+    for at, ref in ((0, first_ref), (half, second_ref)):
+        rows = dot(ref[...], panel, 1, 0)
+        for i in range(o_ref.shape[0]):
+            o_ref[i, at : at + half] = rows
 
 
 def total_body(x_ref, *outs):
@@ -128,12 +159,6 @@
         at += out.shape[0]
 
 
-def solve_body(inv_ref, panel_ref, o_ref):
-    rows = dot(inv_ref[...], panel_ref[...], 1, 0)
-    for i in range(o_ref.shape[0]):
-        o_ref[i] = rows
-
-
 def halves(x):
     high = x.astype(jnp.bfloat16)
     return high, (x - high.astype(jnp.float32)).astype(jnp.bfloat16)
@@ -146,22 +171,71 @@
     return one(a[0], b[0]) + (one(a[0], b[1]) + one(a[1], b[0]))
 
 
-def turn_body(own_ref, panel_ref, high_ref, low_ref):
+def turn_body(masks, zl_ref, own_ref, panel_ref, high_ref, low_ref):
+    per = own_ref.shape[1] // (4 * len(masks))
+    starts = [
+        pl.multiple_of((y * len(masks) + (zl_ref[0] ^ mask)) * per, per)
+        for y in range(4)
+        for mask in masks
+    ]
+    own = jnp.concatenate([own_ref[0, pl.ds(s, per)] for s in starts], axis=0)
+    panel = jnp.concatenate([panel_ref[pl.ds(s, per)] for s in starts], axis=0)
     at = 0
-    for x in (own_ref[0], panel_ref[...]):
+    for x in (own, panel):
         rows = slice(at, at + x.shape[1])
         high_ref[rows], low_ref[rows] = halves(x.T)
         at += x.shape[1]
 
 
-def terms_body(high_ref, low_ref, solved_ref, o_ref):
-    width = high_ref.shape[0] - PANEL
+def terms_body(core_ref, high_ref, solved_ref, low_ref, keep_ref, send_ref, low, sem):
+    fetch = pltpu.make_async_copy(low_ref, low, sem)
+    fetch.start()
+    width, half = high_ref.shape[0] - PANEL, PANEL // 2
+    first = core_ref[0] == 0
+    one = lambda a, b: jnp.dot(a, b, preferred_element_type=jnp.float32)
     s = halves(solved_ref[...])
+    x = one(high_ref[...], s[0]) + one(high_ref[...], s[1])
+    fetch.wait()
+    x = x + one(low[...], s[0])
+    rows, x = x[:width], x[width:]
+    last = jnp.concatenate(
+        [x[half : half + half // 2, half:], x[half + half // 2 :, half:]], axis=1
+    )
+    x = jnp.concatenate([x[:half], last], axis=0)
+    piv = x.shape[0] // 2
+    at = keep_ref.shape[0] - piv
+    keep_ref[at:] = jnp.where(first, x[:piv], x[piv:])
+    send_ref[at:] = jnp.where(first, x[piv:], x[:piv])
+    x = rows.reshape(4, 2, at // 4, PANEL)
+    keep_ref[:at] = jnp.where(first, x[:, 0], x[:, 1]).reshape(at, PANEL)
+    send_ref[:at] = jnp.where(first, x[:, 1], x[:, 0]).reshape(at, PANEL)
+
+
+def multiply(core, high, low, solved, rows):
+    return pl.pallas_call(
+        terms_body,
+        name="terms",
+        out_shape=[f32(rows, PANEL)] * 2,
+        compiler_params=PARAMS,
+        in_specs=[
+            pl.BlockSpec(memory_space=pltpu.SMEM), VMEM, VMEM,
+            pl.BlockSpec(memory_space=pltpu.HBM),
+        ],
+        out_specs=[VMEM] * 2,
+        scratch_shapes=[pltpu.VMEM(low.shape, low.dtype), pltpu.SemaphoreType.DMA],
+        cost_estimate=pl.CostEstimate(
+            flops=6 * high.size * PANEL, bytes_accessed=4 * high.size, transcendentals=0
+        ),
+    )(core, high, solved, pltpu.with_memory_space_constraint(low, pltpu.HBM))
+
+
+def share_body(keep_ref, other_ref, o_ref):
     n = o_ref.shape[0]
-    for at, rows, out in ((0, width, 0), (width, PANEL, width // n)):
-        part = slice(at, at + rows)
-        x = dot_halves((high_ref[part], low_ref[part]), s, 1, 0)
-        o_ref[:, out : out + rows // n] = x.reshape(n, rows // n, PANEL)
+    total = keep_ref[...] + other_ref[...]
+    rows = (total.shape[0] - PANEL * 3 // 8) // n
+    for i in range(n):
+        o_ref[i, :rows] = total[rows * i : rows * i + rows]
+        o_ref[i, rows:] = total[rows * n :]
 
 
 def finish_body(top_ref, s_ref, m_ref, u_ref, o_ref, left):
@@ -225,50 +299,55 @@
     parts = []
     for k in range(1, n_y):
         parts.append(lax.ppermute(cut(k), ("y", "zl"), [(0, k * n_zl)]))
-    inv = swap(copies(n_zl, inverse_slabs[0]), "zl").reshape(-1, depth)
-    mine = jnp.where((y == 0) & (zl == 0), cut(0), 0.0)
-    for part in parts:
-        mine = mine + part
-    step = n_zl // 2
+    first = jnp.where((y == 0) & (zl == 0), cut(0), 0.0)
+    inv, masks = inverse_slabs[0], [0]
+    mine, step = None, n_zl // 2
     while step:
-        pairs = [(j, j + step) for j in range(0, n_zl, 2 * step)]
+        far = lax.ppermute(inv, "zl", [(z, z ^ step) for z in range(n_zl)])
+        if mine is None:
+            mine = call(sum_body, f32(per, PANEL), first, *parts)
+        pairs = [(z, z + step) for z in range(0, n_zl, 2 * step)]
         got = lax.ppermute(mine, "zl", pairs)
+        masks = masks + [m ^ step for m in masks]
         if step > 1:
             mine = mine + got
+            inv = jnp.concatenate([inv, far], axis=0)
         step //= 2
     panel = swap(copies(n_y, mine, got), "y").reshape(depth, PANEL)
 
     solved = call(
-        solve_body, f32(n_y, depth // n_y, PANEL), inv, panel,
-        flops=2 * depth // n_y * depth * PANEL,
+        solve_body, f32(n_y, per, PANEL), inv, far, panel,
+        flops=2 * per * depth * PANEL,
     )
     solved = swap(solved, "y").reshape(depth, PANEL)
-
+    one = lambda i: i.astype(jnp.int32).reshape(1)
+    core = one(lax.axis_index("core"))
     high, low = call(
-        turn_body, [jax.ShapeDtypeStruct((width + PANEL, depth), jnp.bfloat16)] * 2,
-        coupling, panel, flops=10**9,
-    )
-    n_row, n_piv = width // n_xc, PANEL // n_xc
-    terms = call(
-        terms_body, f32(n_xc, n_row + n_piv, PANEL), high, low, solved,
-        flops=6 * (width + PANEL) * depth * PANEL,
-    )
-    terms = swap(terms, ("x", "core"))
+        functools.partial(turn_body, masks), [bf16(width + PANEL, depth)] * 2,
+        one(zl), coupling, panel, flops=10**9, scalars=1,
+    )
+
+    n_row, n_piv = width // n_xc, 3 * PANEL // 8
+    keep, send = multiply(core, high, low, solved, n_x * n_row + n_piv)
+    other_core = [(0, 1), (1, 0)]
+    other = lax.ppermute(send, "core", other_core)
+    terms = call(share_body, f32(n_x, n_row + n_piv, PANEL), keep, other)
+    terms = swap(terms, "x")
     rows, pivot = call(total_body, [f32(n_row, PANEL), f32(n_piv, PANEL)], terms)
 
     half = n_zl // 2
     flip = [(z, (z + (half if z // half % 2 else -half)) % n_z) for z in range(n_z)]
-    other = lax.ppermute(pivot, ("zh", "zl"), flip)
-    pivot = swap(copies(n_xc, pivot, other), ("x", "core")).reshape(PANEL, PANEL)
+    pivot = pivot + lax.ppermute(pivot, ("zh", "zl"), flip)
+    other_pivot = lax.ppermute(pivot, "core", other_core)
     other = lax.ppermute(rows, "zh", [(0, 1), (1, 0)])
     rows = swap(copies(n_xc, rows, other), ("x", "core")).reshape(width, PANEL)
 
     m, u = call(
         factor_body, [f32(PANEL, PANEL), f32(PANEL, LANES)],
-        pivot, barrier_diagonal[:PANEL].reshape(1, PANEL),
-        flops=6 * 10**9,
-    )
-    top = ((y == 0) & (zl == 0)).astype(jnp.int32).reshape(1)
+        core, pivot, other_pivot, barrier_diagonal[:PANEL].reshape(1, PANEL),
+        flops=6 * 10**9, scalars=1,
+    )
+    top = one((y == 0) & (zl == 0))
     return finish(top, rows, m, u)
 
 

time: 149 us -> 143 us (0.960)
  blocking collectives: 41.6 us -> 13.7 us
  starting transfers between devices: 52.8 us -> 64.6 us
  waiting for transfers between devices: 30.7 us -> 40.5 us
    all_to_all x2 -> x1, blocking collectives: 41.6 us -> 13.7 us  [shards(): terms = swap(terms, 'x')]
    ppermute x1 -> x6, starting transfers between devices: 9.96 us -> 32.7 us  [the longest x3 15.2 us: shards(): far = lax.ppermute(inv, 'zl', [(z, z ^ step) for z in range(n_zl)])]
    ppermute x1 -> x6, waiting for transfers between devices: 2.15 us -> 15.6 us  [the longest x3 7.17 us: shards(): far = lax.ppermute(inv, 'zl', [(z, z ^ step) for z in range(n_zl)])]
    all_to_all x1, waiting for transfers between devices: 8.06 us -> 0.01 us  [shards(): panel = swap(copies(n_y, mine, got), 'y').reshape(depth, PANEL)]
    ppermute x1, starting transfers between devices: 12.9 us -> 5.96 us  [shards(): other = lax.ppermute(rows, 'zh', [(0, 1), (1, 0)])]
    all_to_all x1 -> x0, starting transfers between devices: 5.42 us -> none  [shards(): swap(copies(n_xc, pivot, other), ('x', 'core')).reshape(PANEL, PANEL)]
    ppermute x1, waiting for transfers between devices: 3.71 us -> 8.54 us  [shards(): other = lax.ppermute(rows, 'zh', [(0, 1), (1, 0)])]
    ppermute x3, waiting for transfers between devices: 7.72 us -> 5.39 us  [shards(): got = lax.ppermute(mine, 'zl', pairs)]
  transfers between devices with their start and end apart: 12 -> 16, of which waited for: 9 -> 11; matrix products, arithmetic and copies ran while one was open for 0% -> 1% of each run, Pallas kernels for 8% -> 9%
where the time goes in v3:
time: 143 us; the launch traced here: 141 us
  starting transfers between devices  64.6 us (45%)
  waiting for transfers between devices  40.5 us (28%)
  Pallas kernels  19 us (13%)
  blocking collectives  13.7 us (10%)
  local copies, waits for them, and re-layouts  1.58 us (1%)
    ppermute x3, starting transfers between devices, shards(): far = lax.ppermute(inv, 'zl', [(z, z ^ step) for z in range(n_zl)])  15.2 us
    pallas_call x8, Pallas kernels, call(): pl.pallas_call(body, compiler_params=PARAMS, out_shape=outs, in_specs=[sm...  14.2 us
    all_to_all x1, blocking collectives, shards(): terms = swap(terms, 'x')  13.7 us
    ppermute x1, starting transfers between devices, shards(): pivot = pivot + lax.ppermute(pivot, ('zh', 'zl'), flip)  13.6 us
    ppermute x1, waiting for transfers between devices, shards(): other = lax.ppermute(rows, 'zh', [(0, 1), (1, 0)])  8.54 us
    ppermute x3, starting transfers between devices, shards(): parts.append(lax.ppermute(cut(k), ('y', 'zl'), [(0, k * n_zl)]))  7.52 us
    ppermute x3, waiting for transfers between devices, shards(): far = lax.ppermute(inv, 'zl', [(z, z ^ step) for z in range(n_zl)])  7.17 us
    ppermute x1, waiting for transfers between devices, shards(): pivot = pivot + lax.ppermute(pivot, ('zh', 'zl'), flip)  6.79 us
  transfers between devices with their start and end apart: 16, of which 11 were waited for; matrix products, arithmetic and copies ran while one was open for 1% of the time, Pallas kernels for 9%

profile of v3, /device:TPU:6, one launch (start us, length us, event | category | flops | bytes accessed | tf_op | source)
XLA Modules:
  0.0 140.8 jit_solution(5444549598034645003)
XLA Ops:
  0.0 1.1 fusion
  1.1 4.9 %collective-permute-start.2 = (f32[128,256]{1,0:T(8,128)S(1)}, f32[128,256]{1,0:T(8,128)S(1)}, u32[]{:S(2)}, u32[]{:S(2)}) collective-permute-start(f32[128,256]{1,0:T(8,128)S(1)} %get-tuple-element.21), channel_id=1, source_target_pairs={{0,24},{32,56},{64,88},{96,120},{128,152},{160,184},{192,216},{224... | collective-permute-start | bytes 393224 | tf_op jit(solution)/shard_map/ppermute | solution.py:301
  6.1 1.3 collective-permute-start.1
  7.4 1.3 collective-permute-start
  8.7 0.1 collective-permute-done.2.refs_3_
  8.8 2.4 %collective-permute-done.1.refs_2_ = f32[128,256]{1,0:T(8,128)S(1)} collective-permute-done((f32[128,256]{1,0:T(8,128)S(1)}, f32[128,256]{1,0:T(8,128)S(1)}, u32[]{:S(2)}, u32[]{:S(2)}) %collective-permute-start.1) | collective-permute-done | bytes 131104 | tf_op jit(solution)/shard_map/ppermute | solution.py:301
  11.2 1.7 %collective-permute-done.refs_1_ = f32[128,256]{1,0:T(8,128)S(1)} collective-permute-done((f32[128,256]{1,0:T(8,128)S(1)}, f32[128,256]{1,0:T(8,128)S(1)}, u32[]{:S(2)}, u32[]{:S(2)}) %collective-permute-start) | collective-permute-done | bytes 131104 | tf_op jit(solution)/shard_map/ppermute | solution.py:301
  13.0 1.3 collective-permute-start.3
  14.3 2.5 %collective-permute-done.3 = f32[128,256]{1,0:T(8,128)S(1)} collective-permute-done((f32[128,256]{1,0:T(8,128)S(1)}, f32[128,256]{1,0:T(8,128)S(1)}, u32[]{:S(2)}, u32[]{:S(2)}) %collective-permute-start.3) | collective-permute-done | bytes 131104 | tf_op jit(solution)/shard_map/ppermute | solution.py:310
  16.8 0.0 copy-start.2
  16.8 1.3 collective-permute-start.4
  18.1 2.9 %collective-permute-done.4 = f32[128,256]{1,0:T(8,128)S(1)} collective-permute-done((f32[128,256]{1,0:T(8,128)S(1)}, f32[128,256]{1,0:T(8,128)S(1)}, u32[]{:S(2)}, u32[]{:S(2)}) %collective-permute-start.4) | collective-permute-done | bytes 131104 | tf_op jit(solution)/shard_map/ppermute | solution.py:310
  21.0 1.3 collective-permute-start.5
  22.3 0.0 copy-done.2
  22.3 8.0 %collective-permute-start.6 = (f32[16,512]{1,0:T(8,128)S(1)}, f32[16,512]{1,0:T(8,128)S(1)}, u32[]{:S(2)}, u32[]{:S(2)}) collective-permute-start(f32[16,512]{1,0:T(8,128)S(1)} %bitcast.15), channel_id=1, source_target_pairs={{0,4},{1,5},{2,6},{3,7},{4,0},{5,1},{6,2},{7,3},{8,12},{9,13},{10,... | collective-permute-start | bytes 98312 | tf_op jit(solution)/shard_map/ppermute | solution.py:306
  30.3 0.0 collective-permute-done.5.refs_1_
  30.3 0.8 shard_map.38
  31.2 4.2 %all-to-all-start = ((f32[4,128,256]{2,1,0:T(8,128)}), f32[4,128,256]{2,1,0:T(8,128)S(1)}, u32[]{:S(2)}, u32[]{:S(2)}) async-start(f32[4,128,256]{2,1,0:T(8,128)} %shard_map.38), calls=%async_computation | async-start | bytes 1048576 | tf_op jit(solution)/shard_map/all_to_all | solution.py:316
  35.4 0.0 collective-permute-done.6
  35.4 5.3 %collective-permute-start.7 = (f32[32,512]{1,0:T(8,128)S(1)}, f32[32,512]{1,0:T(8,128)S(1)}, u32[]{:S(2)}, u32[]{:S(2)}) collective-permute-start(f32[32,512]{1,0:T(8,128)S(1)} %pad_maximum_fusion.1), channel_id=1, source_target_pairs={{0,2},{1,3},{2,0},{3,1},{4,6},{5,7},{6,4},{7,5},{8,10},{9,11},{10,... | collective-permute-start | bytes 196616 | tf_op jit(solution)/shard_map/ppermute | solution.py:306
  40.7 2.2 %collective-permute-done.7 = f32[32,512]{1,0:T(8,128)S(1)} collective-permute-done((f32[32,512]{1,0:T(8,128)S(1)}, f32[32,512]{1,0:T(8,128)S(1)}, u32[]{:S(2)}, u32[]{:S(2)}) %collective-permute-start.7) | collective-permute-done | bytes 65568 | tf_op jit(solution)/shard_map/ppermute | solution.py:306
  43.0 1.9 %collective-permute-start.8 = (f32[64,512]{1,0:T(8,128)S(1)}, f32[64,512]{1,0:T(8,128)S(1)}, u32[]{:S(2)}, u32[]{:S(2)}) collective-permute-start(f32[64,512]{1,0:T(8,128)S(1)} %pad_maximum_fusion.first_ref), channel_id=1, source_target_pairs={{0,1},{1,0},{2,3},{3,2},{4,5},{5,4},{6,7},{7,6},{8,9},{9,8},{10,11... | collective-permute-start | bytes 393224 | tf_op jit(solution)/shard_map/ppermute | solution.py:306
  44.9 4.9 %collective-permute-done.8.second_ref = f32[64,512]{1,0:T(8,128)S(1)} collective-permute-done((f32[64,512]{1,0:T(8,128)S(1)}, f32[64,512]{1,0:T(8,128)S(1)}, u32[]{:S(2)}, u32[]{:S(2)}) %collective-permute-start.8) | collective-permute-done | bytes 131104 | tf_op jit(solution)/shard_map/ppermute | solution.py:306
  49.8 0.0 all-to-all-done
  49.8 0.0 copy-start
  49.8 1.5 %shard_map.40 = f32[4,128,256]{2,1,0:T(8,128)} custom-call(f32[64,512]{1,0:T(8,128)S(1)} %pad_maximum_fusion.first_ref, f32[64,512]{1,0:T(8,128)S(1)} %collective-permute-done.8.second_ref, f32[512,256]{1,0:T(8,128)S(1)} %bitcast.9), custom_call_target="tpu_custom_call" | custom-call | flops 33554432 | bytes 786432 | tf_op jit(solution)/shard_map/pallas_call | solution.py:36
  51.3 4.8 %all-to-all-start.1 = ((f32[4,128,256]{2,1,0:T(8,128)}), f32[4,128,256]{2,1,0:T(8,128)S(1)}, u32[]{:S(2)}, u32[]{:S(2)}) async-start(f32[4,128,256]{2,1,0:T(8,128)} %shard_map.40), calls=%async_computation.1 | async-start | bytes 1048576 | tf_op jit(solution)/shard_map/all_to_all | solution.py:322
  56.1 0.0 copy-done
  56.1 0.5 shard_map.39
  56.6 0.0 copy-start.1
  56.6 0.9 copy-done.1
  57.5 6.7 %all-to-all-done.1 = f32[4,128,256]{2,1,0:T(8,128)S(1)} async-done(((f32[4,128,256]{2,1,0:T(8,128)}), f32[4,128,256]{2,1,0:T(8,128)S(1)}, u32[]{:S(2)}, u32[]{:S(2)}) %all-to-all-start.1) | async-done | bytes 524320 | tf_op jit(solution)/shard_map/all_to_all | solution.py:322
  64.2 2.2 %terms.1 = (f32[352,256]{1,0:T(8,128)S(1)}, f32[352,256]{1,0:T(8,128)S(1)}) custom-call(s32[1]{0:T(128)} %bitcast.1.core_ref, bf16[768,512]{1,0:T(8,128)(2,1)S(1)} %get-tuple-element.13.high_ref, f32[512,256]{1,0:T(8,128)S(1)} %bitcast.12, bf16[768,512]{1,0:T(8,128)(2,1)} %copy-done.1), custom_call_target="tpu_custom_call" | custom-call | flops 603979776 | bytes 1572864 | tf_op jit(solution)/shard_map/terms/pallas_call | solution.py:215
  66.4 1.9 %collective-permute-start.9 = (f32[352,256]{1,0:T(8,128)S(1)}, f32[352,256]{1,0:T(8,128)S(1)}, u32[]{:S(2)}, u32[]{:S(2)}) collective-permute-start(f32[352,256]{1,0:T(8,128)S(1)} %get-tuple-element.16), channel_id=1, source_target_pairs={{0,32},{32,0},{1,33},{33,1},{2,34},{34,2},{3,35},{35,3},{4,36},{36... | collective-permute-start | bytes 1081352 | tf_op jit(solution)/shard_map/ppermute | solution.py:333
  68.3 1.6 %collective-permute-done.9.other_ref = f32[352,256]{1,0:T(8,128)S(1)} collective-permute-done((f32[352,256]{1,0:T(8,128)S(1)}, f32[352,256]{1,0:T(8,128)S(1)}, u32[]{:S(2)}, u32[]{:S(2)}) %collective-permute-start.9) | collective-permute-done | bytes 360480 | tf_op jit(solution)/shard_map/ppermute | solution.py:333
  70.0 0.1 shard_map.41
  70.0 13.7 %all_to_all.20.x_ref = f32[4,160,256]{2,1,0:T(8,128)S(1)} all-to-all(f32[4,160,256]{2,1,0:T(8,128)S(1)} %shard_map.41), channel_id=1, replica_groups=mesh['zh'=2,'x'=4,'core'=2,'y'=4,'zl'=8] {'x'}, dimensions={0} | all-to-all | bytes 1310720 | tf_op jit(solution)/shard_map/all_to_all | solution.py:335
  83.8 13.6 %collective-permute-start.11 = (f32[96,256]{1,0:T(8,128)S(1)}, f32[96,256]{1,0:T(8,128)S(1)}, u32[]{:S(2)}, u32[]{:S(2)}) collective-permute-start(f32[96,256]{1,0:T(8,128)S(1)} %get-tuple-element.18), channel_id=1, source_target_pairs={{0,260},{1,261},{2,262},{3,263},{4,256},{5,257},{6,258},{7,259},{2... | collective-permute-start | bytes 294920 | tf_op jit(solution)/shard_map/ppermute | solution.py:340
  97.4 6.8 %collective-permute-done.11 = f32[96,256]{1,0:T(8,128)S(1)} collective-permute-done((f32[96,256]{1,0:T(8,128)S(1)}, f32[96,256]{1,0:T(8,128)S(1)}, u32[]{:S(2)}, u32[]{:S(2)}) %collective-permute-start.11) | collective-permute-done | bytes 98336 | tf_op jit(solution)/shard_map/ppermute | solution.py:340
  104.2 1.9 %collective-permute-start.12 = (f32[96,256]{1,0:T(8,128)S(1)}, f32[96,256]{1,0:T(8,128)S(1)}, u32[]{:S(2)}, u32[]{:S(2)}) collective-permute-start(f32[96,256]{1,0:T(8,128)S(1)} %add.11.mine_ref), channel_id=1, source_target_pairs={{0,32},{32,0},{1,33},{33,1},{2,34},{34,2},{3,35},{35,3},{4,36},{36... | collective-permute-start | bytes 294920 | tf_op jit(solution)/shard_map/ppermute | solution.py:341
  106.1 6.0 %collective-permute-start.10 = (f32[64,256]{1,0:T(8,128)S(1)}, f32[64,256]{1,0:T(8,128)S(1)}, u32[]{:S(2)}, u32[]{:S(2)}) collective-permute-start(f32[64,256]{1,0:T(8,128)S(1)} %get-tuple-element.17.refs_0_), channel_id=1, source_target_pairs={{0,256},{256,0},{1,257},{257,1},{2,258},{258,2},{3,259},{259,3},{4... | collective-permute-start | bytes 196616 | tf_op jit(solution)/shard_map/ppermute | solution.py:342
  112.1 0.7 slice.19
  112.8 8.5 %collective-permute-done.10.refs_1_ = f32[64,256]{1,0:T(8,128)S(1)} collective-permute-done((f32[64,256]{1,0:T(8,128)S(1)}, f32[64,256]{1,0:T(8,128)S(1)}, u32[]{:S(2)}, u32[]{:S(2)}) %collective-permute-start.10) | collective-permute-done | bytes 65568 | tf_op jit(solution)/shard_map/ppermute | solution.py:342
  121.3 0.8 shard_map.43
  122.2 5.5 %all-to-all-start.3 = ((f32[8,64,256]{2,1,0:T(8,128)}), f32[8,64,256]{2,1,0:T(8,128)S(1)}, u32[]{:S(2)}, u32[]{:S(2)}) async-start(f32[8,64,256]{2,1,0:T(8,128)} %shard_map.43), calls=%async_computation.3 | async-start | bytes 1048576 | tf_op jit(solution)/shard_map/all_to_all | solution.py:343
  127.7 0.0 collective-permute-done.12.other_ref
  127.7 10.4 %shard_map.44 = (f32[256,256]{1,0:T(8,128)S(1)}, f32[256,128]{1,0:T(8,128)S(1)}) custom-call(s32[1]{0:T(128)} %bitcast.1.core_ref, f32[96,256]{1,0:T(8,128)S(1)} %add.11.mine_ref, f32[96,256]{1,0:T(8,128)S(1)} %collective-permute-done.12.other_ref, f32[1,256]{1,0:T(1,128)S(1)} %bitcast.14), custom_call_target="tpu_custom_call" | custom-call | flops 6000000000 | bytes 197636 | tf_op jit(solution)/shard_map/pallas_call | solution.py:36
  138.1 0.0 all-to-all-done.3
  138.1 2.7 %finish.1 = f32[512,256]{1,0:T(8,128)} custom-call(s32[1]{0:T(128)} %bitcast.top_ref, f32[512,256]{1,0:T(8,128)S(1)} %bitcast.11, f32[256,256]{1,0:T(8,128)S(1)} %get-tuple-element.19.m_ref, f32[256,128]{1,0:T(8,128)S(1)} %get-tuple-element.20.u_ref), custom_call_target="tpu_custom_call" | custom-call | flops 67108864 | bytes 1048576 | tf_op jit(solution)/shard_map/finish/pallas_call | solution.py:269
  (7 shorter events, 0.1 us)
Async XLA Ops:
  1.1 7.7 %collective-permute-start.2 = (f32[128,256]{1,0:T(8,128)S(1)}, f32[128,256]{1,0:T(8,128)S(1)}, u32[]{:S(2)}, u32[]{:S(2)}) collective-permute-start(f32[128,256]{1,0:T(8,128)S(1)} %get-tuple-element.21), channel_id=1, source_target_pairs={{0,24},{32,56},{64,88},{96,120},{128,152},{160,184},{192,216},{224... | collective-permute-start | bytes 393224 | tf_op jit(solution)/shard_map/ppermute | solution.py:301
  6.1 5.2 %collective-permute-start.1 = (f32[128,256]{1,0:T(8,128)S(1)}, f32[128,256]{1,0:T(8,128)S(1)}, u32[]{:S(2)}, u32[]{:S(2)}) collective-permute-start(f32[128,256]{1,0:T(8,128)S(1)} %get-tuple-element.22), channel_id=1, source_target_pairs={{0,16},{32,48},{64,80},{96,112},{128,144},{160,176},{192,208},{224... | collective-permute-start | bytes 393224 | tf_op jit(solution)/shard_map/ppermute | solution.py:301
  7.4 5.5 %collective-permute-start = (f32[128,256]{1,0:T(8,128)S(1)}, f32[128,256]{1,0:T(8,128)S(1)}, u32[]{:S(2)}, u32[]{:S(2)}) collective-permute-start(f32[128,256]{1,0:T(8,128)S(1)} %get-tuple-element.23), channel_id=1, source_target_pairs={{0,8},{32,40},{64,72},{96,104},{128,136},{160,168},{192,200},{224,... | collective-permute-start | bytes 393224 | tf_op jit(solution)/shard_map/ppermute | solution.py:301
  13.0 3.8 %collective-permute-start.3 = (f32[128,256]{1,0:T(8,128)S(1)}, f32[128,256]{1,0:T(8,128)S(1)}, u32[]{:S(2)}, u32[]{:S(2)}) collective-permute-start(f32[128,256]{1,0:T(8,128)S(1)} %shard_map.37), channel_id=1, source_target_pairs={{0,4},{8,12},{16,20},{24,28},{32,36},{40,44},{48,52},{56,60},{64,6... | collective-permute-start | bytes 393224 | tf_op jit(solution)/shard_map/ppermute | solution.py:310
  16.8 5.5 %copy-start.2 = (f32[1,16,512]{2,1,0:T(8,128)S(1)}, f32[1,16,512]{2,1,0:T(8,128)}, u32[]{:S(2)}) copy-start(f32[1,16,512]{2,1,0:T(8,128)} %param.4) | copy-start | bytes 98308
  16.8 4.2 %collective-permute-start.4 = (f32[128,256]{1,0:T(8,128)S(1)}, f32[128,256]{1,0:T(8,128)S(1)}, u32[]{:S(2)}, u32[]{:S(2)}) collective-permute-start(f32[128,256]{1,0:T(8,128)S(1)} %add.9), channel_id=1, source_target_pairs={{0,2},{4,6},{8,10},{12,14},{16,18},{20,22},{24,26},{28,30},{32,34}... | collective-permute-start | bytes 393224 | tf_op jit(solution)/shard_map/ppermute | solution.py:310
  21.0 9.3 %collective-permute-start.5 = (f32[128,256]{1,0:T(8,128)S(1)}, f32[128,256]{1,0:T(8,128)S(1)}, u32[]{:S(2)}, u32[]{:S(2)}) collective-permute-start(f32[128,256]{1,0:T(8,128)S(1)} %add.10.refs_0_), channel_id=1, source_target_pairs={{0,1},{2,3},{4,5},{6,7},{8,9},{10,11},{12,13},{14,15},{16,17},{18,... | collective-permute-start | bytes 393224 | tf_op jit(solution)/shard_map/ppermute | solution.py:310
  22.3 13.1 %collective-permute-start.6 = (f32[16,512]{1,0:T(8,128)S(1)}, f32[16,512]{1,0:T(8,128)S(1)}, u32[]{:S(2)}, u32[]{:S(2)}) collective-permute-start(f32[16,512]{1,0:T(8,128)S(1)} %bitcast.15), channel_id=1, source_target_pairs={{0,4},{1,5},{2,6},{3,7},{4,0},{5,1},{6,2},{7,3},{8,12},{9,13},{10,... | collective-permute-start | bytes 98312 | tf_op jit(solution)/shard_map/ppermute | solution.py:306
  31.2 18.7 %all-to-all-start = ((f32[4,128,256]{2,1,0:T(8,128)}), f32[4,128,256]{2,1,0:T(8,128)S(1)}, u32[]{:S(2)}, u32[]{:S(2)}) async-start(f32[4,128,256]{2,1,0:T(8,128)} %shard_map.38), calls=%async_computation | async-start | bytes 1048576 | tf_op jit(solution)/shard_map/all_to_all | solution.py:316
  35.4 7.5 %collective-permute-start.7 = (f32[32,512]{1,0:T(8,128)S(1)}, f32[32,512]{1,0:T(8,128)S(1)}, u32[]{:S(2)}, u32[]{:S(2)}) collective-permute-start(f32[32,512]{1,0:T(8,128)S(1)} %pad_maximum_fusion.1), channel_id=1, source_target_pairs={{0,2},{1,3},{2,0},{3,1},{4,6},{5,7},{6,4},{7,5},{8,10},{9,11},{10,... | collective-permute-start | bytes 196616 | tf_op jit(solution)/shard_map/ppermute | solution.py:306
  43.0 6.9 %collective-permute-start.8 = (f32[64,512]{1,0:T(8,128)S(1)}, f32[64,512]{1,0:T(8,128)S(1)}, u32[]{:S(2)}, u32[]{:S(2)}) collective-permute-start(f32[64,512]{1,0:T(8,128)S(1)} %pad_maximum_fusion.first_ref), channel_id=1, source_target_pairs={{0,1},{1,0},{2,3},{3,2},{4,5},{5,4},{6,7},{7,6},{8,9},{9,8},{10,11... | collective-permute-start | bytes 393224 | tf_op jit(solution)/shard_map/ppermute | solution.py:306
  49.8 6.3 %copy-start = (f32[1,512,512]{2,1,0:T(8,128)S(1)}, f32[1,512,512]{2,1,0:T(8,128)}, u32[]{:S(2)}) copy-start(f32[1,512,512]{2,1,0:T(8,128)} %own_ref.1) | copy-start | bytes 3145732
  51.3 12.9 %all-to-all-start.1 = ((f32[4,128,256]{2,1,0:T(8,128)}), f32[4,128,256]{2,1,0:T(8,128)S(1)}, u32[]{:S(2)}, u32[]{:S(2)}) async-start(f32[4,128,256]{2,1,0:T(8,128)} %shard_map.40), calls=%async_computation.1 | async-start | bytes 1048576 | tf_op jit(solution)/shard_map/all_to_all | solution.py:322
  56.6 0.9 copy-start.1
  66.4 3.6 %collective-permute-start.9 = (f32[352,256]{1,0:T(8,128)S(1)}, f32[352,256]{1,0:T(8,128)S(1)}, u32[]{:S(2)}, u32[]{:S(2)}) collective-permute-start(f32[352,256]{1,0:T(8,128)S(1)} %get-tuple-element.16), channel_id=1, source_target_pairs={{0,32},{32,0},{1,33},{33,1},{2,34},{34,2},{3,35},{35,3},{4,36},{36... | collective-permute-start | bytes 1081352 | tf_op jit(solution)/shard_map/ppermute | solution.py:333
  83.8 20.4 %collective-permute-start.11 = (f32[96,256]{1,0:T(8,128)S(1)}, f32[96,256]{1,0:T(8,128)S(1)}, u32[]{:S(2)}, u32[]{:S(2)}) collective-permute-start(f32[96,256]{1,0:T(8,128)S(1)} %get-tuple-element.18), channel_id=1, source_target_pairs={{0,260},{1,261},{2,262},{3,263},{4,256},{5,257},{6,258},{7,259},{2... | collective-permute-start | bytes 294920 | tf_op jit(solution)/shard_map/ppermute | solution.py:340
  104.2 23.5 %collective-permute-start.12 = (f32[96,256]{1,0:T(8,128)S(1)}, f32[96,256]{1,0:T(8,128)S(1)}, u32[]{:S(2)}, u32[]{:S(2)}) collective-permute-start(f32[96,256]{1,0:T(8,128)S(1)} %add.11.mine_ref), channel_id=1, source_target_pairs={{0,32},{32,0},{1,33},{33,1},{2,34},{34,2},{3,35},{35,3},{4,36},{36... | collective-permute-start | bytes 294920 | tf_op jit(solution)/shard_map/ppermute | solution.py:341
  106.1 15.2 %collective-permute-start.10 = (f32[64,256]{1,0:T(8,128)S(1)}, f32[64,256]{1,0:T(8,128)S(1)}, u32[]{:S(2)}, u32[]{:S(2)}) collective-permute-start(f32[64,256]{1,0:T(8,128)S(1)} %get-tuple-element.17.refs_0_), channel_id=1, source_target_pairs={{0,256},{256,0},{1,257},{257,1},{2,258},{258,2},{3,259},{259,3},{4... | collective-permute-start | bytes 196616 | tf_op jit(solution)/shard_map/ppermute | solution.py:342
  122.2 15.9 %all-to-all-start.3 = ((f32[8,64,256]{2,1,0:T(8,128)}), f32[8,64,256]{2,1,0:T(8,128)S(1)}, u32[]{:S(2)}, u32[]{:S(2)}) async-start(f32[8,64,256]{2,1,0:T(8,128)} %shard_map.43), calls=%async_computation.3 | async-start | bytes 1048576 | tf_op jit(solution)/shard_map/all_to_all | solution.py:343

commit v4 on v3

--- a/solution.py
+++ b/solution.py
@@ -10,6 +10,7 @@
 PANEL = 256
 BLOCK = 64
 LANES = 128
+PACKED = 160
 AXES = ("zh", "x", "core", "y", "zl")
 HIGHEST = lax.Precision.HIGHEST
 VMEM = pl.BlockSpec(memory_space=pltpu.VMEM)
@@ -77,19 +78,18 @@
 
 
 def factor_body(core_ref, mine_ref, other_ref, diag_ref, m_ref, u_ref):
-    half = PANEL // 2
-    r = lax.broadcasted_iota(jnp.int32, (half, PANEL), 0)
-    c = lax.broadcasted_iota(jnp.int32, (half, PANEL), 1)
-    diag = diag_ref[...]
     mine, other, first = mine_ref[...], other_ref[...], core_ref[0] == 0
     p = jnp.concatenate(
         [jnp.where(first, mine, other), jnp.where(first, other, mine)], axis=0
     )
-    m_ref[:half] = p[:half] + jnp.where(r == c, diag, 0.0)
-    last = p[half:]
-    last = jnp.concatenate([last[:, :half], last[:, half:]], axis=0)
-    last = jnp.concatenate([jnp.zeros_like(last), last], axis=1)
-    m_ref[half:] = last + jnp.where(r + half == c, diag, 0.0)
+    b = BLOCK
+    third = p[2 * b :]
+    third = jnp.concatenate([third[:, LANES:], third[:, :LANES]], axis=0)
+    blocks = (p[:b], p[b : 2 * b], jnp.concatenate([third, third], axis=1))
+    r = lax.broadcasted_iota(jnp.int32, (b, PANEL), 0)
+    c = lax.broadcasted_iota(jnp.int32, (b, PANEL), 1)
+    for i, rows in enumerate(blocks + (pltpu.roll(p[b : 2 * b], 3 * b, 1),)):
+        m_ref[b * i : b * i + b] = rows + jnp.where(r + b * i == c, diag_ref[...], 0.0)
     lane = lax.broadcasted_iota(jnp.int32, (BLOCK, LANES), 1)
     sub = lax.broadcasted_iota(jnp.int32, (BLOCK, LANES), 0)
     wlane = lax.broadcasted_iota(jnp.int32, (BLOCK, PANEL), 1)
@@ -139,13 +139,15 @@
     return call(copies_body, f32(n, *parts[0].shape), *parts)
 
 
-def solve_body(first_ref, second_ref, panel_ref, o_ref):
-    panel = panel_ref[...]
-    half = first_ref.shape[0]
-    for at, ref in ((0, first_ref), (half, second_ref)):
-        rows = dot(ref[...], panel, 1, 0)
-        for i in range(o_ref.shape[0]):
-            o_ref[i, at : at + half] = rows
+def solve_body(y_ref, inv_ref, *refs):
+    *parts, panel_ref, o_ref = refs
+    per = parts[0].shape[0]
+    for ahead, part in enumerate(parts):
+        y = lax.rem(y_ref[0] + ahead, len(parts))
+        panel_ref[pl.ds(pl.multiple_of(y * per, per), per)] = part[...]
+    rows = dot(inv_ref[...], panel_ref[...], 1, 0)
+    for i in range(o_ref.shape[0]):
+        o_ref[i] = rows
 
 
 def total_body(x_ref, *outs):
@@ -171,68 +173,60 @@
     return one(a[0], b[0]) + (one(a[0], b[1]) + one(a[1], b[0]))
 
 
-def turn_body(masks, zl_ref, own_ref, panel_ref, high_ref, low_ref):
-    per = own_ref.shape[1] // (4 * len(masks))
-    starts = [
-        pl.multiple_of((y * len(masks) + (zl_ref[0] ^ mask)) * per, per)
-        for y in range(4)
-        for mask in masks
-    ]
-    own = jnp.concatenate([own_ref[0, pl.ds(s, per)] for s in starts], axis=0)
-    panel = jnp.concatenate([panel_ref[pl.ds(s, per)] for s in starts], axis=0)
-    at = 0
-    for x in (own, panel):
-        rows = slice(at, at + x.shape[1])
-        high_ref[rows], low_ref[rows] = halves(x.T)
-        at += x.shape[1]
-
-
-def terms_body(core_ref, high_ref, solved_ref, low_ref, keep_ref, send_ref, low, sem):
+def turn_body(own_ref, panel_ref, own_high, own_low, panel_high, panel_low):
+    own_high[...], own_low[...] = halves(own_ref[0].T)
+    panel_high[...], panel_low[...] = halves(panel_ref[...].T)
+
+
+def terms_body(
+    core_ref, own_high, panel_high, panel_low, solved_ref, low_ref, keep_ref, send_ref, low, sem
+):
     fetch = pltpu.make_async_copy(low_ref, low, sem)
     fetch.start()
-    width, half = high_ref.shape[0] - PANEL, PANEL // 2
+    s = halves(solved_ref[...])
     first = core_ref[0] == 0
-    one = lambda a, b: jnp.dot(a, b, preferred_element_type=jnp.float32)
-    s = halves(solved_ref[...])
-    x = one(high_ref[...], s[0]) + one(high_ref[...], s[1])
-    fetch.wait()
-    x = x + one(low[...], s[0])
-    rows, x = x[:width], x[width:]
-    last = jnp.concatenate(
-        [x[half : half + half // 2, half:], x[half + half // 2 :, half:]], axis=1
-    )
-    x = jnp.concatenate([x[:half], last], axis=0)
+    x = dot_halves((panel_high[...], panel_low[...]), s, 1, 0)
+    b, w = BLOCK, LANES
+    third = jnp.concatenate([x[2 * b + b // 2 : 3 * b, w:], x[2 * b : 2 * b + b // 2, w:]], axis=1)
+    lane = lax.broadcasted_iota(jnp.int32, (b, PANEL), 1)
+    second = jnp.where(lane < b, pltpu.roll(x[3 * b :], b, 1), x[b : 2 * b])
+    x = jnp.concatenate([x[:b], second, third], axis=0)
     piv = x.shape[0] // 2
     at = keep_ref.shape[0] - piv
     keep_ref[at:] = jnp.where(first, x[:piv], x[piv:])
     send_ref[at:] = jnp.where(first, x[piv:], x[:piv])
-    x = rows.reshape(4, 2, at // 4, PANEL)
+    one = lambda a, b: jnp.dot(a, b, preferred_element_type=jnp.float32)
+    x = one(own_high[...], s[0]) + one(own_high[...], s[1])
+    fetch.wait()
+    x = x + one(low[...], s[0])
+    x = x.reshape(4, 2, at // 4, PANEL)
     keep_ref[:at] = jnp.where(first, x[:, 0], x[:, 1]).reshape(at, PANEL)
     send_ref[:at] = jnp.where(first, x[:, 1], x[:, 0]).reshape(at, PANEL)
 
 
-def multiply(core, high, low, solved, rows):
+def multiply(core, parts, solved, rows):
+    high, low, *panels = parts
     return pl.pallas_call(
         terms_body,
         name="terms",
         out_shape=[f32(rows, PANEL)] * 2,
         compiler_params=PARAMS,
         in_specs=[
-            pl.BlockSpec(memory_space=pltpu.SMEM), VMEM, VMEM,
+            pl.BlockSpec(memory_space=pltpu.SMEM), VMEM, VMEM, VMEM, VMEM,
             pl.BlockSpec(memory_space=pltpu.HBM),
         ],
         out_specs=[VMEM] * 2,
         scratch_shapes=[pltpu.VMEM(low.shape, low.dtype), pltpu.SemaphoreType.DMA],
         cost_estimate=pl.CostEstimate(
-            flops=6 * high.size * PANEL, bytes_accessed=4 * high.size, transcendentals=0
+            flops=9 * high.size * PANEL, bytes_accessed=6 * high.size, transcendentals=0
         ),
-    )(core, high, solved, pltpu.with_memory_space_constraint(low, pltpu.HBM))
+    )(core, high, *panels, solved, pltpu.with_memory_space_constraint(low, pltpu.HBM))
 
 
 def share_body(keep_ref, other_ref, o_ref):
     n = o_ref.shape[0]
     total = keep_ref[...] + other_ref[...]
-    rows = (total.shape[0] - PANEL * 3 // 8) // n
+    rows = (total.shape[0] - PACKED // 2) // n
     for i in range(n):
         o_ref[i, :rows] = total[rows * i : rows * i + rows]
         o_ref[i, rows:] = total[rows * n :]
@@ -294,41 +288,36 @@
     y, zl = lax.axis_index("y"), lax.axis_index("zl")
     swap = functools.partial(lax.all_to_all, split_axis=0, concat_axis=0)
 
+    one = lambda i: i.astype(jnp.int32).reshape(1)
     per = depth // n_y
     cut = lambda k: own[per * k : per * k + per, :PANEL]
     parts = []
     for k in range(1, n_y):
         parts.append(lax.ppermute(cut(k), ("y", "zl"), [(0, k * n_zl)]))
     first = jnp.where((y == 0) & (zl == 0), cut(0), 0.0)
-    inv, masks = inverse_slabs[0], [0]
-    mine, step = None, n_zl // 2
+    mine = call(sum_body, f32(per, PANEL), first, *parts)
+    step = n_zl // 2
     while step:
-        far = lax.ppermute(inv, "zl", [(z, z ^ step) for z in range(n_zl)])
-        if mine is None:
-            mine = call(sum_body, f32(per, PANEL), first, *parts)
         pairs = [(z, z + step) for z in range(0, n_zl, 2 * step)]
-        got = lax.ppermute(mine, "zl", pairs)
-        masks = masks + [m ^ step for m in masks]
-        if step > 1:
-            mine = mine + got
-            inv = jnp.concatenate([inv, far], axis=0)
+        mine = mine + lax.ppermute(mine, "zl", pairs)
         step //= 2
-    panel = swap(copies(n_y, mine, got), "y").reshape(depth, PANEL)
-
-    solved = call(
-        solve_body, f32(n_y, per, PANEL), inv, far, panel,
-        flops=2 * per * depth * PANEL,
+    inv = swap(copies(n_zl, inverse_slabs[0]), "zl").reshape(per, depth)
+    parts = [mine]
+    for k in range(1, n_y):
+        parts.append(lax.ppermute(mine, "y", [(i, (i - k) % n_y) for i in range(n_y)]))
+    panel, solved = call(
+        solve_body, [f32(depth, PANEL), f32(n_y, per, PANEL)], one(y), inv, *parts,
+        flops=2 * per * depth * PANEL, scalars=1,
     )
     solved = swap(solved, "y").reshape(depth, PANEL)
-    one = lambda i: i.astype(jnp.int32).reshape(1)
     core = one(lax.axis_index("core"))
-    high, low = call(
-        functools.partial(turn_body, masks), [bf16(width + PANEL, depth)] * 2,
-        one(zl), coupling, panel, flops=10**9, scalars=1,
-    )
-
-    n_row, n_piv = width // n_xc, 3 * PANEL // 8
-    keep, send = multiply(core, high, low, solved, n_x * n_row + n_piv)
+    parts = call(
+        turn_body, [bf16(width, depth)] * 2 + [bf16(PANEL, depth)] * 2,
+        coupling, panel, flops=10**9,
+    )
+
+    n_row, n_piv = width // n_xc, PACKED // 2
+    keep, send = multiply(core, parts, solved, n_x * n_row + n_piv)
     other_core = [(0, 1), (1, 0)]
     other = lax.ppermute(send, "core", other_core)
     terms = call(share_body, f32(n_x, n_row + n_piv, PANEL), keep, other)

time: 143 us -> 140 us (0.979)
    all_to_all x1, starting transfers between devices: 4.25 us -> 12.5 us  [shards(): inv = swap(copies(n_zl, inverse_slabs[0]), 'zl').reshape(per, depth)]
    ppermute x6, starting transfers between devices: 19.1 us -> 14.9 us  [the longest x3 10.8 us: shards(): lax.ppermute(mine, 'y', [(i, (i - k) % n_y) for i in range(n_y)])]
    ppermute x1, starting transfers between devices: 13.6 us -> 9.57 us  [shards(): pivot = pivot + lax.ppermute(pivot, ('zh', 'zl'), flip)]
    ppermute x3, waiting for transfers between devices: 4.23 us -> 2.49 us  [shards(): parts.append(lax.ppermute(cut(k), ('y', 'zl'), [(0, k * n_zl)]))]
where the time goes in v4:
time: 140 us; the launch traced here: 138 us
  starting transfers between devices  63.3 us (45%)
  waiting for transfers between devices  39.6 us (28%)
  Pallas kernels  18.1 us (13%)
  blocking collectives  13 us (9%)
  local copies, waits for them, and re-layouts  2.26 us (2%)
    pallas_call x8, Pallas kernels, call(): pl.pallas_call(body, compiler_params=PARAMS, out_shape=outs, in_specs=[sm...  13.9 us
    all_to_all x1, blocking collectives, shards(): terms = swap(terms, 'x')  13 us
    all_to_all x1, starting transfers between devices, shards(): inv = swap(copies(n_zl, inverse_slabs[0]), 'zl').reshape(per, depth)  12.5 us
    ppermute x3, starting transfers between devices, shards(): lax.ppermute(mine, 'y', [(i, (i - k) % n_y) for i in range(n_y)])  10.8 us
    ppermute x1, starting transfers between devices, shards(): pivot = pivot + lax.ppermute(pivot, ('zh', 'zl'), flip)  9.57 us
    ppermute x1, waiting for transfers between devices, shards(): other = lax.ppermute(rows, 'zh', [(0, 1), (1, 0)])  8.16 us
    ppermute x3, waiting for transfers between devices, shards(): mine = mine + lax.ppermute(mine, 'zl', pairs)  8.13 us
    ppermute x1, waiting for transfers between devices, shards(): pivot = pivot + lax.ppermute(pivot, ('zh', 'zl'), flip)  7.15 us
  transfers between devices with their start and end apart: 16, of which 11 were waited for; matrix products, arithmetic and copies ran while one was open for 1% of the time, Pallas kernels for 9%

profile of v4, /device:TPU:6, one launch (start us, length us, event | category | flops | bytes accessed | tf_op | source)
XLA Modules:
  0.0 137.6 jit_solution(11679408496443316932)
XLA Ops:
  0.0 0.0 copy-start.1
  0.0 0.8 copy-done.1
  0.8 0.7 shard_map.37
  1.5 12.5 %all-to-all-start = ((f32[8,16,512]{2,1,0:T(8,128)}), f32[8,16,512]{2,1,0:T(8,128)S(1)}, u32[]{:S(2)}, u32[]{:S(2)}) async-start(f32[8,16,512]{2,1,0:T(8,128)} %shard_map.37), calls=%async_computation | async-start | bytes 524288 | tf_op jit(solution)/shard_map/all_to_all | solution.py:304
  14.0 1.1 fusion
  15.2 3.5 %collective-permute-start = (f32[128,256]{1,0:T(8,128)S(1)}, f32[128,256]{1,0:T(8,128)S(1)}, u32[]{:S(2)}, u32[]{:S(2)}) collective-permute-start(f32[128,256]{1,0:T(8,128)S(1)} %get-tuple-element.31), channel_id=1, source_target_pairs={{0,8},{32,40},{64,72},{96,104},{128,136},{160,168},{192,200},{224,... | collective-permute-start | bytes 393224 | tf_op jit(solution)/shard_map/ppermute | solution.py:296
  18.6 2.3 %collective-permute-start.1 = (f32[128,256]{1,0:T(8,128)S(1)}, f32[128,256]{1,0:T(8,128)S(1)}, u32[]{:S(2)}, u32[]{:S(2)}) collective-permute-start(f32[128,256]{1,0:T(8,128)S(1)} %get-tuple-element.30), channel_id=1, source_target_pairs={{0,16},{32,48},{64,80},{96,112},{128,144},{160,176},{192,208},{224... | collective-permute-start | bytes 393224 | tf_op jit(solution)/shard_map/ppermute | solution.py:296
  20.9 1.3 collective-permute-start.2
  22.2 0.0 collective-permute-done.refs_1_
  22.3 1.7 %collective-permute-done.1.refs_2_ = f32[128,256]{1,0:T(8,128)S(1)} collective-permute-done((f32[128,256]{1,0:T(8,128)S(1)}, f32[128,256]{1,0:T(8,128)S(1)}, u32[]{:S(2)}, u32[]{:S(2)}) %collective-permute-start.1) | collective-permute-done | bytes 131104 | tf_op jit(solution)/shard_map/ppermute | solution.py:296
  23.9 0.8 collective-permute-done.2.refs_3_
  24.8 1.3 collective-permute-start.3
  26.1 2.6 %collective-permute-done.3 = f32[128,256]{1,0:T(8,128)S(1)} collective-permute-done((f32[128,256]{1,0:T(8,128)S(1)}, f32[128,256]{1,0:T(8,128)S(1)}, u32[]{:S(2)}, u32[]{:S(2)}) %collective-permute-start.3) | collective-permute-done | bytes 131104 | tf_op jit(solution)/shard_map/ppermute | solution.py:302
  28.7 1.3 collective-permute-start.4
  30.0 3.0 %collective-permute-done.4 = f32[128,256]{1,0:T(8,128)S(1)} collective-permute-done((f32[128,256]{1,0:T(8,128)S(1)}, f32[128,256]{1,0:T(8,128)S(1)}, u32[]{:S(2)}, u32[]{:S(2)}) %collective-permute-start.4) | collective-permute-done | bytes 131104 | tf_op jit(solution)/shard_map/ppermute | solution.py:302
  33.1 0.0 copy-start
  33.1 1.4 %collective-permute-start.5 = (f32[128,256]{1,0:T(8,128)S(1)}, f32[128,256]{1,0:T(8,128)S(1)}, u32[]{:S(2)}, u32[]{:S(2)}) collective-permute-start(f32[128,256]{1,0:T(8,128)S(1)} %add.13), channel_id=1, source_target_pairs={{0,1},{2,3},{4,5},{6,7},{8,9},{10,11},{12,13},{14,15},{16,17},{18,... | collective-permute-start | bytes 393224 | tf_op jit(solution)/shard_map/ppermute | solution.py:302
  34.5 2.5 %collective-permute-done.5 = f32[128,256]{1,0:T(8,128)S(1)} collective-permute-done((f32[128,256]{1,0:T(8,128)S(1)}, f32[128,256]{1,0:T(8,128)S(1)}, u32[]{:S(2)}, u32[]{:S(2)}) %collective-permute-start.5) | collective-permute-done | bytes 131104 | tf_op jit(solution)/shard_map/ppermute | solution.py:302
  37.0 6.2 %collective-permute-start.6 = (f32[128,256]{1,0:T(8,128)S(1)}, f32[128,256]{1,0:T(8,128)S(1)}, u32[]{:S(2)}, u32[]{:S(2)}) collective-permute-start(f32[128,256]{1,0:T(8,128)S(1)} %add.14.refs_0_), channel_id=1, source_target_pairs={{0,24},{8,0},{16,8},{24,16},{1,25},{9,1},{17,9},{25,17},{2,26},{10... | collective-permute-start | bytes 393224 | tf_op jit(solution)/shard_map/ppermute | solution.py:307
  43.2 1.9 %collective-permute-start.7 = (f32[128,256]{1,0:T(8,128)S(1)}, f32[128,256]{1,0:T(8,128)S(1)}, u32[]{:S(2)}, u32[]{:S(2)}) collective-permute-start(f32[128,256]{1,0:T(8,128)S(1)} %add.14.refs_0_), channel_id=1, source_target_pairs={{0,16},{8,24},{16,0},{24,8},{1,17},{9,25},{17,1},{25,9},{2,18},{10... | collective-permute-start | bytes 393224 | tf_op jit(solution)/shard_map/ppermute | solution.py:307
  45.1 2.8 %collective-permute-start.8 = (f32[128,256]{1,0:T(8,128)S(1)}, f32[128,256]{1,0:T(8,128)S(1)}, u32[]{:S(2)}, u32[]{:S(2)}) collective-permute-start(f32[128,256]{1,0:T(8,128)S(1)} %add.14.refs_0_), channel_id=1, source_target_pairs={{0,8},{8,16},{16,24},{24,0},{1,9},{9,17},{17,25},{25,1},{2,10},{10... | collective-permute-start | bytes 393224 | tf_op jit(solution)/shard_map/ppermute | solution.py:307
  47.9 0.0 collective-permute-done.6.refs_1_
  47.9 3.7 %collective-permute-done.7.refs_2_ = f32[128,256]{1,0:T(8,128)S(1)} collective-permute-done((f32[128,256]{1,0:T(8,128)S(1)}, f32[128,256]{1,0:T(8,128)S(1)}, u32[]{:S(2)}, u32[]{:S(2)}) %collective-permute-start.7) | collective-permute-done | bytes 131104 | tf_op jit(solution)/shard_map/ppermute | solution.py:307
  51.6 1.6 %collective-permute-done.8.refs_3_ = f32[128,256]{1,0:T(8,128)S(1)} collective-permute-done((f32[128,256]{1,0:T(8,128)S(1)}, f32[128,256]{1,0:T(8,128)S(1)}, u32[]{:S(2)}, u32[]{:S(2)}) %collective-permute-start.8) | collective-permute-done | bytes 131104 | tf_op jit(solution)/shard_map/ppermute | solution.py:307
  53.2 0.0 all-to-all-done
  53.2 1.3 shard_map.39
  54.5 3.6 %all-to-all-start.1 = ((f32[4,128,256]{2,1,0:T(8,128)}), f32[4,128,256]{2,1,0:T(8,128)S(1)}, u32[]{:S(2)}, u32[]{:S(2)}) async-start(f32[4,128,256]{2,1,0:T(8,128)} %get-tuple-element.21), calls=%async_computation.1 | async-start | bytes 1048576 | tf_op jit(solution)/shard_map/all_to_all | solution.py:312
  58.1 0.0 copy-done
  58.1 0.5 shard_map.40
  58.6 0.0 copy-start.2
  58.6 0.8 copy-done.2
  59.4 6.8 %all-to-all-done.1 = f32[4,128,256]{2,1,0:T(8,128)S(1)} async-done(((f32[4,128,256]{2,1,0:T(8,128)}), f32[4,128,256]{2,1,0:T(8,128)S(1)}, u32[]{:S(2)}, u32[]{:S(2)}) %all-to-all-start.1) | async-done | bytes 524320 | tf_op jit(solution)/shard_map/all_to_all | solution.py:312
  66.2 1.5 %terms.1 = (f32[336,256]{1,0:T(8,128)S(1)}, f32[336,256]{1,0:T(8,128)S(1)}) custom-call(s32[1]{0:T(128)} %bitcast.1.core_ref, bf16[512,512]{1,0:T(8,128)(2,1)S(1)} %get-tuple-element.18.own_high, bf16[256,512]{1,0:T(8,128)(2,1)S(1)} %get-tuple-element.19.panel_high, bf16[256,512]{1,0:T(8,128)(2,1)S(1)} %get-tuple-element.20.panel_low, ...), custom_call_target="tpu_custom_call" | custom-call | flops 603979776 | bytes 1572864 | tf_op jit(solution)/shard_map/terms/pallas_call | solution.py:209
  67.6 1.9 %collective-permute-start.9 = (f32[336,256]{1,0:T(8,128)S(1)}, f32[336,256]{1,0:T(8,128)S(1)}, u32[]{:S(2)}, u32[]{:S(2)}) collective-permute-start(f32[336,256]{1,0:T(8,128)S(1)} %get-tuple-element.24), channel_id=1, source_target_pairs={{0,32},{32,0},{1,33},{33,1},{2,34},{34,2},{3,35},{35,3},{4,36},{36... | collective-permute-start | bytes 1032200 | tf_op jit(solution)/shard_map/ppermute | solution.py:322
  69.6 1.6 %collective-permute-done.9.other_ref = f32[336,256]{1,0:T(8,128)S(1)} collective-permute-done((f32[336,256]{1,0:T(8,128)S(1)}, f32[336,256]{1,0:T(8,128)S(1)}, u32[]{:S(2)}, u32[]{:S(2)}) %collective-permute-start.9) | collective-permute-done | bytes 344096 | tf_op jit(solution)/shard_map/ppermute | solution.py:322
  71.2 13.0 %all_to_all.20.x_ref = f32[4,144,256]{2,1,0:T(8,128)S(1)} all-to-all(f32[4,144,256]{2,1,0:T(8,128)S(1)} %shard_map.41), channel_id=1, replica_groups=mesh['zh'=2,'x'=4,'core'=2,'y'=4,'zl'=8] {'x'}, dimensions={0} | all-to-all | bytes 1179648 | tf_op jit(solution)/shard_map/all_to_all | solution.py:324
  84.2 9.6 %collective-permute-start.11 = (f32[80,256]{1,0:T(8,128)S(1)}, f32[80,256]{1,0:T(8,128)S(1)}, u32[]{:S(2)}, u32[]{:S(2)}) collective-permute-start(f32[80,256]{1,0:T(8,128)S(1)} %get-tuple-element.26), channel_id=1, source_target_pairs={{0,260},{1,261},{2,262},{3,263},{4,256},{5,257},{6,258},{7,259},{2... | collective-permute-start | bytes 245768 | tf_op jit(solution)/shard_map/ppermute | solution.py:329
  93.8 7.1 %collective-permute-done.11 = f32[80,256]{1,0:T(8,128)S(1)} collective-permute-done((f32[80,256]{1,0:T(8,128)S(1)}, f32[80,256]{1,0:T(8,128)S(1)}, u32[]{:S(2)}, u32[]{:S(2)}) %collective-permute-start.11) | collective-permute-done | bytes 81952 | tf_op jit(solution)/shard_map/ppermute | solution.py:329
  101.0 1.9 %collective-permute-start.12 = (f32[80,256]{1,0:T(8,128)S(1)}, f32[80,256]{1,0:T(8,128)S(1)}, u32[]{:S(2)}, u32[]{:S(2)}) collective-permute-start(f32[80,256]{1,0:T(8,128)S(1)} %add.15.mine_ref), channel_id=1, source_target_pairs={{0,32},{32,0},{1,33},{33,1},{2,34},{34,2},{3,35},{35,3},{4,36},{36... | collective-permute-start | bytes 245768 | tf_op jit(solution)/shard_map/ppermute | solution.py:330
  102.9 6.3 %collective-permute-start.10 = (f32[64,256]{1,0:T(8,128)S(1)}, f32[64,256]{1,0:T(8,128)S(1)}, u32[]{:S(2)}, u32[]{:S(2)}) collective-permute-start(f32[64,256]{1,0:T(8,128)S(1)} %get-tuple-element.25.refs_0_), channel_id=1, source_target_pairs={{0,256},{256,0},{1,257},{257,1},{2,258},{258,2},{3,259},{259,3},{4... | collective-permute-start | bytes 196616 | tf_op jit(solution)/shard_map/ppermute | solution.py:331
  109.3 0.7 slice.19
  110.0 8.2 %collective-permute-done.10.refs_1_ = f32[64,256]{1,0:T(8,128)S(1)} collective-permute-done((f32[64,256]{1,0:T(8,128)S(1)}, f32[64,256]{1,0:T(8,128)S(1)}, u32[]{:S(2)}, u32[]{:S(2)}) %collective-permute-start.10) | collective-permute-done | bytes 65568 | tf_op jit(solution)/shard_map/ppermute | solution.py:331
  118.1 0.8 shard_map.43
  118.9 5.5 %all-to-all-start.3 = ((f32[8,64,256]{2,1,0:T(8,128)}), f32[8,64,256]{2,1,0:T(8,128)S(1)}, u32[]{:S(2)}, u32[]{:S(2)}) async-start(f32[8,64,256]{2,1,0:T(8,128)} %shard_map.43), calls=%async_computation.3 | async-start | bytes 1048576 | tf_op jit(solution)/shard_map/all_to_all | solution.py:332
  124.4 0.0 collective-permute-done.12.other_ref
  124.5 10.5 %shard_map.44 = (f32[256,256]{1,0:T(8,128)S(1)}, f32[256,128]{1,0:T(8,128)S(1)}) custom-call(s32[1]{0:T(128)} %bitcast.1.core_ref, f32[80,256]{1,0:T(8,128)S(1)} %add.15.mine_ref, f32[80,256]{1,0:T(8,128)S(1)} %collective-permute-done.12.other_ref, f32[1,256]{1,0:T(1,128)S(1)} %bitcast.14), custom_call_target="tpu_custom_call" | custom-call | flops 6000000000 | bytes 164868 | tf_op jit(solution)/shard_map/pallas_call | solution.py:37
  134.9 0.0 all-to-all-done.3
  135.0 2.7 %finish.1 = f32[512,256]{1,0:T(8,128)} custom-call(s32[1]{0:T(128)} %bitcast.top_ref, f32[512,256]{1,0:T(8,128)S(1)} %bitcast.9, f32[256,256]{1,0:T(8,128)S(1)} %get-tuple-element.27.m_ref, f32[256,128]{1,0:T(8,128)S(1)} %get-tuple-element.28.u_ref), custom_call_target="tpu_custom_call" | custom-call | flops 67108864 | bytes 1048576 | tf_op jit(solution)/shard_map/finish/pallas_call | solution.py:263
  (7 shorter events, 0.2 us)
Async XLA Ops:
  0.0 0.8 copy-start.1
  1.5 51.7 %all-to-all-start = ((f32[8,16,512]{2,1,0:T(8,128)}), f32[8,16,512]{2,1,0:T(8,128)S(1)}, u32[]{:S(2)}, u32[]{:S(2)}) async-start(f32[8,16,512]{2,1,0:T(8,128)} %shard_map.37), calls=%async_computation | async-start | bytes 524288 | tf_op jit(solution)/shard_map/all_to_all | solution.py:304
  15.2 7.1 %collective-permute-start = (f32[128,256]{1,0:T(8,128)S(1)}, f32[128,256]{1,0:T(8,128)S(1)}, u32[]{:S(2)}, u32[]{:S(2)}) collective-permute-start(f32[128,256]{1,0:T(8,128)S(1)} %get-tuple-element.31), channel_id=1, source_target_pairs={{0,8},{32,40},{64,72},{96,104},{128,136},{160,168},{192,200},{224,... | collective-permute-start | bytes 393224 | tf_op jit(solution)/shard_map/ppermute | solution.py:296
  18.6 5.3 %collective-permute-start.1 = (f32[128,256]{1,0:T(8,128)S(1)}, f32[128,256]{1,0:T(8,128)S(1)}, u32[]{:S(2)}, u32[]{:S(2)}) collective-permute-start(f32[128,256]{1,0:T(8,128)S(1)} %get-tuple-element.30), channel_id=1, source_target_pairs={{0,16},{32,48},{64,80},{96,112},{128,144},{160,176},{192,208},{224... | collective-permute-start | bytes 393224 | tf_op jit(solution)/shard_map/ppermute | solution.py:296
  20.9 3.8 %collective-permute-start.2 = (f32[128,256]{1,0:T(8,128)S(1)}, f32[128,256]{1,0:T(8,128)S(1)}, u32[]{:S(2)}, u32[]{:S(2)}) collective-permute-start(f32[128,256]{1,0:T(8,128)S(1)} %get-tuple-element.29), channel_id=1, source_target_pairs={{0,24},{32,56},{64,88},{96,120},{128,152},{160,184},{192,216},{224... | collective-permute-start | bytes 393224 | tf_op jit(solution)/shard_map/ppermute | solution.py:296
  24.8 3.9 %collective-permute-start.3 = (f32[128,256]{1,0:T(8,128)S(1)}, f32[128,256]{1,0:T(8,128)S(1)}, u32[]{:S(2)}, u32[]{:S(2)}) collective-permute-start(f32[128,256]{1,0:T(8,128)S(1)} %shard_map.38), channel_id=1, source_target_pairs={{0,4},{8,12},{16,20},{24,28},{32,36},{40,44},{48,52},{56,60},{64,6... | collective-permute-start | bytes 393224 | tf_op jit(solution)/shard_map/ppermute | solution.py:302
  28.7 4.3 %collective-permute-start.4 = (f32[128,256]{1,0:T(8,128)S(1)}, f32[128,256]{1,0:T(8,128)S(1)}, u32[]{:S(2)}, u32[]{:S(2)}) collective-permute-start(f32[128,256]{1,0:T(8,128)S(1)} %add.12), channel_id=1, source_target_pairs={{0,2},{4,6},{8,10},{12,14},{16,18},{20,22},{24,26},{28,30},{32,34}... | collective-permute-start | bytes 393224 | tf_op jit(solution)/shard_map/ppermute | solution.py:302
  33.1 25.0 %copy-start = (f32[1,512,512]{2,1,0:T(8,128)S(1)}, f32[1,512,512]{2,1,0:T(8,128)}, u32[]{:S(2)}) copy-start(f32[1,512,512]{2,1,0:T(8,128)} %own_ref.1) | copy-start | bytes 3145732
  33.1 3.9 %collective-permute-start.5 = (f32[128,256]{1,0:T(8,128)S(1)}, f32[128,256]{1,0:T(8,128)S(1)}, u32[]{:S(2)}, u32[]{:S(2)}) collective-permute-start(f32[128,256]{1,0:T(8,128)S(1)} %add.13), channel_id=1, source_target_pairs={{0,1},{2,3},{4,5},{6,7},{8,9},{10,11},{12,13},{14,15},{16,17},{18,... | collective-permute-start | bytes 393224 | tf_op jit(solution)/shard_map/ppermute | solution.py:302
  37.0 10.9 %collective-permute-start.6 = (f32[128,256]{1,0:T(8,128)S(1)}, f32[128,256]{1,0:T(8,128)S(1)}, u32[]{:S(2)}, u32[]{:S(2)}) collective-permute-start(f32[128,256]{1,0:T(8,128)S(1)} %add.14.refs_0_), channel_id=1, source_target_pairs={{0,24},{8,0},{16,8},{24,16},{1,25},{9,1},{17,9},{25,17},{2,26},{10... | collective-permute-start | bytes 393224 | tf_op jit(solution)/shard_map/ppermute | solution.py:307
  43.2 8.4 %collective-permute-start.7 = (f32[128,256]{1,0:T(8,128)S(1)}, f32[128,256]{1,0:T(8,128)S(1)}, u32[]{:S(2)}, u32[]{:S(2)}) collective-permute-start(f32[128,256]{1,0:T(8,128)S(1)} %add.14.refs_0_), channel_id=1, source_target_pairs={{0,16},{8,24},{16,0},{24,8},{1,17},{9,25},{17,1},{25,9},{2,18},{10... | collective-permute-start | bytes 393224 | tf_op jit(solution)/shard_map/ppermute | solution.py:307
  45.1 8.1 %collective-permute-start.8 = (f32[128,256]{1,0:T(8,128)S(1)}, f32[128,256]{1,0:T(8,128)S(1)}, u32[]{:S(2)}, u32[]{:S(2)}) collective-permute-start(f32[128,256]{1,0:T(8,128)S(1)} %add.14.refs_0_), channel_id=1, source_target_pairs={{0,8},{8,16},{16,24},{24,0},{1,9},{9,17},{17,25},{25,1},{2,10},{10... | collective-permute-start | bytes 393224 | tf_op jit(solution)/shard_map/ppermute | solution.py:307
  54.5 11.7 %all-to-all-start.1 = ((f32[4,128,256]{2,1,0:T(8,128)}), f32[4,128,256]{2,1,0:T(8,128)S(1)}, u32[]{:S(2)}, u32[]{:S(2)}) async-start(f32[4,128,256]{2,1,0:T(8,128)} %get-tuple-element.21), calls=%async_computation.1 | async-start | bytes 1048576 | tf_op jit(solution)/shard_map/all_to_all | solution.py:312
  58.6 0.8 copy-start.2
  67.6 3.5 %collective-permute-start.9 = (f32[336,256]{1,0:T(8,128)S(1)}, f32[336,256]{1,0:T(8,128)S(1)}, u32[]{:S(2)}, u32[]{:S(2)}) collective-permute-start(f32[336,256]{1,0:T(8,128)S(1)} %get-tuple-element.24), channel_id=1, source_target_pairs={{0,32},{32,0},{1,33},{33,1},{2,34},{34,2},{3,35},{35,3},{4,36},{36... | collective-permute-start | bytes 1032200 | tf_op jit(solution)/shard_map/ppermute | solution.py:322
  84.2 16.7 %collective-permute-start.11 = (f32[80,256]{1,0:T(8,128)S(1)}, f32[80,256]{1,0:T(8,128)S(1)}, u32[]{:S(2)}, u32[]{:S(2)}) collective-permute-start(f32[80,256]{1,0:T(8,128)S(1)} %get-tuple-element.26), channel_id=1, source_target_pairs={{0,260},{1,261},{2,262},{3,263},{4,256},{5,257},{6,258},{7,259},{2... | collective-permute-start | bytes 245768 | tf_op jit(solution)/shard_map/ppermute | solution.py:329
  101.0 23.5 %collective-permute-start.12 = (f32[80,256]{1,0:T(8,128)S(1)}, f32[80,256]{1,0:T(8,128)S(1)}, u32[]{:S(2)}, u32[]{:S(2)}) collective-permute-start(f32[80,256]{1,0:T(8,128)S(1)} %add.15.mine_ref), channel_id=1, source_target_pairs={{0,32},{32,0},{1,33},{33,1},{2,34},{34,2},{3,35},{35,3},{4,36},{36... | collective-permute-start | bytes 245768 | tf_op jit(solution)/shard_map/ppermute | solution.py:330
  102.9 15.2 %collective-permute-start.10 = (f32[64,256]{1,0:T(8,128)S(1)}, f32[64,256]{1,0:T(8,128)S(1)}, u32[]{:S(2)}, u32[]{:S(2)}) collective-permute-start(f32[64,256]{1,0:T(8,128)S(1)} %get-tuple-element.25.refs_0_), channel_id=1, source_target_pairs={{0,256},{256,0},{1,257},{257,1},{2,258},{258,2},{3,259},{259,3},{4... | collective-permute-start | bytes 196616 | tf_op jit(solution)/shard_map/ppermute | solution.py:331
  118.9 16.0 %all-to-all-start.3 = ((f32[8,64,256]{2,1,0:T(8,128)}), f32[8,64,256]{2,1,0:T(8,128)S(1)}, u32[]{:S(2)}, u32[]{:S(2)}) async-start(f32[8,64,256]{2,1,0:T(8,128)} %shard_map.43), calls=%async_computation.3 | async-start | bytes 1048576 | tf_op jit(solution)/shard_map/all_to_all | solution.py:332

commit v5 on v4

--- a/solution.py
+++ b/solution.py
@@ -139,15 +139,17 @@
     return call(copies_body, f32(n, *parts[0].shape), *parts)
 
 
-def solve_body(y_ref, inv_ref, *refs):
-    *parts, panel_ref, o_ref = refs
-    per = parts[0].shape[0]
-    for ahead, part in enumerate(parts):
-        y = lax.rem(y_ref[0] + ahead, len(parts))
-        panel_ref[pl.ds(pl.multiple_of(y * per, per), per)] = part[...]
-    rows = dot(inv_ref[...], panel_ref[...], 1, 0)
-    for i in range(o_ref.shape[0]):
-        o_ref[i] = rows
+def solve_body(masks, zl_ref, first_ref, second_ref, panel_ref, o_ref):
+    panel = panel_ref[...]
+    per = 2 * first_ref.shape[0] // len(masks)
+    blocks = []
+    for ref in (first_ref, second_ref):
+        rows = dot(ref[...], panel, 1, 0)
+        blocks += [rows[at : at + per] for at in range(0, rows.shape[0], per)]
+    for mask, block in zip(masks, blocks):
+        at = pl.ds(pl.multiple_of((zl_ref[0] ^ mask) * per, per), per)
+        for i in range(o_ref.shape[0]):
+            o_ref[i, at] = block
 
 
 def total_body(x_ref, *outs):
@@ -291,23 +293,27 @@
     one = lambda i: i.astype(jnp.int32).reshape(1)
     per = depth // n_y
     cut = lambda k: own[per * k : per * k + per, :PANEL]
+    steps = [n_zl >> i for i in range(1, n_zl.bit_length())]
+    inv, masks = inverse_slabs[0], [0]
+    for step in steps:
+        far = lax.ppermute(inv, "zl", [(z, z ^ step) for z in range(n_zl)])
+        masks = masks + [m ^ step for m in masks]
+        if step > 1:
+            inv = jnp.concatenate([inv, far], axis=0)
     parts = []
     for k in range(1, n_y):
         parts.append(lax.ppermute(cut(k), ("y", "zl"), [(0, k * n_zl)]))
     first = jnp.where((y == 0) & (zl == 0), cut(0), 0.0)
     mine = call(sum_body, f32(per, PANEL), first, *parts)
-    step = n_zl // 2
-    while step:
+    for step in steps:
         pairs = [(z, z + step) for z in range(0, n_zl, 2 * step)]
-        mine = mine + lax.ppermute(mine, "zl", pairs)
-        step //= 2
-    inv = swap(copies(n_zl, inverse_slabs[0]), "zl").reshape(per, depth)
-    parts = [mine]
-    for k in range(1, n_y):
-        parts.append(lax.ppermute(mine, "y", [(i, (i - k) % n_y) for i in range(n_y)]))
-    panel, solved = call(
-        solve_body, [f32(depth, PANEL), f32(n_y, per, PANEL)], one(y), inv, *parts,
-        flops=2 * per * depth * PANEL, scalars=1,
+        got = lax.ppermute(mine, "zl", pairs)
+        if step > 1:
+            mine = mine + got
+    panel = swap(copies(n_y, mine, got), "y").reshape(depth, PANEL)
+    solved = call(
+        functools.partial(solve_body, masks), f32(n_y, per, PANEL),
+        one(zl), inv, far, panel, flops=2 * per * depth * PANEL, scalars=1,
     )
     solved = swap(solved, "y").reshape(depth, PANEL)
     core = one(lax.axis_index("core"))

time: 140 us -> 141 us (level)
  starting transfers between devices: 63.3 us -> 65.4 us
    all_to_all x1, starting transfers between devices: 12.5 us -> 4.25 us  [shards(): panel = swap(copies(n_y, mine, got), 'y').reshape(depth, PANEL)]
    ppermute x6, starting transfers between devices: 14.9 us -> 19.1 us  [the longest x3 15.2 us: shards(): far = lax.ppermute(inv, 'zl', [(z, z ^ step) for z in range(n_zl)])]
    ppermute x1, starting transfers between devices: 9.57 us -> 13.6 us  [shards(): pivot = pivot + lax.ppermute(pivot, ('zh', 'zl'), flip)]
    ppermute x3, waiting for transfers between devices: 2.49 us -> 4.23 us  [shards(): parts.append(lax.ppermute(cut(k), ('y', 'zl'), [(0, k * n_zl)]))]
where the time goes in v5:
time: 141 us; the launch traced here: 138 us
  starting transfers between devices  65.4 us (46%)
  waiting for transfers between devices  38.7 us (27%)
  Pallas kernels  18.4 us (13%)
  blocking collectives  13 us (9%)
  local copies, waits for them, and re-layouts  1.49 us (1%)
    ppermute x3, starting transfers between devices, shards(): far = lax.ppermute(inv, 'zl', [(z, z ^ step) for z in range(n_zl)])  15.2 us
    pallas_call x8, Pallas kernels, call(): pl.pallas_call(body, compiler_params=PARAMS, out_shape=outs, in_specs=[sm...  14.2 us
    ppermute x1, starting transfers between devices, shards(): pivot = pivot + lax.ppermute(pivot, ('zh', 'zl'), flip)  13.6 us
    all_to_all x1, blocking collectives, shards(): terms = swap(terms, 'x')  13 us
    ppermute x1, waiting for transfers between devices, shards(): other = lax.ppermute(rows, 'zh', [(0, 1), (1, 0)])  7.63 us
    ppermute x3, starting transfers between devices, shards(): parts.append(lax.ppermute(cut(k), ('y', 'zl'), [(0, k * n_zl)]))  7.52 us
    ppermute x3, waiting for transfers between devices, shards(): far = lax.ppermute(inv, 'zl', [(z, z ^ step) for z in range(n_zl)])  7.17 us
    all_to_all x1, waiting for transfers between devices, shards(): solved = swap(solved, 'y').reshape(depth, PANEL)  6.8 us
  transfers between devices with their start and end apart: 16, of which 11 were waited for; matrix products, arithmetic and copies ran while one was open for 1% of the time, Pallas kernels for 9%

profile of v5, /device:TPU:6, one launch (start us, length us, event | category | flops | bytes accessed | tf_op | source)
XLA Modules:
  0.0 138.3 jit_solution(7521372172752978049)
XLA Ops:
  0.0 1.1 fusion
  1.1 4.9 %collective-permute-start.2 = (f32[128,256]{1,0:T(8,128)S(1)}, f32[128,256]{1,0:T(8,128)S(1)}, u32[]{:S(2)}, u32[]{:S(2)}) collective-permute-start(f32[128,256]{1,0:T(8,128)S(1)} %get-tuple-element.25), channel_id=1, source_target_pairs={{0,24},{32,56},{64,88},{96,120},{128,152},{160,184},{192,216},{224... | collective-permute-start | bytes 393224 | tf_op jit(solution)/shard_map/ppermute | solution.py:305
  6.1 1.3 collective-permute-start.1
  7.4 1.3 collective-permute-start
  8.7 0.1 collective-permute-done.2.refs_3_
  8.8 2.4 %collective-permute-done.1.refs_2_ = f32[128,256]{1,0:T(8,128)S(1)} collective-permute-done((f32[128,256]{1,0:T(8,128)S(1)}, f32[128,256]{1,0:T(8,128)S(1)}, u32[]{:S(2)}, u32[]{:S(2)}) %collective-permute-start.1) | collective-permute-done | bytes 131104 | tf_op jit(solution)/shard_map/ppermute | solution.py:305
  11.2 1.7 %collective-permute-done.refs_1_ = f32[128,256]{1,0:T(8,128)S(1)} collective-permute-done((f32[128,256]{1,0:T(8,128)S(1)}, f32[128,256]{1,0:T(8,128)S(1)}, u32[]{:S(2)}, u32[]{:S(2)}) %collective-permute-start) | collective-permute-done | bytes 131104 | tf_op jit(solution)/shard_map/ppermute | solution.py:305
  13.0 1.3 collective-permute-start.3
  14.3 2.5 %collective-permute-done.3 = f32[128,256]{1,0:T(8,128)S(1)} collective-permute-done((f32[128,256]{1,0:T(8,128)S(1)}, f32[128,256]{1,0:T(8,128)S(1)}, u32[]{:S(2)}, u32[]{:S(2)}) %collective-permute-start.3) | collective-permute-done | bytes 131104 | tf_op jit(solution)/shard_map/ppermute | solution.py:310
  16.8 0.0 copy-start.2
  16.8 1.3 collective-permute-start.4
  18.1 2.9 %collective-permute-done.4 = f32[128,256]{1,0:T(8,128)S(1)} collective-permute-done((f32[128,256]{1,0:T(8,128)S(1)}, f32[128,256]{1,0:T(8,128)S(1)}, u32[]{:S(2)}, u32[]{:S(2)}) %collective-permute-start.4) | collective-permute-done | bytes 131104 | tf_op jit(solution)/shard_map/ppermute | solution.py:310
  21.0 1.3 collective-permute-start.5
  22.3 0.0 copy-done.2
  22.3 8.0 %collective-permute-start.6 = (f32[16,512]{1,0:T(8,128)S(1)}, f32[16,512]{1,0:T(8,128)S(1)}, u32[]{:S(2)}, u32[]{:S(2)}) collective-permute-start(f32[16,512]{1,0:T(8,128)S(1)} %bitcast.15), channel_id=1, source_target_pairs={{0,4},{1,5},{2,6},{3,7},{4,0},{5,1},{6,2},{7,3},{8,12},{9,13},{10,... | collective-permute-start | bytes 98312 | tf_op jit(solution)/shard_map/ppermute | solution.py:299
  30.3 0.0 collective-permute-done.5.refs_1_
  30.3 0.8 shard_map.38
  31.2 4.2 %all-to-all-start = ((f32[4,128,256]{2,1,0:T(8,128)}), f32[4,128,256]{2,1,0:T(8,128)S(1)}, u32[]{:S(2)}, u32[]{:S(2)}) async-start(f32[4,128,256]{2,1,0:T(8,128)} %shard_map.38), calls=%async_computation | async-start | bytes 1048576 | tf_op jit(solution)/shard_map/all_to_all | solution.py:313
  35.4 0.0 collective-permute-done.6
  35.4 5.3 %collective-permute-start.7 = (f32[32,512]{1,0:T(8,128)S(1)}, f32[32,512]{1,0:T(8,128)S(1)}, u32[]{:S(2)}, u32[]{:S(2)}) collective-permute-start(f32[32,512]{1,0:T(8,128)S(1)} %pad_maximum_fusion.1), channel_id=1, source_target_pairs={{0,2},{1,3},{2,0},{3,1},{4,6},{5,7},{6,4},{7,5},{8,10},{9,11},{10,... | collective-permute-start | bytes 196616 | tf_op jit(solution)/shard_map/ppermute | solution.py:299
  40.7 2.2 %collective-permute-done.7 = f32[32,512]{1,0:T(8,128)S(1)} collective-permute-done((f32[32,512]{1,0:T(8,128)S(1)}, f32[32,512]{1,0:T(8,128)S(1)}, u32[]{:S(2)}, u32[]{:S(2)}) %collective-permute-start.7) | collective-permute-done | bytes 65568 | tf_op jit(solution)/shard_map/ppermute | solution.py:299
  43.0 1.9 %collective-permute-start.8 = (f32[64,512]{1,0:T(8,128)S(1)}, f32[64,512]{1,0:T(8,128)S(1)}, u32[]{:S(2)}, u32[]{:S(2)}) collective-permute-start(f32[64,512]{1,0:T(8,128)S(1)} %pad_maximum_fusion.first_ref), channel_id=1, source_target_pairs={{0,1},{1,0},{2,3},{3,2},{4,5},{5,4},{6,7},{7,6},{8,9},{9,8},{10,11... | collective-permute-start | bytes 393224 | tf_op jit(solution)/shard_map/ppermute | solution.py:299
  44.9 4.9 %collective-permute-done.8.second_ref = f32[64,512]{1,0:T(8,128)S(1)} collective-permute-done((f32[64,512]{1,0:T(8,128)S(1)}, f32[64,512]{1,0:T(8,128)S(1)}, u32[]{:S(2)}, u32[]{:S(2)}) %collective-permute-start.8) | collective-permute-done | bytes 131104 | tf_op jit(solution)/shard_map/ppermute | solution.py:299
  49.8 0.0 all-to-all-done
  49.8 0.0 copy-start
  49.8 1.5 %shard_map.40 = f32[4,128,256]{2,1,0:T(8,128)} custom-call(s32[1]{0:T(128)} %bitcast.4.zl_ref, f32[64,512]{1,0:T(8,128)S(1)} %pad_maximum_fusion.first_ref, f32[64,512]{1,0:T(8,128)S(1)} %collective-permute-done.8.second_ref, f32[512,256]{1,0:T(8,128)S(1)} %bitcast.9), custom_call_target="tpu_custom_call" | custom-call | flops 33554432 | bytes 786436 | tf_op jit(solution)/shard_map/pallas_call | solution.py:37
  51.3 4.8 %all-to-all-start.1 = ((f32[4,128,256]{2,1,0:T(8,128)}), f32[4,128,256]{2,1,0:T(8,128)S(1)}, u32[]{:S(2)}, u32[]{:S(2)}) async-start(f32[4,128,256]{2,1,0:T(8,128)} %shard_map.40), calls=%async_computation.1 | async-start | bytes 1048576 | tf_op jit(solution)/shard_map/all_to_all | solution.py:318
  56.1 0.0 copy-done
  56.1 0.5 shard_map.39
  56.6 0.0 copy-start.1
  56.6 0.8 copy-done.1
  57.4 6.8 %all-to-all-done.1 = f32[4,128,256]{2,1,0:T(8,128)S(1)} async-done(((f32[4,128,256]{2,1,0:T(8,128)}), f32[4,128,256]{2,1,0:T(8,128)S(1)}, u32[]{:S(2)}, u32[]{:S(2)}) %all-to-all-start.1) | async-done | bytes 524320 | tf_op jit(solution)/shard_map/all_to_all | solution.py:318
  64.2 1.5 %terms.1 = (f32[336,256]{1,0:T(8,128)S(1)}, f32[336,256]{1,0:T(8,128)S(1)}) custom-call(s32[1]{0:T(128)} %bitcast.1.core_ref, bf16[512,512]{1,0:T(8,128)(2,1)S(1)} %get-tuple-element.15.own_high, bf16[256,512]{1,0:T(8,128)(2,1)S(1)} %get-tuple-element.16.panel_high, bf16[256,512]{1,0:T(8,128)(2,1)S(1)} %get-tuple-element.17.panel_low, ...), custom_call_target="tpu_custom_call" | custom-call | flops 603979776 | bytes 1572864 | tf_op jit(solution)/shard_map/terms/pallas_call | solution.py:211
  65.7 1.9 %collective-permute-start.9 = (f32[336,256]{1,0:T(8,128)S(1)}, f32[336,256]{1,0:T(8,128)S(1)}, u32[]{:S(2)}, u32[]{:S(2)}) collective-permute-start(f32[336,256]{1,0:T(8,128)S(1)} %get-tuple-element.20), channel_id=1, source_target_pairs={{0,32},{32,0},{1,33},{33,1},{2,34},{34,2},{3,35},{35,3},{4,36},{36... | collective-permute-start | bytes 1032200 | tf_op jit(solution)/shard_map/ppermute | solution.py:328
  67.6 1.6 %collective-permute-done.9.other_ref = f32[336,256]{1,0:T(8,128)S(1)} collective-permute-done((f32[336,256]{1,0:T(8,128)S(1)}, f32[336,256]{1,0:T(8,128)S(1)}, u32[]{:S(2)}, u32[]{:S(2)}) %collective-permute-start.9) | collective-permute-done | bytes 344096 | tf_op jit(solution)/shard_map/ppermute | solution.py:328
  69.3 13.0 %all_to_all.20.x_ref = f32[4,144,256]{2,1,0:T(8,128)S(1)} all-to-all(f32[4,144,256]{2,1,0:T(8,128)S(1)} %shard_map.41), channel_id=1, replica_groups=mesh['zh'=2,'x'=4,'core'=2,'y'=4,'zl'=8] {'x'}, dimensions={0} | all-to-all | bytes 1179648 | tf_op jit(solution)/shard_map/all_to_all | solution.py:330
  82.3 13.6 %collective-permute-start.11 = (f32[80,256]{1,0:T(8,128)S(1)}, f32[80,256]{1,0:T(8,128)S(1)}, u32[]{:S(2)}, u32[]{:S(2)}) collective-permute-start(f32[80,256]{1,0:T(8,128)S(1)} %get-tuple-element.22), channel_id=1, source_target_pairs={{0,260},{1,261},{2,262},{3,263},{4,256},{5,257},{6,258},{7,259},{2... | collective-permute-start | bytes 245768 | tf_op jit(solution)/shard_map/ppermute | solution.py:335
  96.0 5.8 %collective-permute-done.11 = f32[80,256]{1,0:T(8,128)S(1)} collective-permute-done((f32[80,256]{1,0:T(8,128)S(1)}, f32[80,256]{1,0:T(8,128)S(1)}, u32[]{:S(2)}, u32[]{:S(2)}) %collective-permute-start.11) | collective-permute-done | bytes 81952 | tf_op jit(solution)/shard_map/ppermute | solution.py:335
  101.8 1.9 %collective-permute-start.12 = (f32[80,256]{1,0:T(8,128)S(1)}, f32[80,256]{1,0:T(8,128)S(1)}, u32[]{:S(2)}, u32[]{:S(2)}) collective-permute-start(f32[80,256]{1,0:T(8,128)S(1)} %add.11.mine_ref), channel_id=1, source_target_pairs={{0,32},{32,0},{1,33},{33,1},{2,34},{34,2},{3,35},{35,3},{4,36},{36... | collective-permute-start | bytes 245768 | tf_op jit(solution)/shard_map/ppermute | solution.py:336
  103.7 6.8 %collective-permute-start.10 = (f32[64,256]{1,0:T(8,128)S(1)}, f32[64,256]{1,0:T(8,128)S(1)}, u32[]{:S(2)}, u32[]{:S(2)}) collective-permute-start(f32[64,256]{1,0:T(8,128)S(1)} %get-tuple-element.21.refs_0_), channel_id=1, source_target_pairs={{0,256},{256,0},{1,257},{257,1},{2,258},{258,2},{3,259},{259,3},{4... | collective-permute-start | bytes 196616 | tf_op jit(solution)/shard_map/ppermute | solution.py:337
  110.5 0.7 slice.19
  111.2 7.6 %collective-permute-done.10.refs_1_ = f32[64,256]{1,0:T(8,128)S(1)} collective-permute-done((f32[64,256]{1,0:T(8,128)S(1)}, f32[64,256]{1,0:T(8,128)S(1)}, u32[]{:S(2)}, u32[]{:S(2)}) %collective-permute-start.10) | collective-permute-done | bytes 65568 | tf_op jit(solution)/shard_map/ppermute | solution.py:337
  118.8 0.8 shard_map.43
  119.6 5.5 %all-to-all-start.3 = ((f32[8,64,256]{2,1,0:T(8,128)}), f32[8,64,256]{2,1,0:T(8,128)S(1)}, u32[]{:S(2)}, u32[]{:S(2)}) async-start(f32[8,64,256]{2,1,0:T(8,128)} %shard_map.43), calls=%async_computation.3 | async-start | bytes 1048576 | tf_op jit(solution)/shard_map/all_to_all | solution.py:338
  125.1 0.0 collective-permute-done.12.other_ref
  125.1 10.5 %shard_map.44 = (f32[256,256]{1,0:T(8,128)S(1)}, f32[256,128]{1,0:T(8,128)S(1)}) custom-call(s32[1]{0:T(128)} %bitcast.1.core_ref, f32[80,256]{1,0:T(8,128)S(1)} %add.11.mine_ref, f32[80,256]{1,0:T(8,128)S(1)} %collective-permute-done.12.other_ref, f32[1,256]{1,0:T(1,128)S(1)} %bitcast.14), custom_call_target="tpu_custom_call" | custom-call | flops 6000000000 | bytes 164868 | tf_op jit(solution)/shard_map/pallas_call | solution.py:37
  135.6 0.0 all-to-all-done.3
  135.6 2.7 %finish.1 = f32[512,256]{1,0:T(8,128)} custom-call(s32[1]{0:T(128)} %bitcast.top_ref, f32[512,256]{1,0:T(8,128)S(1)} %bitcast.11, f32[256,256]{1,0:T(8,128)S(1)} %get-tuple-element.23.m_ref, f32[256,128]{1,0:T(8,128)S(1)} %get-tuple-element.24.u_ref), custom_call_target="tpu_custom_call" | custom-call | flops 67108864 | bytes 1048576 | tf_op jit(solution)/shard_map/finish/pallas_call | solution.py:265
  (8 shorter events, 0.2 us)
Async XLA Ops:
  1.1 7.7 %collective-permute-start.2 = (f32[128,256]{1,0:T(8,128)S(1)}, f32[128,256]{1,0:T(8,128)S(1)}, u32[]{:S(2)}, u32[]{:S(2)}) collective-permute-start(f32[128,256]{1,0:T(8,128)S(1)} %get-tuple-element.25), channel_id=1, source_target_pairs={{0,24},{32,56},{64,88},{96,120},{128,152},{160,184},{192,216},{224... | collective-permute-start | bytes 393224 | tf_op jit(solution)/shard_map/ppermute | solution.py:305
  6.1 5.2 %collective-permute-start.1 = (f32[128,256]{1,0:T(8,128)S(1)}, f32[128,256]{1,0:T(8,128)S(1)}, u32[]{:S(2)}, u32[]{:S(2)}) collective-permute-start(f32[128,256]{1,0:T(8,128)S(1)} %get-tuple-element.26), channel_id=1, source_target_pairs={{0,16},{32,48},{64,80},{96,112},{128,144},{160,176},{192,208},{224... | collective-permute-start | bytes 393224 | tf_op jit(solution)/shard_map/ppermute | solution.py:305
  7.4 5.5 %collective-permute-start = (f32[128,256]{1,0:T(8,128)S(1)}, f32[128,256]{1,0:T(8,128)S(1)}, u32[]{:S(2)}, u32[]{:S(2)}) collective-permute-start(f32[128,256]{1,0:T(8,128)S(1)} %get-tuple-element.27), channel_id=1, source_target_pairs={{0,8},{32,40},{64,72},{96,104},{128,136},{160,168},{192,200},{224,... | collective-permute-start | bytes 393224 | tf_op jit(solution)/shard_map/ppermute | solution.py:305
  13.0 3.8 %collective-permute-start.3 = (f32[128,256]{1,0:T(8,128)S(1)}, f32[128,256]{1,0:T(8,128)S(1)}, u32[]{:S(2)}, u32[]{:S(2)}) collective-permute-start(f32[128,256]{1,0:T(8,128)S(1)} %shard_map.37), channel_id=1, source_target_pairs={{0,4},{8,12},{16,20},{24,28},{32,36},{40,44},{48,52},{56,60},{64,6... | collective-permute-start | bytes 393224 | tf_op jit(solution)/shard_map/ppermute | solution.py:310
  16.8 5.5 %copy-start.2 = (f32[1,16,512]{2,1,0:T(8,128)S(1)}, f32[1,16,512]{2,1,0:T(8,128)}, u32[]{:S(2)}) copy-start(f32[1,16,512]{2,1,0:T(8,128)} %param.4) | copy-start | bytes 98308
  16.8 4.2 %collective-permute-start.4 = (f32[128,256]{1,0:T(8,128)S(1)}, f32[128,256]{1,0:T(8,128)S(1)}, u32[]{:S(2)}, u32[]{:S(2)}) collective-permute-start(f32[128,256]{1,0:T(8,128)S(1)} %add.9), channel_id=1, source_target_pairs={{0,2},{4,6},{8,10},{12,14},{16,18},{20,22},{24,26},{28,30},{32,34}... | collective-permute-start | bytes 393224 | tf_op jit(solution)/shard_map/ppermute | solution.py:310
  21.0 9.3 %collective-permute-start.5 = (f32[128,256]{1,0:T(8,128)S(1)}, f32[128,256]{1,0:T(8,128)S(1)}, u32[]{:S(2)}, u32[]{:S(2)}) collective-permute-start(f32[128,256]{1,0:T(8,128)S(1)} %add.10.refs_0_), channel_id=1, source_target_pairs={{0,1},{2,3},{4,5},{6,7},{8,9},{10,11},{12,13},{14,15},{16,17},{18,... | collective-permute-start | bytes 393224 | tf_op jit(solution)/shard_map/ppermute | solution.py:310
  22.3 13.1 %collective-permute-start.6 = (f32[16,512]{1,0:T(8,128)S(1)}, f32[16,512]{1,0:T(8,128)S(1)}, u32[]{:S(2)}, u32[]{:S(2)}) collective-permute-start(f32[16,512]{1,0:T(8,128)S(1)} %bitcast.15), channel_id=1, source_target_pairs={{0,4},{1,5},{2,6},{3,7},{4,0},{5,1},{6,2},{7,3},{8,12},{9,13},{10,... | collective-permute-start | bytes 98312 | tf_op jit(solution)/shard_map/ppermute | solution.py:299
  31.2 18.7 %all-to-all-start = ((f32[4,128,256]{2,1,0:T(8,128)}), f32[4,128,256]{2,1,0:T(8,128)S(1)}, u32[]{:S(2)}, u32[]{:S(2)}) async-start(f32[4,128,256]{2,1,0:T(8,128)} %shard_map.38), calls=%async_computation | async-start | bytes 1048576 | tf_op jit(solution)/shard_map/all_to_all | solution.py:313
  35.4 7.5 %collective-permute-start.7 = (f32[32,512]{1,0:T(8,128)S(1)}, f32[32,512]{1,0:T(8,128)S(1)}, u32[]{:S(2)}, u32[]{:S(2)}) collective-permute-start(f32[32,512]{1,0:T(8,128)S(1)} %pad_maximum_fusion.1), channel_id=1, source_target_pairs={{0,2},{1,3},{2,0},{3,1},{4,6},{5,7},{6,4},{7,5},{8,10},{9,11},{10,... | collective-permute-start | bytes 196616 | tf_op jit(solution)/shard_map/ppermute | solution.py:299
  43.0 6.9 %collective-permute-start.8 = (f32[64,512]{1,0:T(8,128)S(1)}, f32[64,512]{1,0:T(8,128)S(1)}, u32[]{:S(2)}, u32[]{:S(2)}) collective-permute-start(f32[64,512]{1,0:T(8,128)S(1)} %pad_maximum_fusion.first_ref), channel_id=1, source_target_pairs={{0,1},{1,0},{2,3},{3,2},{4,5},{5,4},{6,7},{7,6},{8,9},{9,8},{10,11... | collective-permute-start | bytes 393224 | tf_op jit(solution)/shard_map/ppermute | solution.py:299
  49.8 6.3 %copy-start = (f32[1,512,512]{2,1,0:T(8,128)S(1)}, f32[1,512,512]{2,1,0:T(8,128)}, u32[]{:S(2)}) copy-start(f32[1,512,512]{2,1,0:T(8,128)} %own_ref.1) | copy-start | bytes 3145732
  51.3 12.9 %all-to-all-start.1 = ((f32[4,128,256]{2,1,0:T(8,128)}), f32[4,128,256]{2,1,0:T(8,128)S(1)}, u32[]{:S(2)}, u32[]{:S(2)}) async-start(f32[4,128,256]{2,1,0:T(8,128)} %shard_map.40), calls=%async_computation.1 | async-start | bytes 1048576 | tf_op jit(solution)/shard_map/all_to_all | solution.py:318
  56.6 0.8 copy-start.1
  65.7 3.5 %collective-permute-start.9 = (f32[336,256]{1,0:T(8,128)S(1)}, f32[336,256]{1,0:T(8,128)S(1)}, u32[]{:S(2)}, u32[]{:S(2)}) collective-permute-start(f32[336,256]{1,0:T(8,128)S(1)} %get-tuple-element.20), channel_id=1, source_target_pairs={{0,32},{32,0},{1,33},{33,1},{2,34},{34,2},{3,35},{35,3},{4,36},{36... | collective-permute-start | bytes 1032200 | tf_op jit(solution)/shard_map/ppermute | solution.py:328
  82.3 19.4 %collective-permute-start.11 = (f32[80,256]{1,0:T(8,128)S(1)}, f32[80,256]{1,0:T(8,128)S(1)}, u32[]{:S(2)}, u32[]{:S(2)}) collective-permute-start(f32[80,256]{1,0:T(8,128)S(1)} %get-tuple-element.22), channel_id=1, source_target_pairs={{0,260},{1,261},{2,262},{3,263},{4,256},{5,257},{6,258},{7,259},{2... | collective-permute-start | bytes 245768 | tf_op jit(solution)/shard_map/ppermute | solution.py:335
  101.8 23.4 %collective-permute-start.12 = (f32[80,256]{1,0:T(8,128)S(1)}, f32[80,256]{1,0:T(8,128)S(1)}, u32[]{:S(2)}, u32[]{:S(2)}) collective-permute-start(f32[80,256]{1,0:T(8,128)S(1)} %add.11.mine_ref), channel_id=1, source_target_pairs={{0,32},{32,0},{1,33},{33,1},{2,34},{34,2},{3,35},{35,3},{4,36},{36... | collective-permute-start | bytes 245768 | tf_op jit(solution)/shard_map/ppermute | solution.py:336
  103.7 15.1 %collective-permute-start.10 = (f32[64,256]{1,0:T(8,128)S(1)}, f32[64,256]{1,0:T(8,128)S(1)}, u32[]{:S(2)}, u32[]{:S(2)}) collective-permute-start(f32[64,256]{1,0:T(8,128)S(1)} %get-tuple-element.21.refs_0_), channel_id=1, source_target_pairs={{0,256},{256,0},{1,257},{257,1},{2,258},{258,2},{3,259},{259,3},{4... | collective-permute-start | bytes 196616 | tf_op jit(solution)/shard_map/ppermute | solution.py:337
  119.6 16.0 %all-to-all-start.3 = ((f32[8,64,256]{2,1,0:T(8,128)}), f32[8,64,256]{2,1,0:T(8,128)S(1)}, u32[]{:S(2)}, u32[]{:S(2)}) async-start(f32[8,64,256]{2,1,0:T(8,128)} %shard_map.43), calls=%async_computation.3 | async-start | bytes 1048576 | tf_op jit(solution)/shard_map/all_to_all | solution.py:338

commit v6 on v4

--- a/solution.py
+++ b/solution.py
@@ -85,11 +85,12 @@
     b = BLOCK
     third = p[2 * b :]
     third = jnp.concatenate([third[:, LANES:], third[:, :LANES]], axis=0)
+    diag = jnp.concatenate([diag_ref[0:1], diag_ref[1:2]], axis=1)
     blocks = (p[:b], p[b : 2 * b], jnp.concatenate([third, third], axis=1))
     r = lax.broadcasted_iota(jnp.int32, (b, PANEL), 0)
     c = lax.broadcasted_iota(jnp.int32, (b, PANEL), 1)
     for i, rows in enumerate(blocks + (pltpu.roll(p[b : 2 * b], 3 * b, 1),)):
-        m_ref[b * i : b * i + b] = rows + jnp.where(r + b * i == c, diag_ref[...], 0.0)
+        m_ref[b * i : b * i + b] = rows + jnp.where(r + b * i == c, diag, 0.0)
     lane = lax.broadcasted_iota(jnp.int32, (BLOCK, LANES), 1)
     sub = lax.broadcasted_iota(jnp.int32, (BLOCK, LANES), 0)
     wlane = lax.broadcasted_iota(jnp.int32, (BLOCK, PANEL), 1)
@@ -139,12 +140,7 @@
     return call(copies_body, f32(n, *parts[0].shape), *parts)
 
 
-def solve_body(y_ref, inv_ref, *refs):
-    *parts, panel_ref, o_ref = refs
-    per = parts[0].shape[0]
-    for ahead, part in enumerate(parts):
-        y = lax.rem(y_ref[0] + ahead, len(parts))
-        panel_ref[pl.ds(pl.multiple_of(y * per, per), per)] = part[...]
+def solve_body(inv_ref, panel_ref, o_ref):
     rows = dot(inv_ref[...], panel_ref[...], 1, 0)
     for i in range(o_ref.shape[0]):
         o_ref[i] = rows
@@ -299,16 +295,13 @@
     step = n_zl // 2
     while step:
         pairs = [(z, z + step) for z in range(0, n_zl, 2 * step)]
-        mine = mine + lax.ppermute(mine, "zl", pairs)
+        got = lax.ppermute(mine, "zl", pairs)
+        if step > 1:
+            mine = mine + got
         step //= 2
+    panel = swap(copies(n_y, mine, got), "y").reshape(depth, PANEL)
     inv = swap(copies(n_zl, inverse_slabs[0]), "zl").reshape(per, depth)
-    parts = [mine]
-    for k in range(1, n_y):
-        parts.append(lax.ppermute(mine, "y", [(i, (i - k) % n_y) for i in range(n_y)]))
-    panel, solved = call(
-        solve_body, [f32(depth, PANEL), f32(n_y, per, PANEL)], one(y), inv, *parts,
-        flops=2 * per * depth * PANEL, scalars=1,
-    )
+    solved = call(solve_body, f32(n_y, per, PANEL), inv, panel, flops=2 * per * depth * PANEL)
     solved = swap(solved, "y").reshape(depth, PANEL)
     core = one(lax.axis_index("core"))
     parts = call(
@@ -333,7 +326,7 @@
 
     m, u = call(
         factor_body, [f32(PANEL, PANEL), f32(PANEL, LANES)],
-        core, pivot, other_pivot, barrier_diagonal[:PANEL].reshape(1, PANEL),
+        core, pivot, other_pivot, barrier_diagonal.reshape(-1, LANES),
         flops=6 * 10**9, scalars=1,
     )
     top = one((y == 0) & (zl == 0))

time: 140 us -> 137 us (0.979)
  blocking collectives: 13 us -> 25.2 us
  starting transfers between devices: 63.3 us -> 52.3 us
  waiting for transfers between devices: 39.6 us -> 36.6 us
    all_to_all x0 -> x1, blocking collectives: none -> 12.3 us  [shards(): panel = swap(copies(n_y, mine, got), 'y').reshape(depth, PANEL)]
    ppermute x6 -> x3, starting transfers between devices: 14.9 us -> 3.89 us  [shards(): got = lax.ppermute(mine, 'zl', pairs)]
    ppermute x6 -> x3, waiting for transfers between devices: 13.4 us -> 8.27 us  [shards(): got = lax.ppermute(mine, 'zl', pairs)]
    ppermute x3, waiting for transfers between devices: 2.49 us -> 3.95 us  [shards(): parts.append(lax.ppermute(cut(k), ('y', 'zl'), [(0, k * n_zl)]))]
    pallas_call x8 -> x9, Pallas kernels: 13.9 us -> 13.9 us  [call(): pl.pallas_call(body, compiler_params=PARAMS, out_shape=outs, in_specs=[sm...]
  transfers between devices with their start and end apart: 16 -> 13, of which waited for: 11 -> 9; matrix products, arithmetic and copies ran while one was open for 1% -> 1% of each run, Pallas kernels for 9% -> 9%
where the time goes in v6:
time: 137 us; the launch traced here: 135 us
  starting transfers between devices  52.3 us (38%)
  waiting for transfers between devices  36.6 us (27%)
  blocking collectives  25.2 us (18%)
  Pallas kernels  18 us (13%)
  local copies, waits for them, and re-layouts  1.57 us (1%)
    pallas_call x9, Pallas kernels, call(): pl.pallas_call(body, compiler_params=PARAMS, out_shape=outs, in_specs=[sm...  13.9 us
    all_to_all x1, blocking collectives, shards(): terms = swap(terms, 'x')  13 us
    all_to_all x1, starting transfers between devices, shards(): inv = swap(copies(n_zl, inverse_slabs[0]), 'zl').reshape(per, depth)  12.5 us
    all_to_all x1, blocking collectives, shards(): panel = swap(copies(n_y, mine, got), 'y').reshape(depth, PANEL)  12.3 us
    ppermute x1, starting transfers between devices, shards(): pivot = pivot + lax.ppermute(pivot, ('zh', 'zl'), flip)  9.07 us
    ppermute x1, waiting for transfers between devices, shards(): other = lax.ppermute(rows, 'zh', [(0, 1), (1, 0)])  8.85 us
    ppermute x3, waiting for transfers between devices, shards(): got = lax.ppermute(mine, 'zl', pairs)  8.27 us
    ppermute x3, starting transfers between devices, shards(): parts.append(lax.ppermute(cut(k), ('y', 'zl'), [(0, k * n_zl)]))  7.52 us
  transfers between devices with their start and end apart: 13, of which 9 were waited for; matrix products, arithmetic and copies ran while one was open for 1% of the time, Pallas kernels for 9%

profile of v6, /device:TPU:6, one launch (start us, length us, event | category | flops | bytes accessed | tf_op | source)
XLA Modules:
  0.0 135.1 jit_solution(6462367015683691252)
XLA Ops:
  0.0 0.0 copy-start.1
  0.0 0.8 copy-done.1
  0.8 0.7 shard_map.40
  1.5 12.5 %all-to-all-start.1 = ((f32[8,16,512]{2,1,0:T(8,128)}), f32[8,16,512]{2,1,0:T(8,128)S(1)}, u32[]{:S(2)}, u32[]{:S(2)}) async-start(f32[8,16,512]{2,1,0:T(8,128)} %shard_map.40), calls=%async_computation.1 | async-start | bytes 524288 | tf_op jit(solution)/shard_map/all_to_all | solution.py:303
  14.0 1.1 fusion
  15.2 4.9 %collective-permute-start.2 = (f32[128,256]{1,0:T(8,128)S(1)}, f32[128,256]{1,0:T(8,128)S(1)}, u32[]{:S(2)}, u32[]{:S(2)}) collective-permute-start(f32[128,256]{1,0:T(8,128)S(1)} %get-tuple-element.25), channel_id=1, source_target_pairs={{0,24},{32,56},{64,88},{96,120},{128,152},{160,184},{192,216},{224... | collective-permute-start | bytes 393224 | tf_op jit(solution)/shard_map/ppermute | solution.py:292
  20.1 1.3 collective-permute-start.1
  21.4 1.3 collective-permute-start
  22.7 0.0 collective-permute-done.2.refs_3_
  22.7 2.5 %collective-permute-done.1.refs_2_ = f32[128,256]{1,0:T(8,128)S(1)} collective-permute-done((f32[128,256]{1,0:T(8,128)S(1)}, f32[128,256]{1,0:T(8,128)S(1)}, u32[]{:S(2)}, u32[]{:S(2)}) %collective-permute-start.1) | collective-permute-done | bytes 131104 | tf_op jit(solution)/shard_map/ppermute | solution.py:292
  25.3 1.4 %collective-permute-done.refs_1_ = f32[128,256]{1,0:T(8,128)S(1)} collective-permute-done((f32[128,256]{1,0:T(8,128)S(1)}, f32[128,256]{1,0:T(8,128)S(1)}, u32[]{:S(2)}, u32[]{:S(2)}) %collective-permute-start) | collective-permute-done | bytes 131104 | tf_op jit(solution)/shard_map/ppermute | solution.py:292
  26.7 1.3 collective-permute-start.3
  28.0 2.6 %collective-permute-done.3 = f32[128,256]{1,0:T(8,128)S(1)} collective-permute-done((f32[128,256]{1,0:T(8,128)S(1)}, f32[128,256]{1,0:T(8,128)S(1)}, u32[]{:S(2)}, u32[]{:S(2)}) %collective-permute-start.3) | collective-permute-done | bytes 131104 | tf_op jit(solution)/shard_map/ppermute | solution.py:298
  30.6 1.3 collective-permute-start.4
  31.9 3.2 %collective-permute-done.4 = f32[128,256]{1,0:T(8,128)S(1)} collective-permute-done((f32[128,256]{1,0:T(8,128)S(1)}, f32[128,256]{1,0:T(8,128)S(1)}, u32[]{:S(2)}, u32[]{:S(2)}) %collective-permute-start.4) | collective-permute-done | bytes 131104 | tf_op jit(solution)/shard_map/ppermute | solution.py:298
  35.1 1.3 collective-permute-start.5
  36.4 2.5 %collective-permute-done.5.refs_1_ = f32[128,256]{1,0:T(8,128)S(1)} collective-permute-done((f32[128,256]{1,0:T(8,128)S(1)}, f32[128,256]{1,0:T(8,128)S(1)}, u32[]{:S(2)}, u32[]{:S(2)}) %collective-permute-start.5) | collective-permute-done | bytes 131104 | tf_op jit(solution)/shard_map/ppermute | solution.py:298
  39.0 0.0 all-to-all-done.1
  39.0 12.3 %all_to_all.25 = f32[4,128,256]{2,1,0:T(8,128)S(1)} all-to-all(f32[4,128,256]{2,1,0:T(8,128)S(1)} %shard_map.38), channel_id=1, replica_groups=mesh['zh'=2,'x'=4,'core'=2,'y'=4,'zl'=8] {'y'}, dimensions={0} | all-to-all | bytes 1048576 | tf_op jit(solution)/shard_map/all_to_all | solution.py:302
  51.2 0.0 copy-start
  51.2 1.2 shard_map.41
  52.5 3.5 %all-to-all-start.2 = ((f32[4,128,256]{2,1,0:T(8,128)}), f32[4,128,256]{2,1,0:T(8,128)S(1)}, u32[]{:S(2)}, u32[]{:S(2)}) async-start(f32[4,128,256]{2,1,0:T(8,128)} %shard_map.41), calls=%async_computation.2 | async-start | bytes 1048576 | tf_op jit(solution)/shard_map/all_to_all | solution.py:305
  55.9 0.0 copy-done
  56.0 0.5 shard_map.39
  56.4 0.0 copy-start.3
  56.4 0.8 copy-done.3
  57.2 6.7 %all-to-all-done.2 = f32[4,128,256]{2,1,0:T(8,128)S(1)} async-done(((f32[4,128,256]{2,1,0:T(8,128)}), f32[4,128,256]{2,1,0:T(8,128)S(1)}, u32[]{:S(2)}, u32[]{:S(2)}) %all-to-all-start.2) | async-done | bytes 524320 | tf_op jit(solution)/shard_map/all_to_all | solution.py:305
  64.0 1.5 %terms.1 = (f32[336,256]{1,0:T(8,128)S(1)}, f32[336,256]{1,0:T(8,128)S(1)}) custom-call(s32[1]{0:T(128)} %bitcast.1.core_ref, bf16[512,512]{1,0:T(8,128)(2,1)S(1)} %get-tuple-element.15.own_high, bf16[256,512]{1,0:T(8,128)(2,1)S(1)} %get-tuple-element.16.panel_high, bf16[256,512]{1,0:T(8,128)(2,1)S(1)} %get-tuple-element.17.panel_low, ...), custom_call_target="tpu_custom_call" | custom-call | flops 603979776 | bytes 1572864 | tf_op jit(solution)/shard_map/terms/pallas_call | solution.py:205
  65.5 1.9 %collective-permute-start.6 = (f32[336,256]{1,0:T(8,128)S(1)}, f32[336,256]{1,0:T(8,128)S(1)}, u32[]{:S(2)}, u32[]{:S(2)}) collective-permute-start(f32[336,256]{1,0:T(8,128)S(1)} %get-tuple-element.20), channel_id=1, source_target_pairs={{0,32},{32,0},{1,33},{33,1},{2,34},{34,2},{3,35},{35,3},{4,36},{36... | collective-permute-start | bytes 1032200 | tf_op jit(solution)/shard_map/ppermute | solution.py:315
  67.4 1.6 %collective-permute-done.6.other_ref = f32[336,256]{1,0:T(8,128)S(1)} collective-permute-done((f32[336,256]{1,0:T(8,128)S(1)}, f32[336,256]{1,0:T(8,128)S(1)}, u32[]{:S(2)}, u32[]{:S(2)}) %collective-permute-start.6) | collective-permute-done | bytes 344096 | tf_op jit(solution)/shard_map/ppermute | solution.py:315
  69.1 13.0 %all_to_all.26.x_ref = f32[4,144,256]{2,1,0:T(8,128)S(1)} all-to-all(f32[4,144,256]{2,1,0:T(8,128)S(1)} %shard_map.42), channel_id=1, replica_groups=mesh['zh'=2,'x'=4,'core'=2,'y'=4,'zl'=8] {'x'}, dimensions={0} | all-to-all | bytes 1179648 | tf_op jit(solution)/shard_map/all_to_all | solution.py:317
  82.1 9.1 %collective-permute-start.8 = (f32[80,256]{1,0:T(8,128)S(1)}, f32[80,256]{1,0:T(8,128)S(1)}, u32[]{:S(2)}, u32[]{:S(2)}) collective-permute-start(f32[80,256]{1,0:T(8,128)S(1)} %get-tuple-element.22), channel_id=1, source_target_pairs={{0,260},{1,261},{2,262},{3,263},{4,256},{5,257},{6,258},{7,259},{2... | collective-permute-start | bytes 245768 | tf_op jit(solution)/shard_map/ppermute | solution.py:322
  91.2 7.1 %collective-permute-done.8 = f32[80,256]{1,0:T(8,128)S(1)} collective-permute-done((f32[80,256]{1,0:T(8,128)S(1)}, f32[80,256]{1,0:T(8,128)S(1)}, u32[]{:S(2)}, u32[]{:S(2)}) %collective-permute-start.8) | collective-permute-done | bytes 81952 | tf_op jit(solution)/shard_map/ppermute | solution.py:322
  98.3 1.9 %collective-permute-start.9 = (f32[80,256]{1,0:T(8,128)S(1)}, f32[80,256]{1,0:T(8,128)S(1)}, u32[]{:S(2)}, u32[]{:S(2)}) collective-permute-start(f32[80,256]{1,0:T(8,128)S(1)} %add.11.mine_ref), channel_id=1, source_target_pairs={{0,32},{32,0},{1,33},{33,1},{2,34},{34,2},{3,35},{35,3},{4,36},{36... | collective-permute-start | bytes 245768 | tf_op jit(solution)/shard_map/ppermute | solution.py:323
  100.2 6.3 %collective-permute-start.7 = (f32[64,256]{1,0:T(8,128)S(1)}, f32[64,256]{1,0:T(8,128)S(1)}, u32[]{:S(2)}, u32[]{:S(2)}) collective-permute-start(f32[64,256]{1,0:T(8,128)S(1)} %get-tuple-element.21.refs_0_), channel_id=1, source_target_pairs={{0,256},{256,0},{1,257},{257,1},{2,258},{258,2},{3,259},{259,3},{4... | collective-permute-start | bytes 196616 | tf_op jit(solution)/shard_map/ppermute | solution.py:324
  106.6 8.9 %collective-permute-done.7.refs_1_ = f32[64,256]{1,0:T(8,128)S(1)} collective-permute-done((f32[64,256]{1,0:T(8,128)S(1)}, f32[64,256]{1,0:T(8,128)S(1)}, u32[]{:S(2)}, u32[]{:S(2)}) %collective-permute-start.7) | collective-permute-done | bytes 65568 | tf_op jit(solution)/shard_map/ppermute | solution.py:324
  115.4 0.8 shard_map.44
  116.3 0.0 copy-start.2
  116.3 5.6 %all-to-all-start.4 = ((f32[8,64,256]{2,1,0:T(8,128)}), f32[8,64,256]{2,1,0:T(8,128)S(1)}, u32[]{:S(2)}, u32[]{:S(2)}) async-start(f32[8,64,256]{2,1,0:T(8,128)} %shard_map.44), calls=%async_computation.4 | async-start | bytes 1048576 | tf_op jit(solution)/shard_map/all_to_all | solution.py:325
  121.9 0.0 collective-permute-done.9.other_ref
  121.9 0.0 copy-done.2
  121.9 10.5 %shard_map.45 = (f32[256,256]{1,0:T(8,128)S(1)}, f32[256,128]{1,0:T(8,128)S(1)}) custom-call(s32[1]{0:T(128)} %bitcast.1.core_ref, f32[80,256]{1,0:T(8,128)S(1)} %add.11.mine_ref, f32[80,256]{1,0:T(8,128)S(1)} %collective-permute-done.9.other_ref, f32[128,128]{1,0:T(8,128)S(1)} %bitcast.16), custom_call_target="tpu_custom_call" | custom-call | flops 6000000000 | bytes 229380 | tf_op jit(solution)/shard_map/pallas_call | solution.py:37
  132.4 0.0 all-to-all-done.4
  132.4 2.7 %finish.1 = f32[512,256]{1,0:T(8,128)} custom-call(s32[1]{0:T(128)} %bitcast.top_ref, f32[512,256]{1,0:T(8,128)S(1)} %bitcast.11, f32[256,256]{1,0:T(8,128)S(1)} %get-tuple-element.23.m_ref, f32[256,128]{1,0:T(8,128)S(1)} %get-tuple-element.24.u_ref), custom_call_target="tpu_custom_call" | custom-call | flops 67108864 | bytes 1048576 | tf_op jit(solution)/shard_map/finish/pallas_call | solution.py:259
  (7 shorter events, 0.2 us)
Async XLA Ops:
  0.0 0.8 copy-start.1
  1.5 37.5 %all-to-all-start.1 = ((f32[8,16,512]{2,1,0:T(8,128)}), f32[8,16,512]{2,1,0:T(8,128)S(1)}, u32[]{:S(2)}, u32[]{:S(2)}) async-start(f32[8,16,512]{2,1,0:T(8,128)} %shard_map.40), calls=%async_computation.1 | async-start | bytes 524288 | tf_op jit(solution)/shard_map/all_to_all | solution.py:303
  15.2 7.5 %collective-permute-start.2 = (f32[128,256]{1,0:T(8,128)S(1)}, f32[128,256]{1,0:T(8,128)S(1)}, u32[]{:S(2)}, u32[]{:S(2)}) collective-permute-start(f32[128,256]{1,0:T(8,128)S(1)} %get-tuple-element.25), channel_id=1, source_target_pairs={{0,24},{32,56},{64,88},{96,120},{128,152},{160,184},{192,216},{224... | collective-permute-start | bytes 393224 | tf_op jit(solution)/shard_map/ppermute | solution.py:292
  20.1 5.2 %collective-permute-start.1 = (f32[128,256]{1,0:T(8,128)S(1)}, f32[128,256]{1,0:T(8,128)S(1)}, u32[]{:S(2)}, u32[]{:S(2)}) collective-permute-start(f32[128,256]{1,0:T(8,128)S(1)} %get-tuple-element.26), channel_id=1, source_target_pairs={{0,16},{32,48},{64,80},{96,112},{128,144},{160,176},{192,208},{224... | collective-permute-start | bytes 393224 | tf_op jit(solution)/shard_map/ppermute | solution.py:292
  21.4 5.3 %collective-permute-start = (f32[128,256]{1,0:T(8,128)S(1)}, f32[128,256]{1,0:T(8,128)S(1)}, u32[]{:S(2)}, u32[]{:S(2)}) collective-permute-start(f32[128,256]{1,0:T(8,128)S(1)} %get-tuple-element.27), channel_id=1, source_target_pairs={{0,8},{32,40},{64,72},{96,104},{128,136},{160,168},{192,200},{224,... | collective-permute-start | bytes 393224 | tf_op jit(solution)/shard_map/ppermute | solution.py:292
  26.7 3.9 %collective-permute-start.3 = (f32[128,256]{1,0:T(8,128)S(1)}, f32[128,256]{1,0:T(8,128)S(1)}, u32[]{:S(2)}, u32[]{:S(2)}) collective-permute-start(f32[128,256]{1,0:T(8,128)S(1)} %shard_map.37), channel_id=1, source_target_pairs={{0,4},{8,12},{16,20},{24,28},{32,36},{40,44},{48,52},{56,60},{64,6... | collective-permute-start | bytes 393224 | tf_op jit(solution)/shard_map/ppermute | solution.py:298
  30.6 4.5 %collective-permute-start.4 = (f32[128,256]{1,0:T(8,128)S(1)}, f32[128,256]{1,0:T(8,128)S(1)}, u32[]{:S(2)}, u32[]{:S(2)}) collective-permute-start(f32[128,256]{1,0:T(8,128)S(1)} %add.9), channel_id=1, source_target_pairs={{0,2},{4,6},{8,10},{12,14},{16,18},{20,22},{24,26},{28,30},{32,34}... | collective-permute-start | bytes 393224 | tf_op jit(solution)/shard_map/ppermute | solution.py:298
  35.1 3.8 %collective-permute-start.5 = (f32[128,256]{1,0:T(8,128)S(1)}, f32[128,256]{1,0:T(8,128)S(1)}, u32[]{:S(2)}, u32[]{:S(2)}) collective-permute-start(f32[128,256]{1,0:T(8,128)S(1)} %add.10.refs_0_), channel_id=1, source_target_pairs={{0,1},{2,3},{4,5},{6,7},{8,9},{10,11},{12,13},{14,15},{16,17},{18,... | collective-permute-start | bytes 393224 | tf_op jit(solution)/shard_map/ppermute | solution.py:298
  51.2 4.7 %copy-start = (f32[1,512,512]{2,1,0:T(8,128)S(1)}, f32[1,512,512]{2,1,0:T(8,128)}, u32[]{:S(2)}) copy-start(f32[1,512,512]{2,1,0:T(8,128)} %own_ref.1) | copy-start | bytes 3145732
  52.5 11.5 %all-to-all-start.2 = ((f32[4,128,256]{2,1,0:T(8,128)}), f32[4,128,256]{2,1,0:T(8,128)S(1)}, u32[]{:S(2)}, u32[]{:S(2)}) async-start(f32[4,128,256]{2,1,0:T(8,128)} %shard_map.41), calls=%async_computation.2 | async-start | bytes 1048576 | tf_op jit(solution)/shard_map/all_to_all | solution.py:305
  56.4 0.8 copy-start.3
  65.5 3.5 %collective-permute-start.6 = (f32[336,256]{1,0:T(8,128)S(1)}, f32[336,256]{1,0:T(8,128)S(1)}, u32[]{:S(2)}, u32[]{:S(2)}) collective-permute-start(f32[336,256]{1,0:T(8,128)S(1)} %get-tuple-element.20), channel_id=1, source_target_pairs={{0,32},{32,0},{1,33},{33,1},{2,34},{34,2},{3,35},{35,3},{4,36},{36... | collective-permute-start | bytes 1032200 | tf_op jit(solution)/shard_map/ppermute | solution.py:315
  82.1 16.2 %collective-permute-start.8 = (f32[80,256]{1,0:T(8,128)S(1)}, f32[80,256]{1,0:T(8,128)S(1)}, u32[]{:S(2)}, u32[]{:S(2)}) collective-permute-start(f32[80,256]{1,0:T(8,128)S(1)} %get-tuple-element.22), channel_id=1, source_target_pairs={{0,260},{1,261},{2,262},{3,263},{4,256},{5,257},{6,258},{7,259},{2... | collective-permute-start | bytes 245768 | tf_op jit(solution)/shard_map/ppermute | solution.py:322
  98.3 23.6 %collective-permute-start.9 = (f32[80,256]{1,0:T(8,128)S(1)}, f32[80,256]{1,0:T(8,128)S(1)}, u32[]{:S(2)}, u32[]{:S(2)}) collective-permute-start(f32[80,256]{1,0:T(8,128)S(1)} %add.11.mine_ref), channel_id=1, source_target_pairs={{0,32},{32,0},{1,33},{33,1},{2,34},{34,2},{3,35},{35,3},{4,36},{36... | collective-permute-start | bytes 245768 | tf_op jit(solution)/shard_map/ppermute | solution.py:323
  100.2 15.2 %collective-permute-start.7 = (f32[64,256]{1,0:T(8,128)S(1)}, f32[64,256]{1,0:T(8,128)S(1)}, u32[]{:S(2)}, u32[]{:S(2)}) collective-permute-start(f32[64,256]{1,0:T(8,128)S(1)} %get-tuple-element.21.refs_0_), channel_id=1, source_target_pairs={{0,256},{256,0},{1,257},{257,1},{2,258},{258,2},{3,259},{259,3},{4... | collective-permute-start | bytes 196616 | tf_op jit(solution)/shard_map/ppermute | solution.py:324
  116.3 5.6 %copy-start.2 = (f32[16384]{0:T(1024)S(1)}, f32[16384]{0:T(1024)}, u32[]{:S(2)}) copy-start(f32[16384]{0:T(1024)} %param.5) | copy-start | bytes 196612
  116.3 16.1 %all-to-all-start.4 = ((f32[8,64,256]{2,1,0:T(8,128)}), f32[8,64,256]{2,1,0:T(8,128)S(1)}, u32[]{:S(2)}, u32[]{:S(2)}) async-start(f32[8,64,256]{2,1,0:T(8,128)} %shard_map.44), calls=%async_computation.4 | async-start | bytes 1048576 | tf_op jit(solution)/shard_map/all_to_all | solution.py:325

commit v7 on v6

--- a/solution.py
+++ b/solution.py
@@ -53,27 +53,39 @@
 def base(tiles, lane0):
     row = lax.broadcasted_iota(jnp.int32, (8, LANES), 0)
     n = len(tiles)
+    columns = lambda t, group: [lane_of(tiles[t], lane0 + 8 * group + j) for j in range(8)]
+    tree = lambda p: ((p[0] + p[1]) + (p[2] + p[3])) + ((p[4] + p[5]) + (p[6] + p[7]))
+    cols = columns(0, 0)
     for s in range(n):
         x = tiles[s]
-        cols = [lane_of(x, lane0 + 8*s + j) for j in range(8)]
-        rest = [[lane_of(tiles[t], lane0 + 8*s + j) for j in range(8)] for t in range(s+1, n)]
+        last = s + 1 == n
+        after = [] if last else columns(s, s + 1)
+        ahead = [] if last else columns(s + 1, s + 1)
+        rest = [columns(t, s) for t in range(s + 1, n)]
         done = None
         for j in range(8):
             rs = lax.rsqrt(row_of(cols[j], j))
-            u = row_of(x, j)
-            scaled = u * rs
-            g = scaled * rs
+            r2 = rs * rs
+            col = cols[j]
+
+            def eliminate(v):
+                pivot_row = row_of(v, j)
+                return jnp.where(row == j, pivot_row * r2, v - (col * pivot_row) * r2)
+
+            scaled = row_of(x, j) * rs
             done = scaled if done is None else jnp.where(row >= j, scaled, done)
-            x = jnp.where(row == j, g, x - cols[j] * g)
-            for l in range(j+1, 8):
-                cl = row_of(cols[l], j) * (rs * rs)
-                cols[l] = jnp.where(row == j, cl, cols[l] - cols[j] * cl)
+            cols = cols[: j + 1] + [eliminate(v) for v in cols[j + 1 :]]
+            after = [eliminate(v) for v in after]
+            x = eliminate(x)
         tiles[s] = done
-        gs = [row_of(x, j) for j in range(8)]
-        for i, t in enumerate(range(s+1, n)):
-            acc = tiles[t]
-            for j in range(8): acc = acc - rest[i][j] * gs[j]
-            tiles[t] = acc
+        if not last:
+            cols = [
+                ahead[m] - tree([rest[0][j] * row_of(after[m], j) for j in range(8)])
+                for m in range(8)
+            ]
+        rows = [row_of(x, j) for j in range(8)]
+        for i, t in enumerate(range(s + 1, n)):
+            tiles[t] = tiles[t] - tree([rest[i][j] * rows[j] for j in range(8)])
     return tiles
 
 
@@ -109,10 +121,11 @@
         mrow = jnp.where(wlane // BLOCK == k, (wlane == wsub + BLOCK*k).astype(jnp.float32), mrow)
         z = jnp.zeros((BLOCK, PANEL), jnp.float32)
         rhs = jnp.concatenate([mrow, z] if odd else [z, mrow], axis=0)
-        nk = lax.dot_general(left, rhs, (((1,),(0,)),((),())), precision=HIGHEST, preferred_element_type=jnp.float32)
+        nk = dot_halves(halves(left), halves(rhs), 1, 0)
         m_ref[BLOCK*k:BLOCK*k+BLOCK, :] = nk
         if k + 1 < PANEL // BLOCK:
-            upd = lax.dot_general(nk, nk, (((0,),(0,)),((),())), precision=HIGHEST, preferred_element_type=jnp.float32)
+            high, low = halves(nk)
+            upd = dot_halves((high.T, low.T), (high, low), 1, 0)
             lo = BLOCK*(k+1)
             below = m_ref[lo:, :]
             wl = lax.broadcasted_iota(jnp.int32, below.shape, 1)
@@ -239,22 +252,18 @@
 
     o_ref[...] = dot_halves(halves(s_ref[...]), (left[0], left[1]), 1, 1)
 
-    @pl.when((top_ref[0] == 1) & (step < PANEL // per))
+    @pl.when((top_ref[0] == 1) & (step * per < PANEL))
     def _():
         r, c = block((PANEL, LANES), 0), block((PANEL, LANES), 1)
         for half in range(PANEL // LANES):
             lanes = slice(LANES * half, LANES * half + LANES)
             inside = (r // BLOCK) == (c + LANES * half) // BLOCK
             upper = jnp.where(inside, u_ref[...], m_ref[:, lanes])
-            upper = jnp.where(r <= c + LANES * half, upper, 0.0).T
-            for s in range(LANES // per):
-                @pl.when(step == half * (LANES // per) + s)
-                def _():
-                    o_ref[...] = upper[per * s : per * s + per]
+            o_ref[lanes] = jnp.where(r <= c + LANES * half, upper, 0.0).T
 
 
 def finish(top, rows, m, u):
-    width, per = rows.shape[0], 128
+    width, per = rows.shape[0], 256
     whole = lambda x: pl.BlockSpec(x.shape, lambda i: (0, 0))
     return pl.pallas_call(
         finish_body,

time: 137 us -> 136 us (level)
  the two profiles are of different devices: /device:TPU:6 before, /device:TPU:96 now
where the time goes in v7:
time: 136 us; the launch traced here: 135 us
  waiting for transfers between devices  47.3 us (35%)
  starting transfers between devices  43.1 us (32%)
  blocking collectives  26.8 us (20%)
  Pallas kernels  14.5 us (11%)
  local copies, waits for them, and re-layouts  1.57 us (1%)
    ppermute x3, waiting for transfers between devices, shards(): got = lax.ppermute(mine, 'zl', pairs)  20.4 us
    all_to_all x1, blocking collectives, shards(): terms = swap(terms, 'x')  14.6 us
    all_to_all x1, blocking collectives, shards(): panel = swap(copies(n_y, mine, got), 'y').reshape(depth, PANEL)  12.3 us
    all_to_all x1, starting transfers between devices, shards(): inv = swap(copies(n_zl, inverse_slabs[0]), 'zl').reshape(per, depth)  11.7 us
    pallas_call x9, Pallas kernels, call(): pl.pallas_call(body, compiler_params=PARAMS, out_shape=outs, in_specs=[sm...  11.7 us
    ppermute x1, waiting for transfers between devices, shards(): other = lax.ppermute(rows, 'zh', [(0, 1), (1, 0)])  11.7 us
    ppermute x1, starting transfers between devices, shards(): pivot = pivot + lax.ppermute(pivot, ('zh', 'zl'), flip)  9.07 us
    all_to_all x1, waiting for transfers between devices, shards(): solved = swap(solved, 'y').reshape(depth, PANEL)  6.74 us
  transfers between devices with their start and end apart: 13, of which 6 were waited for; matrix products, arithmetic and copies ran while one was open for 1% of the time, Pallas kernels for 7%

profile of v7, /device:TPU:96, one launch (start us, length us, event | category | flops | bytes accessed | tf_op | source)
XLA Modules:
  0.0 134.7 jit_solution(2306244905995643269)
XLA Ops:
  0.0 0.0 copy-start.1
  0.0 0.8 copy-done.1
  0.8 0.7 shard_map.40
  1.5 11.7 %all-to-all-start.1 = ((f32[8,16,512]{2,1,0:T(8,128)}), f32[8,16,512]{2,1,0:T(8,128)S(1)}, u32[]{:S(2)}, u32[]{:S(2)}) async-start(f32[8,16,512]{2,1,0:T(8,128)} %shard_map.40), calls=%async_computation.1 | async-start | bytes 524288 | tf_op jit(solution)/shard_map/all_to_all | solution.py:312
  13.2 1.1 fusion
  14.3 0.7 collective-permute-start.2
  15.0 0.7 collective-permute-start.1
  15.7 0.7 collective-permute-start
  16.4 0.0 collective-permute-done.2.refs_3_
  16.4 0.0 collective-permute-done.1.refs_2_
  16.4 0.0 collective-permute-done.refs_1_
  16.4 0.7 collective-permute-start.3
  17.1 0.0 collective-permute-done.3
  17.2 0.7 collective-permute-start.4
  17.8 0.0 collective-permute-done.4
  17.9 1.3 collective-permute-start.5
  19.2 20.4 %collective-permute-done.5.refs_1_ = f32[128,256]{1,0:T(8,128)S(1)} collective-permute-done((f32[128,256]{1,0:T(8,128)S(1)}, f32[128,256]{1,0:T(8,128)S(1)}, u32[]{:S(2)}, u32[]{:S(2)}) %collective-permute-start.5) | collective-permute-done | bytes 131104 | tf_op jit(solution)/shard_map/ppermute | solution.py:307
  39.6 0.0 all-to-all-done.1
  39.6 12.3 %all_to_all.25 = f32[4,128,256]{2,1,0:T(8,128)S(1)} all-to-all(f32[4,128,256]{2,1,0:T(8,128)S(1)} %shard_map.38), channel_id=1, replica_groups=mesh['zh'=2,'x'=4,'core'=2,'y'=4,'zl'=8] {'y'}, dimensions={0} | all-to-all | bytes 1048576 | tf_op jit(solution)/shard_map/all_to_all | solution.py:311
  51.9 0.0 copy-start
  51.9 1.2 shard_map.41
  53.1 3.5 %all-to-all-start.2 = ((f32[4,128,256]{2,1,0:T(8,128)}), f32[4,128,256]{2,1,0:T(8,128)S(1)}, u32[]{:S(2)}, u32[]{:S(2)}) async-start(f32[4,128,256]{2,1,0:T(8,128)} %shard_map.41), calls=%async_computation.2 | async-start | bytes 1048576 | tf_op jit(solution)/shard_map/all_to_all | solution.py:314
  56.6 0.0 copy-done
  56.6 0.5 shard_map.39
  57.1 0.0 copy-start.3
  57.1 0.8 copy-done.3
  57.9 6.7 %all-to-all-done.2 = f32[4,128,256]{2,1,0:T(8,128)S(1)} async-done(((f32[4,128,256]{2,1,0:T(8,128)}), f32[4,128,256]{2,1,0:T(8,128)S(1)}, u32[]{:S(2)}, u32[]{:S(2)}) %all-to-all-start.2) | async-done | bytes 524320 | tf_op jit(solution)/shard_map/all_to_all | solution.py:314
  64.6 1.5 %terms.1 = (f32[336,256]{1,0:T(8,128)S(1)}, f32[336,256]{1,0:T(8,128)S(1)}) custom-call(s32[1]{0:T(128)} %bitcast.1.core_ref, bf16[512,512]{1,0:T(8,128)(2,1)S(1)} %get-tuple-element.15.own_high, bf16[256,512]{1,0:T(8,128)(2,1)S(1)} %get-tuple-element.16.panel_high, bf16[256,512]{1,0:T(8,128)(2,1)S(1)} %get-tuple-element.17.panel_low, ...), custom_call_target="tpu_custom_call" | custom-call | flops 603979776 | bytes 1572864 | tf_op jit(solution)/shard_map/terms/pallas_call | solution.py:218
  66.1 1.9 %collective-permute-start.6 = (f32[336,256]{1,0:T(8,128)S(1)}, f32[336,256]{1,0:T(8,128)S(1)}, u32[]{:S(2)}, u32[]{:S(2)}) collective-permute-start(f32[336,256]{1,0:T(8,128)S(1)} %get-tuple-element.20), channel_id=1, source_target_pairs={{0,32},{32,0},{1,33},{33,1},{2,34},{34,2},{3,35},{35,3},{4,36},{36... | collective-permute-start | bytes 1032200 | tf_op jit(solution)/shard_map/ppermute | solution.py:324
  68.0 1.6 %collective-permute-done.6.other_ref = f32[336,256]{1,0:T(8,128)S(1)} collective-permute-done((f32[336,256]{1,0:T(8,128)S(1)}, f32[336,256]{1,0:T(8,128)S(1)}, u32[]{:S(2)}, u32[]{:S(2)}) %collective-permute-start.6) | collective-permute-done | bytes 344096 | tf_op jit(solution)/shard_map/ppermute | solution.py:324
  69.7 14.6 %all_to_all.26.x_ref = f32[4,144,256]{2,1,0:T(8,128)S(1)} all-to-all(f32[4,144,256]{2,1,0:T(8,128)S(1)} %shard_map.42), channel_id=1, replica_groups=mesh['zh'=2,'x'=4,'core'=2,'y'=4,'zl'=8] {'x'}, dimensions={0} | all-to-all | bytes 1179648 | tf_op jit(solution)/shard_map/all_to_all | solution.py:326
  84.3 9.1 %collective-permute-start.8 = (f32[80,256]{1,0:T(8,128)S(1)}, f32[80,256]{1,0:T(8,128)S(1)}, u32[]{:S(2)}, u32[]{:S(2)}) collective-permute-start(f32[80,256]{1,0:T(8,128)S(1)} %get-tuple-element.22), channel_id=1, source_target_pairs={{0,260},{1,261},{2,262},{3,263},{4,256},{5,257},{6,258},{7,259},{2... | collective-permute-start | bytes 245768 | tf_op jit(solution)/shard_map/ppermute | solution.py:331
  93.4 5.0 %collective-permute-done.8 = f32[80,256]{1,0:T(8,128)S(1)} collective-permute-done((f32[80,256]{1,0:T(8,128)S(1)}, f32[80,256]{1,0:T(8,128)S(1)}, u32[]{:S(2)}, u32[]{:S(2)}) %collective-permute-start.8) | collective-permute-done | bytes 81952 | tf_op jit(solution)/shard_map/ppermute | solution.py:331
  98.4 1.9 %collective-permute-start.9 = (f32[80,256]{1,0:T(8,128)S(1)}, f32[80,256]{1,0:T(8,128)S(1)}, u32[]{:S(2)}, u32[]{:S(2)}) collective-permute-start(f32[80,256]{1,0:T(8,128)S(1)} %add.11.mine_ref), channel_id=1, source_target_pairs={{0,32},{32,0},{1,33},{33,1},{2,34},{34,2},{3,35},{35,3},{4,36},{36... | collective-permute-start | bytes 245768 | tf_op jit(solution)/shard_map/ppermute | solution.py:332
  100.3 6.7 %collective-permute-start.7 = (f32[64,256]{1,0:T(8,128)S(1)}, f32[64,256]{1,0:T(8,128)S(1)}, u32[]{:S(2)}, u32[]{:S(2)}) collective-permute-start(f32[64,256]{1,0:T(8,128)S(1)} %get-tuple-element.21.refs_0_), channel_id=1, source_target_pairs={{0,256},{256,0},{1,257},{257,1},{2,258},{258,2},{3,259},{259,3},{4... | collective-permute-start | bytes 196616 | tf_op jit(solution)/shard_map/ppermute | solution.py:333
  107.0 11.7 %collective-permute-done.7.refs_1_ = f32[64,256]{1,0:T(8,128)S(1)} collective-permute-done((f32[64,256]{1,0:T(8,128)S(1)}, f32[64,256]{1,0:T(8,128)S(1)}, u32[]{:S(2)}, u32[]{:S(2)}) %collective-permute-start.7) | collective-permute-done | bytes 65568 | tf_op jit(solution)/shard_map/ppermute | solution.py:333
  118.7 0.8 shard_map.44
  119.5 0.0 copy-start.2
  119.5 3.6 %all-to-all-start.4 = ((f32[8,64,256]{2,1,0:T(8,128)}), f32[8,64,256]{2,1,0:T(8,128)S(1)}, u32[]{:S(2)}, u32[]{:S(2)}) async-start(f32[8,64,256]{2,1,0:T(8,128)} %shard_map.44), calls=%async_computation.4 | async-start | bytes 1048576 | tf_op jit(solution)/shard_map/all_to_all | solution.py:334
  123.1 0.0 collective-permute-done.9.other_ref
  123.1 0.0 copy-done.2
  123.1 8.2 %shard_map.45 = (f32[256,256]{1,0:T(8,128)S(1)}, f32[256,128]{1,0:T(8,128)S(1)}) custom-call(s32[1]{0:T(128)} %bitcast.1.core_ref, f32[80,256]{1,0:T(8,128)S(1)} %add.11.mine_ref, f32[80,256]{1,0:T(8,128)S(1)} %collective-permute-done.9.other_ref, f32[128,128]{1,0:T(8,128)S(1)} %bitcast.16), custom_call_target="tpu_custom_call" | custom-call | flops 6000000000 | bytes 229380 | tf_op jit(solution)/shard_map/pallas_call | solution.py:37
  131.4 2.0 %all-to-all-done.4 = f32[8,64,256]{2,1,0:T(8,128)S(1)} async-done(((f32[8,64,256]{2,1,0:T(8,128)}), f32[8,64,256]{2,1,0:T(8,128)S(1)}, u32[]{:S(2)}, u32[]{:S(2)}) %all-to-all-start.4) | async-done | bytes 524320 | tf_op jit(solution)/shard_map/all_to_all | solution.py:334
  133.4 1.4 %finish.1 = f32[512,256]{1,0:T(8,128)} custom-call(s32[1]{0:T(128)} %bitcast.top_ref, f32[512,256]{1,0:T(8,128)S(1)} %bitcast.11, f32[256,256]{1,0:T(8,128)S(1)} %get-tuple-element.23.m_ref, f32[256,128]{1,0:T(8,128)S(1)} %get-tuple-element.24.u_ref), custom_call_target="tpu_custom_call" | custom-call | flops 67108864 | bytes 1048576 | tf_op jit(solution)/shard_map/finish/pallas_call | solution.py:268
  (7 shorter events, 0.2 us)
Async XLA Ops:
  0.0 0.8 copy-start.1
  1.5 38.1 %all-to-all-start.1 = ((f32[8,16,512]{2,1,0:T(8,128)}), f32[8,16,512]{2,1,0:T(8,128)S(1)}, u32[]{:S(2)}, u32[]{:S(2)}) async-start(f32[8,16,512]{2,1,0:T(8,128)} %shard_map.40), calls=%async_computation.1 | async-start | bytes 524288 | tf_op jit(solution)/shard_map/all_to_all | solution.py:312
  14.3 2.0 %collective-permute-start.2 = (f32[128,256]{1,0:T(8,128)S(1)}, f32[128,256]{1,0:T(8,128)S(1)}, u32[]{:S(2)}, u32[]{:S(2)}) collective-permute-start(f32[128,256]{1,0:T(8,128)S(1)} %get-tuple-element.25), channel_id=1, source_target_pairs={{0,24},{32,56},{64,88},{96,120},{128,152},{160,184},{192,216},{224... | collective-permute-start | bytes 393224 | tf_op jit(solution)/shard_map/ppermute | solution.py:301
  15.0 1.4 %collective-permute-start.1 = (f32[128,256]{1,0:T(8,128)S(1)}, f32[128,256]{1,0:T(8,128)S(1)}, u32[]{:S(2)}, u32[]{:S(2)}) collective-permute-start(f32[128,256]{1,0:T(8,128)S(1)} %get-tuple-element.26), channel_id=1, source_target_pairs={{0,16},{32,48},{64,80},{96,112},{128,144},{160,176},{192,208},{224... | collective-permute-start | bytes 393224 | tf_op jit(solution)/shard_map/ppermute | solution.py:301
  15.7 0.7 collective-permute-start
  16.4 0.7 collective-permute-start.3
  17.2 0.7 collective-permute-start.4
  17.9 21.7 %collective-permute-start.5 = (f32[128,256]{1,0:T(8,128)S(1)}, f32[128,256]{1,0:T(8,128)S(1)}, u32[]{:S(2)}, u32[]{:S(2)}) collective-permute-start(f32[128,256]{1,0:T(8,128)S(1)} %add.10.refs_0_), channel_id=1, source_target_pairs={{0,1},{2,3},{4,5},{6,7},{8,9},{10,11},{12,13},{14,15},{16,17},{18,... | collective-permute-start | bytes 393224 | tf_op jit(solution)/shard_map/ppermute | solution.py:307
  51.9 4.7 %copy-start = (f32[1,512,512]{2,1,0:T(8,128)S(1)}, f32[1,512,512]{2,1,0:T(8,128)}, u32[]{:S(2)}) copy-start(f32[1,512,512]{2,1,0:T(8,128)} %own_ref.1) | copy-start | bytes 3145732
  53.1 11.5 %all-to-all-start.2 = ((f32[4,128,256]{2,1,0:T(8,128)}), f32[4,128,256]{2,1,0:T(8,128)S(1)}, u32[]{:S(2)}, u32[]{:S(2)}) async-start(f32[4,128,256]{2,1,0:T(8,128)} %shard_map.41), calls=%async_computation.2 | async-start | bytes 1048576 | tf_op jit(solution)/shard_map/all_to_all | solution.py:314
  57.1 0.8 copy-start.3
  66.1 3.5 %collective-permute-start.6 = (f32[336,256]{1,0:T(8,128)S(1)}, f32[336,256]{1,0:T(8,128)S(1)}, u32[]{:S(2)}, u32[]{:S(2)}) collective-permute-start(f32[336,256]{1,0:T(8,128)S(1)} %get-tuple-element.20), channel_id=1, source_target_pairs={{0,32},{32,0},{1,33},{33,1},{2,34},{34,2},{3,35},{35,3},{4,36},{36... | collective-permute-start | bytes 1032200 | tf_op jit(solution)/shard_map/ppermute | solution.py:324
  84.3 14.0 %collective-permute-start.8 = (f32[80,256]{1,0:T(8,128)S(1)}, f32[80,256]{1,0:T(8,128)S(1)}, u32[]{:S(2)}, u32[]{:S(2)}) collective-permute-start(f32[80,256]{1,0:T(8,128)S(1)} %get-tuple-element.22), channel_id=1, source_target_pairs={{0,260},{1,261},{2,262},{3,263},{4,256},{5,257},{6,258},{7,259},{2... | collective-permute-start | bytes 245768 | tf_op jit(solution)/shard_map/ppermute | solution.py:331
  98.4 24.8 %collective-permute-start.9 = (f32[80,256]{1,0:T(8,128)S(1)}, f32[80,256]{1,0:T(8,128)S(1)}, u32[]{:S(2)}, u32[]{:S(2)}) collective-permute-start(f32[80,256]{1,0:T(8,128)S(1)} %add.11.mine_ref), channel_id=1, source_target_pairs={{0,32},{32,0},{1,33},{33,1},{2,34},{34,2},{3,35},{35,3},{4,36},{36... | collective-permute-start | bytes 245768 | tf_op jit(solution)/shard_map/ppermute | solution.py:332
  100.3 18.4 %collective-permute-start.7 = (f32[64,256]{1,0:T(8,128)S(1)}, f32[64,256]{1,0:T(8,128)S(1)}, u32[]{:S(2)}, u32[]{:S(2)}) collective-permute-start(f32[64,256]{1,0:T(8,128)S(1)} %get-tuple-element.21.refs_0_), channel_id=1, source_target_pairs={{0,256},{256,0},{1,257},{257,1},{2,258},{258,2},{3,259},{259,3},{4... | collective-permute-start | bytes 196616 | tf_op jit(solution)/shard_map/ppermute | solution.py:333
  119.5 3.6 %copy-start.2 = (f32[16384]{0:T(1024)S(1)}, f32[16384]{0:T(1024)}, u32[]{:S(2)}) copy-start(f32[16384]{0:T(1024)} %param.5) | copy-start | bytes 196612
  119.5 13.9 %all-to-all-start.4 = ((f32[8,64,256]{2,1,0:T(8,128)}), f32[8,64,256]{2,1,0:T(8,128)S(1)}, u32[]{:S(2)}, u32[]{:S(2)}) async-start(f32[8,64,256]{2,1,0:T(8,128)} %shard_map.44), calls=%async_computation.4 | async-start | bytes 1048576 | tf_op jit(solution)/shard_map/all_to_all | solution.py:334
